TPU v7x, 32 devices: a whole 2x2x4 slice. The times are simulated.
32 devices in a mesh: fsdp: 4 (over z), ctx: 8 (over y, x, core).
Axes of the slice: x: 2, y: 2, z: 4, core: 2. Of those that a mesh axis runs over, the one named last changes fastest.
Arguments:
- hidden_in: bfloat16 [4, 1024, 1024], P('fsdp', 'ctx'), may hold values from -6 to 6
- pair_table: int32 [8, 2], replicated, may hold values from 0 to 15, as said below
- attn_gain: float32 [1024], replicated, may hold values from 0.5 to 1.5
- query_proj: bfloat16 [1024, 2048], P('fsdp'), may hold values from -0.1875 to 0.1875
- key_proj: bfloat16 [1024, 1024], P('fsdp'), may hold values from -0.1875 to 0.1875
- value_proj: bfloat16 [1024, 1024], P('fsdp'), may hold values from -0.1875 to 0.1875
- query_gain: float32 [128], replicated, may hold values from 0.6 to 5
- key_gain: float32 [128], replicated, may hold values from 0.6 to 5
- output_proj: bfloat16 [1024, 2048], P('fsdp'), may hold values from -2 to 2
- mlp_gain: float32 [1024], replicated, may hold values from 0.5 to 1.5
- gate_proj: bfloat16 [1024, 3072], P('fsdp'), may hold values from -0.1875 to 0.1875
- up_proj: bfloat16 [1024, 3072], P('fsdp'), may hold values from -0.1875 to 0.1875
- down_proj: bfloat16 [1024, 3072], P('fsdp'), may hold values from -0.109375 to 0.109375
- cotangent: bfloat16 [4, 1024, 1024], P('fsdp', 'ctx'), may hold values from -6 to 6
Outputs:
- block_out: bfloat16 [4, 1024, 1024], P('fsdp', 'ctx')
- input_grad: float32 [4, 1024, 1024], P('fsdp', 'ctx')
- attn_gain_grad: float32 [1024], replicated
- query_proj_grad: float32 [1024, 2048], P('fsdp')
- key_proj_grad: float32 [1024, 1024], P('fsdp')
- value_proj_grad: float32 [1024, 1024], P('fsdp')
- query_gain_grad: float32 [128], replicated
- key_gain_grad: float32 [128], replicated
- output_proj_grad: float32 [1024, 2048], P('fsdp')
- mlp_gain_grad: float32 [1024], replicated
- gate_proj_grad: float32 [1024, 3072], P('fsdp')
- up_proj_grad: float32 [1024, 3072], P('fsdp')
- down_proj_grad: float32 [1024, 3072], P('fsdp')
Inputs may be any that keep to these rules, and one draw needn't show every extreme that they name: `pair_table`: row c is (p, 15 - p); the p of the rows are 0 to 7, each once.
All inputs are finite; a program needn't handle non-finite values.
Results may differ from a plain program's by a relative error of at most 0.028.
The roundings to bfloat16 on the way count: a program that leaves them out, or rounds other values in their place, can miss the bound.
Values may be sent and summed in bfloat16 or wider, within the bound.
No kernel may reach another device: no remote copies, remote signals or barrier semaphores. Data moves between devices by JAX's collectives and lax.ppermute only.
A program may use at most 320 MiB of HBM per device.

v0:
```python
import math

import jax
import jax.numpy as jnp
from jax import lax
from jax.experimental import pallas as pl
from jax.experimental.pallas import tpu as pltpu
from jax.sharding import PartitionSpec as P


NORM_EPS = 1e-06
ROPE_BASE = 1000000.0
MASKED = -1e30
F32 = jnp.float32
BF16 = jnp.bfloat16


def rms_norm(values, gain_vec):
    return (
        values * lax.rsqrt(jnp.mean(values * values, axis=-1, keepdims=True) + NORM_EPS) * gain_vec
    )


def times_transposed(lhs_mat, rhs_mat):
    return lax.dot_general(
        lhs_mat, rhs_mat, (((1,), (1,)), ((), ())), preferred_element_type=F32
    )


def transposed_times(lhs_mat, rhs_mat):
    return lax.dot_general(
        lhs_mat, rhs_mat, (((0,), (0,)), ((), ())), preferred_element_type=F32
    )


def exchange(value, bit, axis):
    count = lax.axis_size(axis)
    return lax.ppermute(value, axis, [(index, index ^ bit) for index in range(count)])


def low_bit(number):
    return number & -number


def top_bit(number):
    return 1 << (number.bit_length() - 1)


def level_of(number):
    return bin(number).count("1")


def even_numbers(count, level):
    return [number for number in range(0, count, 2) if level_of(number) == level]


def gather_levels(count):
    return (count // 2).bit_length() - 1


def gather_step(blocks, count, level):
    half = blocks[0].shape[0] // 2
    blocks = dict(blocks)
    for number in even_numbers(count, level):
        low, top = low_bit(number), top_bit(number)
        if low == top:
            blocks[number] = exchange(blocks[0], low, "ctx")
        else:
            blocks[number] = jnp.concatenate(
                [
                    exchange(blocks[number ^ top][:half], top, "ctx"),
                    exchange(blocks[number ^ low][half:], low, "ctx"),
                ],
                axis=0,
            )
    return blocks


def gather_last(blocks, count):
    even = jnp.concatenate([blocks[number] for number in range(0, count, 2)], axis=0)
    return even, exchange(even, 1, "ctx")


def gather_ctx(own):
    count = lax.axis_size("ctx")
    blocks = {0: own}
    for level in range(1, gather_levels(count) + 1):
        blocks = gather_step(blocks, count, level)
    return gather_last(blocks, count)


def interleave(even, odd, count):
    rows = even.shape[0] * 2 // count
    both = jnp.stack(
        [even.reshape(count // 2, rows, -1), odd.reshape(count // 2, rows, -1)], axis=1
    )
    return both.reshape(count * rows, -1)


def scatter_ctx(even, odd):
    count = lax.axis_size("ctx")
    rows = even.shape[0] * 2 // count
    half = rows // 2
    moved = exchange(odd, 1, "ctx")

    def piece(number, start, stop):
        base = number // 2 * rows
        return even[base + start : base + stop].astype(F32) + moved[
            base + start : base + stop
        ].astype(F32)

    halves = {
        number: [piece(number, 0, half), piece(number, half, rows)]
        for number in range(0, count, 2)
    }
    for level in range(gather_levels(count), 1, -1):
        for number in even_numbers(count, level):
            low, top = low_bit(number), top_bit(number)
            first, second = (part.astype(BF16) for part in halves[number])
            halves[number ^ top][0] += exchange(first, top, "ctx").astype(F32)
            halves[number ^ low][1] += exchange(second, low, "ctx").astype(F32)
    total = jnp.concatenate(halves[0], axis=0)
    for number in even_numbers(count, 1):
        sent = jnp.concatenate(halves[number], axis=0).astype(BF16)
        total = total + exchange(sent, number, "ctx").astype(F32)
    return total


def gather_fsdp_step(blocks, count, level):
    blocks = dict(blocks)
    for number in range(1, count):
        if level_of(number) == level:
            low = low_bit(number)
            blocks[number] = exchange(blocks[number ^ low], low, "fsdp")
    return blocks


def scatter_fsdp_step(sums, count, level):
    sums = dict(sums)
    for number in range(1, count):
        if level_of(number) == level:
            low = low_bit(number)
            sums[number ^ low] = sums[number ^ low].astype(F32) + exchange(
                sums[number].astype(BF16), low, "fsdp"
            ).astype(F32)
    return sums


def sum_all(value):
    for axis in ("ctx", "fsdp"):
        bit = 1
        while bit < lax.axis_size(axis):
            value = value + exchange(value, bit, axis)
            bit *= 2
    return value


def whole(array):
    return pl.BlockSpec(array.shape, lambda *ids: (0,) * len(array.shape))


def pick_columns(picks):
    rows = picks[0][0].shape[0]
    widths = [width for _, _, width in picks]
    if any(width % 128 for width in widths):
        return jnp.concatenate(
            [
                lax.dynamic_slice_in_dim(array, index * width, width, axis=1)
                for array, index, width in picks
            ],
            axis=1,
        )

    def kernel(index_ref, *refs):
        start = 0
        for ref, width in zip(refs, widths):
            refs[-1][:, start : start + width] = ref[...]
            start += width

    def spec(number, width):
        return pl.BlockSpec((rows, width), lambda step, index_ref: (0, index_ref[number]))

    total = sum(widths)
    return pl.pallas_call(
        kernel,
        out_shape=jax.ShapeDtypeStruct((rows, total), picks[0][0].dtype),
        grid_spec=pltpu.PrefetchScalarGridSpec(
            num_scalar_prefetch=1,
            grid=(1,),
            in_specs=[spec(number, width) for number, width in enumerate(widths)],
            out_specs=pl.BlockSpec((rows, total), lambda step, index_ref: (0, 0)),
        ),
        cost_estimate=pl.CostEstimate(
            flops=0, bytes_accessed=4 * rows * total, transcendentals=0
        ),
        name="pick_columns",
    )(jnp.stack([index for _, index, _ in picks]).astype(jnp.int32), *[p[0] for p in picks])


def place_columns(even, odd, widths, ctx_index):
    count = lax.axis_size("ctx")
    rows = even.shape[0] * 2 // count
    starts = [sum(widths[:number]) for number in range(len(widths))]
    if any(width % 128 for width in widths):
        placed = []
        for start, width in zip(starts, widths):
            result = jnp.zeros((rows, count * width), F32)
            for number in range(count):
                base = number // 2 * rows
                result = lax.dynamic_update_slice_in_dim(
                    result,
                    (odd if number % 2 else even)[
                        base : base + rows, start : start + width
                    ].astype(F32),
                    (ctx_index ^ number) * width,
                    axis=1,
                )
            placed.append(result)
        return placed

    def kernel(index_ref, even_ref, odd_ref, *out_refs):
        for parity in range(2):

            @pl.when(index_ref[0] == parity)
            def _():
                sides = (odd_ref, even_ref) if parity else (even_ref, odd_ref)
                for out_ref, start, width in zip(out_refs, starts, widths):
                    for side, ref in enumerate(sides):
                        out_ref[:, side * width : (side + 1) * width] = ref[
                            :, start : start + width
                        ].astype(F32)

    block = pl.BlockSpec((rows, sum(widths)), lambda step, index_ref: (step, 0))
    index = [ctx_index % 2] + [(ctx_index ^ number) // 2 for number in range(0, count, 2)]
    return pl.pallas_call(
        kernel,
        out_shape=[jax.ShapeDtypeStruct((rows, count * width), F32) for width in widths],
        grid_spec=pltpu.PrefetchScalarGridSpec(
            num_scalar_prefetch=1,
            grid=(count // 2,),
            in_specs=[block, block],
            out_specs=[
                pl.BlockSpec((rows, 2 * width), lambda step, index_ref: (0, index_ref[step + 1]))
                for width in widths
            ],
        ),
        cost_estimate=pl.CostEstimate(
            flops=0, bytes_accessed=6 * count * rows * sum(widths), transcendentals=0
        ),
        name="place_columns",
    )(jnp.stack(index).astype(jnp.int32), even, odd)


def own_kernel(index_ref, hidden_ref, cot_ref, gains_ref, both_ref, order_ref):
    width = hidden_ref.shape[1]
    count = index_ref.shape[0]
    size = width // count
    for number in range(count):
        source = pl.ds(pl.multiple_of(index_ref[number] * size, size), size)
        target = slice(number * size, (number + 1) * size)
        both_ref[:, target] = hidden_ref[:, source]
        both_ref[:, width + target.start : width + target.stop] = cot_ref[:, source]
        order_ref[:, target] = gains_ref[:, source]


def own_blocks(hidden, cot, gains, indices):
    rows, width = hidden.shape
    return pl.pallas_call(
        own_kernel,
        out_shape=[
            jax.ShapeDtypeStruct((rows, 2 * width), BF16),
            jax.ShapeDtypeStruct(gains.shape, F32),
        ],
        in_specs=[pl.BlockSpec(memory_space=pltpu.SMEM)]
        + [pl.BlockSpec(memory_space=pltpu.VMEM)] * 3,
        out_specs=[pl.BlockSpec(memory_space=pltpu.VMEM)] * 2,
        cost_estimate=pl.CostEstimate(
            flops=0, bytes_accessed=8 * rows * width, transcendentals=0
        ),
        name="own_blocks",
    )(indices, hidden, cot, gains)


def mlp_kernel(x_even, x_odd, c_even, c_odd, w_ref, right_ref, act_ref, even_ref, odd_ref):
    hidden = act_ref.shape[1]
    rows = x_even.shape[0]
    for x_ref, c_ref, part_ref, start in (
        (x_even, c_even, even_ref, 0),
        (x_odd, c_odd, odd_ref, rows),
    ):
        both = jnp.dot(x_ref[...], w_ref[:, : 2 * hidden], preferred_element_type=F32)
        grad = jnp.dot(c_ref[...], w_ref[:, 2 * hidden :], preferred_element_type=F32)
        gate = both[:, :hidden]
        upper = both[:, hidden:]
        sigma = jax.nn.sigmoid(gate)
        gate_sigma = gate * sigma
        act_ref[start : start + rows, :] = (gate_sigma * upper).astype(BF16)
        right = jnp.concatenate(
            [
                (grad * upper * sigma * (1.0 + gate * (1.0 - sigma))).astype(BF16),
                (grad * gate_sigma).astype(BF16),
            ],
            axis=1,
        )
        right_ref[start : start + rows, :] = right
        part_ref[...] = lax.dot_general(
            right,
            w_ref[:, : 2 * hidden],
            (((1,), (1,)), ((), ())),
            preferred_element_type=F32,
        ).astype(BF16)


def mlp_both(x_even, x_odd, c_even, c_odd, weights, count):
    rows = x_even.shape[0] * 2 // count
    width = x_even.shape[1]
    hidden = weights.shape[1] // 3
    total = count * rows
    block = pl.BlockSpec((rows, width), lambda step: (step, 0))
    side = pl.BlockSpec((rows, width), lambda step: (step, 1))
    return pl.pallas_call(
        mlp_kernel,
        out_shape=[
            jax.ShapeDtypeStruct((total, 2 * hidden), BF16),
            jax.ShapeDtypeStruct((total, hidden), BF16),
            jax.ShapeDtypeStruct(x_even.shape, BF16),
            jax.ShapeDtypeStruct(x_even.shape, BF16),
        ],
        grid=(count // 2,),
        in_specs=[block, block, side, side, whole(weights)],
        out_specs=[
            pl.BlockSpec((2 * rows, 2 * hidden), lambda step: (step, 0)),
            pl.BlockSpec((2 * rows, hidden), lambda step: (step, 0)),
            block,
            block,
        ],
        cost_estimate=pl.CostEstimate(
            flops=10 * total * width * hidden,
            bytes_accessed=8 * total * width,
            transcendentals=total * hidden,
        ),
        name="mlp_both",
    )(x_even, x_odd, c_even, c_odd, weights)


def rotated(values, cosine, sine_part):
    return values * cosine + pltpu.roll(values, values.shape[1] // 2, 1) * sine_part


def head_scale(raw):
    return lax.rsqrt(jnp.mean(raw * raw, axis=-1, keepdims=True) + NORM_EPS)


def head_back(grad, raw, gain_row, cosine, sine_part):
    turned = grad * cosine + pltpu.roll(grad * sine_part, grad.shape[1] // 2, 1)
    scale = head_scale(raw)
    scaled = turned * gain_row
    mean_part = jnp.mean(scaled * raw, axis=-1, keepdims=True)
    return scale * scaled - raw * (scale * scale * scale * mean_part), turned * raw * scale


def project_kernel(
    x_even, x_odd, gain_ref, w_ref, qgain_ref, kgain_ref, cos_ref, sin_ref,
    in_ref, raw_ref, q_ref, k_ref, v_ref,
):
    head = qgain_ref.shape[1]
    q_width = q_ref.shape[1]
    kv_width = k_ref.shape[1]
    rows = x_even.shape[0]
    for x_ref, start in ((x_even, 0), (x_odd, rows)):
        x = x_ref[...].astype(F32)
        normed = rms_norm(x, gain_ref[...]).astype(BF16)
        in_ref[start : start + rows, :] = normed
        raw = jnp.dot(normed, w_ref[:, : q_width + 2 * kv_width], preferred_element_type=F32)
        raw_ref[start : start + rows, :] = raw[:, : q_width + kv_width]
        cosine = cos_ref[start : start + rows, :]
        sine_part = sin_ref[start : start + rows, :]
        for column in range(0, q_width, head):
            part = raw[:, column : column + head]
            q_ref[start : start + rows, column : column + head] = rotated(
                part * head_scale(part) * qgain_ref[...], cosine, sine_part
            ).astype(BF16)
        for column in range(0, kv_width, head):
            part = raw[:, q_width + column : q_width + column + head]
            k_ref[start : start + rows, column : column + head] = rotated(
                part * head_scale(part) * kgain_ref[...], cosine, sine_part
            ).astype(BF16)
        v_ref[start : start + rows, :] = raw[:, q_width + kv_width :].astype(BF16)


def project(x_even, x_odd, gain, weights, q_gain, k_gain, cosine, sine_part, q_width, kv_width):
    width = gain.shape[1]
    head = q_gain.shape[1]
    total = cosine.shape[0]
    rows = total // (2 * lax.axis_size("ctx") // 2)
    block = pl.BlockSpec((rows, width), lambda step: (step, 0))

    def wide(columns):
        return pl.BlockSpec((2 * rows, columns), lambda step: (step, 0))

    return pl.pallas_call(
        project_kernel,
        out_shape=[
            jax.ShapeDtypeStruct((total, width), BF16),
            jax.ShapeDtypeStruct((total, q_width + kv_width), F32),
            jax.ShapeDtypeStruct((total, q_width), BF16),
            jax.ShapeDtypeStruct((total, kv_width), BF16),
            jax.ShapeDtypeStruct((total, kv_width), BF16),
        ],
        grid=(total // (2 * rows),),
        in_specs=[
            block, block, whole(gain), whole(weights), whole(q_gain), whole(k_gain),
            wide(head), wide(head),
        ],
        out_specs=[
            wide(width), wide(q_width + kv_width), wide(q_width), wide(kv_width), wide(kv_width),
        ],
        cost_estimate=pl.CostEstimate(
            flops=2 * total * width * (q_width + 2 * kv_width),
            bytes_accessed=8 * total * width,
            transcendentals=total,
        ),
        name="project",
    )(x_even, x_odd, gain, weights, q_gain, k_gain, cosine, sine_part)


def nt(lhs, rhs):
    return lax.dot_general(lhs, rhs, (((1,), (1,)), ((), ())), preferred_element_type=F32)


def attend_kernel(
    q_ref, k_ref, v_ref, row_ref, col_ref, w_ref, mix_ref, lse_ref, even_ref, odd_ref, vt_ref
):
    kv_width = k_ref.shape[1]
    q_width = q_ref.shape[1]
    head = q_width // lse_ref.shape[0]
    group = q_width // kv_width
    scale = 1.0 / math.sqrt(head)

    @pl.when(pl.program_id(0) == 0)
    def _():
        vt_ref[...] = v_ref[...].astype(F32).T.astype(BF16)

    allowed = col_ref[...] <= row_ref[...]
    for number in range(q_width // head):
        kv = number // group * head
        column = number * head
        scores = jnp.where(
            allowed, nt(k_ref[:, kv : kv + head], q_ref[:, column : column + head]) * scale, MASKED
        )
        top = jnp.max(scores, axis=0, keepdims=True)
        raised = jnp.exp(scores - top)
        total = jnp.sum(raised, axis=0, keepdims=True)
        lse_ref[number : number + 1, :] = top + jnp.log(total)
        probs = (raised * (1.0 / total)).astype(BF16)
        mixed = jnp.dot(vt_ref[kv : kv + head, :], probs, preferred_element_type=F32)
        mix_ref[:, column : column + head] = mixed.T.astype(BF16)
    rows = even_ref.shape[0]
    out = nt(mix_ref[...], w_ref[...]).astype(BF16)
    even_ref[...] = out[:rows]
    odd_ref[...] = out[rows:]


def attend(q, k, v, pos_row, pos_col, out_w, head):
    total, q_width = q.shape
    kv_width = k.shape[1]
    width = out_w.shape[0]
    steps = lax.axis_size("ctx") // 2
    rows = total // (2 * steps)
    heads = q_width // head

    def wide(columns):
        return pl.BlockSpec((2 * rows, columns), lambda step: (step, 0))

    half = pl.BlockSpec((rows, width), lambda step: (step, 0))
    return pl.pallas_call(
        attend_kernel,
        out_shape=[
            jax.ShapeDtypeStruct((total, q_width), BF16),
            jax.ShapeDtypeStruct((heads, total), F32),
            jax.ShapeDtypeStruct((total // 2, width), BF16),
            jax.ShapeDtypeStruct((total // 2, width), BF16),
        ],
        grid=(steps,),
        in_specs=[
            wide(q_width), whole(k), whole(v),
            pl.BlockSpec((1, 2 * rows), lambda step: (0, step)),
            whole(pos_col), whole(out_w),
        ],
        out_specs=[
            wide(q_width), pl.BlockSpec((heads, 2 * rows), lambda step: (0, step)), half, half,
        ],
        scratch_shapes=[pltpu.VMEM((kv_width, total), BF16)],
        cost_estimate=pl.CostEstimate(
            flops=4 * total * total * q_width,
            bytes_accessed=8 * total * width,
            transcendentals=total * total * heads,
        ),
        name="attend",
    )(q, k, v, pos_row, pos_col, out_w)


def attend_back_kernel(
    q_ref, k_ref, v_ref, row_ref, col_ref, w_ref, mix_ref, lse_ref, g_even, g_odd,
    raw_ref, qgain_ref, cos_ref, sin_ref,
    low_ref, dk_ref, dv_ref, dgain_ref, kt_ref, dmix_ref,
):
    head = qgain_ref.shape[1]
    kv_width = k_ref.shape[1]
    q_width = q_ref.shape[1]
    group = q_width // kv_width
    scale = 1.0 / math.sqrt(head)
    rows = g_even.shape[0]

    @pl.when(pl.program_id(0) == 0)
    def _():
        kt_ref[...] = k_ref[...].astype(F32).T.astype(BF16)
        dk_ref[...] = jnp.zeros_like(dk_ref)
        dv_ref[...] = jnp.zeros_like(dv_ref)
        dgain_ref[...] = jnp.zeros_like(dgain_ref)

    dmix_ref[:rows, :] = jnp.dot(g_even[...], w_ref[...], preferred_element_type=F32).astype(BF16)
    dmix_ref[rows:, :] = jnp.dot(g_odd[...], w_ref[...], preferred_element_type=F32).astype(BF16)
    allowed = col_ref[...] <= row_ref[...]
    for number in range(q_width // head):
        kv = number // group * head
        column = number * head
        q = q_ref[:, column : column + head]
        dmix = dmix_ref[:, column : column + head]
        mix = mix_ref[:, column : column + head]
        delta = jnp.sum((dmix.astype(F32) * mix.astype(F32)).T, axis=0, keepdims=True)
        scores = nt(k_ref[:, kv : kv + head], q) * scale
        probs = jnp.exp(jnp.where(allowed, scores - lse_ref[number : number + 1, :], MASKED))
        dv_ref[:, kv : kv + head] += jnp.dot(
            probs.astype(BF16), dmix, preferred_element_type=F32
        )
        prob_grad = nt(v_ref[:, kv : kv + head], dmix)
        score_grad = (probs * (prob_grad - delta) * scale).astype(BF16)
        dk_ref[:, kv : kv + head] += jnp.dot(score_grad, q, preferred_element_type=F32)
        dq = jnp.dot(kt_ref[kv : kv + head, :], score_grad, preferred_element_type=F32).T
        raw_grad, gain_part = head_back(
            dq, raw_ref[:, column : column + head], qgain_ref[...], cos_ref[...], sin_ref[...]
        )
        low_ref[:, column : column + head] = raw_grad.astype(BF16)
        dgain_ref[...] += jnp.sum(gain_part, axis=0, keepdims=True)


def attend_back(q, k, v, pos_row, pos_col, out_w, mix, lse, g_even, g_odd, raw, q_gain, cosine, sine_part):
    total, q_width = q.shape
    kv_width = k.shape[1]
    width = out_w.shape[0]
    steps = lax.axis_size("ctx") // 2
    rows = total // (2 * steps)
    heads = lse.shape[0]
    head = q_gain.shape[1]

    def wide(columns):
        return pl.BlockSpec((2 * rows, columns), lambda step: (step, 0))

    def fixed(shape):
        return pl.BlockSpec(shape, lambda step: (0, 0))

    half = pl.BlockSpec((rows, width), lambda step: (step, 0))
    return pl.pallas_call(
        attend_back_kernel,
        out_shape=[
            jax.ShapeDtypeStruct((total, q_width), BF16),
            jax.ShapeDtypeStruct((total, kv_width), F32),
            jax.ShapeDtypeStruct((total, kv_width), F32),
            jax.ShapeDtypeStruct((1, head), F32),
        ],
        grid=(steps,),
        in_specs=[
            wide(q_width), whole(k), whole(v),
            pl.BlockSpec((1, 2 * rows), lambda step: (0, step)),
            whole(pos_col), whole(out_w), wide(q_width),
            pl.BlockSpec((heads, 2 * rows), lambda step: (0, step)),
            half, half, wide(q_width), whole(q_gain), wide(head), wide(head),
        ],
        out_specs=[
            wide(q_width), fixed((total, kv_width)), fixed((total, kv_width)), fixed((1, head)),
        ],
        scratch_shapes=[
            pltpu.VMEM((kv_width, total), BF16),
            pltpu.VMEM((2 * rows, q_width), BF16),
        ],
        cost_estimate=pl.CostEstimate(
            flops=10 * total * total * q_width,
            bytes_accessed=8 * total * width,
            transcendentals=total * total * heads,
        ),
        name="attend_back",
    )(q, k, v, pos_row, pos_col, out_w, mix, lse, g_even, g_odd, raw, q_gain, cosine, sine_part)


def project_back_kernel(
    low_ref, dk_ref, dv_ref, raw_ref, kgain_ref, cos_ref, sin_ref, x_even, x_odd, w_ref, blk_ref,
    right_ref, even_ref, odd_ref, again_ref, dgain_ref,
):
    head = kgain_ref.shape[1]
    kv_width = dk_ref.shape[1]
    q_width = low_ref.shape[1]
    rows, width = x_even.shape

    @pl.when(pl.program_id(0) == 0)
    def _():
        again_ref[...] = jnp.zeros_like(again_ref)
        dgain_ref[...] = jnp.zeros_like(dgain_ref)

    right_ref[:, :q_width] = low_ref[...]
    for column in range(0, kv_width, head):
        raw_grad, gain_part = head_back(
            dk_ref[:, column : column + head],
            raw_ref[:, q_width + column : q_width + column + head],
            kgain_ref[...],
            cos_ref[...],
            sin_ref[...],
        )
        right_ref[:, q_width + column : q_width + column + head] = raw_grad.astype(BF16)
        dgain_ref[...] += jnp.sum(gain_part, axis=0, keepdims=True)
    right_ref[:, q_width + kv_width :] = dv_ref[...].astype(BF16)
    for x_ref, part_ref, start in ((x_even, even_ref, 0), (x_odd, odd_ref, rows)):
        part = nt(right_ref[start : start + rows, :], w_ref[...])
        x = x_ref[...].astype(F32)
        again_ref[...] += jnp.sum(part * (x * head_scale(x)), axis=0, keepdims=True)
        part_ref[:, :width] = part.astype(BF16)
        part_ref[:, width:] = blk_ref[start : start + rows, :]


def project_back(low, dk, dv, raw, k_gain, cosine, sine_part, x_even, x_odd, weights, block_part):
    total, q_width = low.shape
    kv_width = dk.shape[1]
    width = weights.shape[0]
    steps = lax.axis_size("ctx") // 2
    rows = total // (2 * steps)
    head = k_gain.shape[1]

    def wide(columns):
        return pl.BlockSpec((2 * rows, columns), lambda step: (step, 0))

    def fixed(shape):
        return pl.BlockSpec(shape, lambda step: (0, 0))

    half = pl.BlockSpec((rows, width), lambda step: (step, 0))
    both = pl.BlockSpec((rows, 2 * width), lambda step: (step, 0))
    return pl.pallas_call(
        project_back_kernel,
        out_shape=[
            jax.ShapeDtypeStruct((total, q_width + 2 * kv_width), BF16),
            jax.ShapeDtypeStruct((total // 2, 2 * width), BF16),
            jax.ShapeDtypeStruct((total // 2, 2 * width), BF16),
            jax.ShapeDtypeStruct((1, width), F32),
            jax.ShapeDtypeStruct((1, head), F32),
        ],
        grid=(steps,),
        in_specs=[
            wide(q_width), wide(kv_width), wide(kv_width), wide(q_width + kv_width),
            whole(k_gain), wide(head), wide(head), half, half, whole(weights), wide(width),
        ],
        out_specs=[
            wide(q_width + 2 * kv_width), both, both, fixed((1, width)), fixed((1, head)),
        ],
        cost_estimate=pl.CostEstimate(
            flops=2 * total * width * (q_width + 2 * kv_width),
            bytes_accessed=12 * total * width,
            transcendentals=total,
        ),
        name="project_back",
    )(low, dk, dv, raw, k_gain, cosine, sine_part, x_even, x_odd, weights, block_part)


def on_device_all(
    hidden_in,
    pair_table,
    attn_gain,
    query_proj,
    key_proj,
    value_proj,
    query_gain,
    key_gain,
    output_proj,
    mlp_gain,
    gate_proj,
    up_proj,
    down_proj,
    cotangent,
):
    fsdp_count = lax.axis_size("fsdp")
    fsdp_index = lax.axis_index("fsdp")
    ctx_count = lax.axis_size("ctx")
    ctx_index = lax.axis_index("ctx")
    row_count, width = hidden_in.shape[1:]
    block_len = row_count // 2
    total_rows = ctx_count * row_count
    shard_rows = width // fsdp_count
    head_width = query_gain.shape[0]
    half_head = head_width // 2
    kvhead_total = key_proj.shape[1] // head_width
    kv_count = max(1, kvhead_total // ctx_count)
    kv_share = max(1, ctx_count // kvhead_total)
    query_width = query_proj.shape[1] // ctx_count
    kv_width = kv_count * head_width
    kv_own = key_proj.shape[1] // ctx_count
    hidden_width = gate_proj.shape[1] // ctx_count

    fsdp_order = fsdp_index ^ jnp.arange(fsdp_count, dtype=jnp.int32)

    def block_order(values):
        return jnp.concatenate(
            [
                lax.dynamic_slice_in_dim(
                    values, (fsdp_index ^ number) * shard_rows, shard_rows, axis=values.ndim - 1
                )
                for number in range(fsdp_count)
            ],
            axis=-1,
        )

    def columns(weights, start, size):
        return lax.dynamic_slice_in_dim(weights, start, size, axis=1)

    kv_index = ctx_index // kv_share
    both_own, gains_rel = own_blocks(
        hidden_in[0], cotangent[0], jnp.stack([attn_gain, mlp_gain]), fsdp_order
    )
    inputs = both_own[:, :width]
    cot_low = both_own[:, width:]
    attn_gain_rel = gains_rel[0]
    mlp_gain_rel = gains_rel[1]
    fsdp_levels = (fsdp_count - 1).bit_length()
    attn_width = query_width + 2 * kv_width

    def joined(blocks):
        return jnp.concatenate([blocks[number] for number in range(fsdp_count)], axis=0)

    both_even, both_odd = gather_ctx(both_own)
    first_shard = pick_columns(
        [
            (query_proj, ctx_index, query_width),
            (key_proj, kv_index, kv_width),
            (value_proj, kv_index, kv_width),
            (output_proj, ctx_index, query_width),
        ]
    )
    first_blocks = {0: first_shard}
    for level in range(1, fsdp_levels + 1):
        first_blocks = gather_fsdp_step(first_blocks, fsdp_count, level)
    first_w = joined(first_blocks)
    attn_w = first_w[:, :attn_width]
    output_w = first_w[:, attn_width:]
    mlp_shard = pick_columns(
        [(weights, ctx_index, hidden_width) for weights in (gate_proj, up_proj, down_proj)]
    )
    mlp_blocks = gather_fsdp_step({0: mlp_shard}, fsdp_count, 1)

    owner_ids = ctx_index ^ jnp.arange(ctx_count, dtype=jnp.int32)
    picked = owner_ids[:, None] == jnp.arange(ctx_count, dtype=jnp.int32)[None, :]
    block_ids = jnp.sum(jnp.where(picked[:, :, None], pair_table[None], 0), axis=1)
    positions = (
        block_ids[:, :, None] * block_len + jnp.arange(block_len, dtype=jnp.int32)
    ).reshape(total_rows)
    pos_row = positions.reshape(1, total_rows)
    pos_col = positions.reshape(total_rows, 1)
    lanes = jnp.arange(head_width, dtype=jnp.int32)
    frequency = ROPE_BASE ** (-((lanes % half_head).astype(F32) * 2.0 / head_width))
    angles = positions.astype(F32)[:, None] * frequency[None, :]
    cosine = jnp.cos(angles)
    sine_part = jnp.sin(angles) * jnp.where(lanes < half_head, -1.0, 1.0)[None, :]

    query_row = query_gain.reshape(1, head_width)
    key_row = key_gain.reshape(1, head_width)
    attn_in, attn_raw, query_heads, key_heads, value_heads = project(
        both_even, both_odd, attn_gain_rel.reshape(1, width), first_w, query_row, key_row,
        cosine, sine_part, query_width, kv_width,
    )
    attn_mix, log_total, mix_even, mix_odd = attend(
        query_heads, key_heads, value_heads, pos_row, pos_col, output_w, head_width
    )

    def split_shards(values):
        return {
            number: values[number * shard_rows : (number + 1) * shard_rows]
            for number in range(fsdp_count)
        }

    resid_sum = scatter_ctx(mix_even, mix_odd)
    cot_even = both_even[:, width:]
    cot_odd = both_odd[:, width:]
    resid = inputs.astype(F32) + resid_sum
    mlp_in = rms_norm(resid, mlp_gain_rel).astype(BF16)
    for level in range(2, fsdp_levels + 1):
        mlp_blocks = gather_fsdp_step(mlp_blocks, fsdp_count, level)
    mlp_w = joined(mlp_blocks)
    down_w = mlp_w[:, 2 * hidden_width :]
    mlp_even, mlp_odd = gather_ctx(mlp_in)
    mlp_right, hidden_act, part_even, part_odd = mlp_both(
        mlp_even, mlp_odd, both_even, both_odd, mlp_w, ctx_count
    )
    mlp_in_grad = scatter_ctx(part_even, part_odd)
    cot_all = interleave(cot_even, cot_odd, ctx_count)
    mlp_sums = split_shards(
        jnp.concatenate(
            [
                transposed_times(interleave(mlp_even, mlp_odd, ctx_count), mlp_right),
                transposed_times(cot_all, hidden_act),
            ],
            axis=1,
        ).astype(BF16)
    )
    resid_part, mlp_gain_grad = jax.vjp(rms_norm, resid, mlp_gain_rel)[1](mlp_in_grad)
    resid_grad = cot_low.astype(F32) + resid_part
    resid_low = resid_grad.astype(BF16)
    for level in range(fsdp_levels, 1, -1):
        mlp_sums = scatter_fsdp_step(mlp_sums, fsdp_count, level)
    resid_even, resid_odd = gather_ctx(resid_low)
    mlp_moved = {
        number: exchange(mlp_sums[number].astype(BF16), number, "fsdp")
        for number in range(1, fsdp_count)
        if level_of(number) == 1
    }
    resid_all = interleave(resid_even, resid_odd, ctx_count)
    block_part = times_transposed(hidden_act, down_w).astype(BF16)
    output_grads = transposed_times(resid_all, attn_mix).astype(BF16)

    query_low, key_grad, value_grad, query_gain_grad = attend_back(
        query_heads, key_heads, value_heads, pos_row, pos_col, output_w, attn_mix, log_total,
        resid_even, resid_odd, attn_raw, query_row, cosine, sine_part,
    )
    bit = 1
    while bit < kv_share:
        moved = exchange(jnp.concatenate([key_grad, value_grad], axis=1), bit, "ctx")
        moved = moved.reshape(ctx_count, row_count, 2 * kv_width)
        moved = jnp.concatenate([moved[number ^ bit] for number in range(ctx_count)], axis=0)
        key_grad = key_grad + moved[:, :kv_width]
        value_grad = value_grad + moved[:, kv_width:]
        bit *= 2
    attn_own_w = attn_w
    own_start = (ctx_index % kv_share) * kv_own
    if kv_share > 1:
        place = jnp.arange(attn_width) - query_width
        owned = (place < 0) | (
            (place % kv_width >= own_start) & (place % kv_width < own_start + kv_own)
        )
        attn_own_w = jnp.where(owned[None, :], attn_w, 0).astype(BF16)
    attn_right, tail_even, tail_odd, attn_gain_grad, key_gain_grad = project_back(
        query_low, key_grad, value_grad, attn_raw, key_row, cosine, sine_part,
        both_even, both_odd, attn_own_w, block_part,
    )
    attn_gain_grad = attn_gain_grad[0]
    query_gain_grad = query_gain_grad[0]
    key_gain_grad = key_gain_grad[0]
    if kv_share > 1:
        attn_right = jnp.concatenate(
            [
                attn_right[:, :query_width],
                columns(attn_right, query_width + own_start, kv_own),
                columns(attn_right, query_width + kv_width + own_start, kv_own),
            ],
            axis=1,
        )
        key_gain_grad = jnp.where(ctx_index % kv_share == 0, key_gain_grad, 0.0)
    attn_sums = split_shards(
        jnp.concatenate(
            [transposed_times(attn_in, attn_right).astype(BF16), output_grads], axis=1
        )
    )
    for level in range(fsdp_levels, 0, -1):
        attn_sums = scatter_fsdp_step(attn_sums, fsdp_count, level)
    attn_grads = attn_sums[0].astype(BF16)
    both_sums = scatter_ctx(tail_even, tail_odd)
    attn_in_grad = both_sums[:, :width]
    block_out = (resid + both_sums[:, width:]).astype(BF16)
    mlp_total = mlp_sums[0].astype(F32)
    for moved in mlp_moved.values():
        mlp_total = mlp_total + moved.astype(F32)
    mlp_grads = mlp_total.astype(BF16)
    own_wide = inputs.astype(F32)
    input_part = jax.vjp(lambda values: rms_norm(values, attn_gain_rel), own_wide)[1](
        attn_in_grad
    )[0]
    input_grad = resid_grad + input_part
    gains = sum_all(
        jnp.concatenate(
            [
                block_order(attn_gain_grad),
                block_order(mlp_gain_grad),
                query_gain_grad,
                key_gain_grad,
            ]
        )
    )

    def placed(own, widths):
        even, odd = gather_ctx(own)
        return place_columns(even, odd, widths, ctx_index)

    mlp_outs = placed(mlp_grads, (hidden_width,) * 3)
    attn_outs = placed(attn_grads, (query_width, kv_own, kv_own, query_width))
    return (
        block_order(block_out)[None],
        block_order(input_grad)[None],
        gains[:width],
        attn_outs[0],
        attn_outs[1],
        attn_outs[2],
        gains[2 * width : 2 * width + head_width],
        gains[2 * width + head_width :],
        attn_outs[3],
        gains[width : 2 * width],
        mlp_outs[0],
        mlp_outs[1],
        mlp_outs[2],
    )


def solution(mesh):
    in_specs = (
        P("fsdp", "ctx", None),
        P(),
        P(),
        P("fsdp", None),
        P("fsdp", None),
        P("fsdp", None),
        P(),
        P(),
        P("fsdp", None),
        P(),
        P("fsdp", None),
        P("fsdp", None),
        P("fsdp", None),
        P("fsdp", "ctx", None),
    )
    out_specs = (
        P("fsdp", "ctx", None),
        P("fsdp", "ctx", None),
        P(),
        P("fsdp", None),
        P("fsdp", None),
        P("fsdp", None),
        P(),
        P(),
        P("fsdp", None),
        P(),
        P("fsdp", None),
        P("fsdp", None),
        P("fsdp", None),
    )
    return jax.shard_map(
        on_device_all, mesh=mesh, in_specs=in_specs, out_specs=out_specs, check_vma=False
    )
```

profile of v0, /device:TPU:0, one launch (start us, length us, event | category | flops | bytes accessed | tf_op | source)
XLA Modules:
  0.0 389.4 jit_solution(12873059771693077426)
XLA Ops:
  10.0 9.5 %collective-permute-done.1 = bf16[128,2048]{1,0:T(8,128)(2,1)S(1)} collective-permute-done((bf16[128,2048]{1,0:T(8,128)(2,1)}, bf16[128,2048]{1,0:T(8,128)(2,1)S(1)}, u32[]{:S(2)}, u32[]{:S(2)}) %collective-permute-start.1) | collective-permute-done | bytes 524320 | tf_op jit(solution)/shard_map/ppermute | solution.py:38
  23.0 5.3 %collective-permute-done.2 = bf16[64,2048]{1,0:T(8,128)(2,1)S(1)} collective-permute-done((bf16[64,2048]{1,0:T(8,128)(2,1)S(1)}, bf16[64,2048]{1,0:T(8,128)(2,1)S(1)}, u32[]{:S(2)}, u32[]{:S(2)}) %collective-permute-start.2) | collective-permute-done | bytes 262176 | tf_op jit(solution)/shard_map/ppermute | solution.py:38
  36.2 16.5 %collective-permute-done.6 = bf16[256,768]{1,0:T(8,128)(2,1)S(1)} collective-permute-done((bf16[256,768]{1,0:T(8,128)(2,1)}, bf16[256,768]{1,0:T(8,128)(2,1)S(1)}, u32[]{:S(2)}, u32[]{:S(2)}) %collective-permute-start.6) | collective-permute-done | bytes 393248 | tf_op jit(solution)/shard_map/ppermute | solution.py:38
  65.6 6.1 %project.1 = (bf16[1024,1024]{1,0:T(8,128)(2,1)}, f32[1024,384]{1,0:T(8,128)}, bf16[1024,256]{1,0:T(8,128)(2,1)}, bf16[1024,128]{1,0:T(8,128)(2,1)}, bf16[1024,128]{1,0:T(8,128)(2,1)}) custom-call(bf16[512,2048]{1,0:T(8,128)(2,1)} %copy-done, bf16[512,2048]{1,0:T(8,128)(2,1)} %collective-permute-done.4.x_odd.c_odd, f32[1,1024]{1,0:T(1,128)} %get-tuple-element.131.gain_ref, ...), custom_call_target="tpu_custom_call" | custom-call | flops 1073741824 | bytes 8388608 | tf_op jit(solution)/shard_map/project/pallas_call | solution.py:401
  71.7 11.2 %attend.1 = (bf16[1024,256]{1,0:T(8,128)(2,1)}, f32[2,1024]{1,0:T(2,128)}, bf16[512,1024]{1,0:T(8,128)(2,1)}, bf16[512,1024]{1,0:T(8,128)(2,1)}) custom-call(bf16[1024,256]{1,0:T(8,128)(2,1)} %get-tuple-element.46.q_ref, bf16[1024,128]{1,0:T(8,128)(2,1)} %get-tuple-element.47.k_ref, bf16[1024,128]{1,0:T(8,128)(2,1)} %get-tuple-element.48.v_ref, ...), custom_call_target="tpu_custom_call" | custom-call | flops 1073741824 | bytes 8388608 | tf_op jit(solution)/shard_map/attend/pallas_call | solution.py:476
  97.5 4.7 %collective-permute-done.12 = bf16[128,1024]{1,0:T(8,128)(2,1)S(1)} collective-permute-done((bf16[128,1024]{1,0:T(8,128)(2,1)S(1)}, bf16[128,1024]{1,0:T(8,128)(2,1)S(1)}, u32[]{:S(2)}, u32[]{:S(2)}) %collective-permute-start.12) | collective-permute-done | bytes 262176 | tf_op jit(solution)/shard_map/ppermute | solution.py:38
  122.2 14.4 %collective-permute-done.19 = bf16[256,1152]{1,0:T(8,128)(2,1)S(1)} collective-permute-done((bf16[256,1152]{1,0:T(8,128)(2,1)}, bf16[256,1152]{1,0:T(8,128)(2,1)S(1)}, u32[]{:S(2)}, u32[]{:S(2)}) %collective-permute-start.19) | collective-permute-done | bytes 589856 | tf_op jit(solution)/shard_map/ppermute | solution.py:38
  137.5 10.8 %collective-permute-done.18 = bf16[256,1152]{1,0:T(8,128)(2,1)S(1)} collective-permute-done((bf16[256,1152]{1,0:T(8,128)(2,1)}, bf16[256,1152]{1,0:T(8,128)(2,1)S(1)}, u32[]{:S(2)}, u32[]{:S(2)}) %collective-permute-start.18) | collective-permute-done | bytes 589856 | tf_op jit(solution)/shard_map/ppermute | solution.py:38
  148.2 12.2 %collective-permute-done.20 = bf16[256,1152]{1,0:T(8,128)(2,1)S(1)} collective-permute-done((bf16[256,1152]{1,0:T(8,128)(2,1)S(1)}, bf16[256,1152]{1,0:T(8,128)(2,1)S(1)}, u32[]{:S(2)}, u32[]{:S(2)}) %collective-permute-start.20) | collective-permute-done | bytes 589856 | tf_op jit(solution)/shard_map/ppermute | solution.py:38
  163.3 10.7 %mlp_both.1 = (bf16[1024,768]{1,0:T(8,128)(2,1)}, bf16[1024,384]{1,0:T(8,128)(2,1)}, bf16[512,1024]{1,0:T(8,128)(2,1)}, bf16[512,1024]{1,0:T(8,128)(2,1)}) custom-call(bf16[512,1024]{1,0:T(8,128)(2,1)} %constant_dynamic-update-slice_fusion.5.x_even, bf16[512,1024]{1,0:T(8,128)(2,1)} %collective-permute-done.17.x_odd, bf16[512,2048]{1,0:T(8,128)(2,1)} %copy-done, ...), custom_call_target="tpu_custom_call" | custom-call | flops 4026531840 | bytes 8388608 | tf_op jit(solution)/shard_map/mlp_both/pallas_call | solution.py:321
  191.1 9.6 %collective-permute-done.50 = bf16[256,1152]{1,0:T(8,128)(2,1)} collective-permute-done((bf16[256,1152]{1,0:T(8,128)(2,1)}, bf16[256,1152]{1,0:T(8,128)(2,1)}, u32[]{:S(2)}, u32[]{:S(2)}) %collective-permute-start.50) | collective-permute-done | bytes 589856 | tf_op jit(solution)/shard_map/ppermute | solution.py:38
  208.2 14.5 %collective-permute-done.49 = bf16[256,1152]{1,0:T(8,128)(2,1)S(1)} collective-permute-done((bf16[256,1152]{1,0:T(8,128)(2,1)S(1)}, bf16[256,1152]{1,0:T(8,128)(2,1)S(1)}, u32[]{:S(2)}, u32[]{:S(2)}) %collective-permute-start.49) | collective-permute-done | bytes 589856 | tf_op jit(solution)/shard_map/ppermute | solution.py:38
  222.7 7.1 %collective-permute-done.51 = bf16[256,1152]{1,0:T(8,128)(2,1)S(1)} collective-permute-done((bf16[256,1152]{1,0:T(8,128)(2,1)S(1)}, bf16[256,1152]{1,0:T(8,128)(2,1)S(1)}, u32[]{:S(2)}, u32[]{:S(2)}) %collective-permute-start.51) | collective-permute-done | bytes 589856 | tf_op jit(solution)/shard_map/ppermute | solution.py:38
  235.2 10.5 %collective-permute-done.28 = bf16[64,1024]{1,0:T(8,128)(2,1)S(1)} collective-permute-done((bf16[64,1024]{1,0:T(8,128)(2,1)S(1)}, bf16[64,1024]{1,0:T(8,128)(2,1)S(1)}, u32[]{:S(2)}, u32[]{:S(2)}) %collective-permute-start.28) | collective-permute-done | bytes 131104 | tf_op jit(solution)/shard_map/ppermute | solution.py:38
  255.6 6.2 %collective-permute-done.54 = bf16[128,1152]{1,0:T(8,128)(2,1)S(1)} collective-permute-done((bf16[128,1152]{1,0:T(8,128)(2,1)S(1)}, bf16[128,1152]{1,0:T(8,128)(2,1)S(1)}, u32[]{:S(2)}, u32[]{:S(2)}) %collective-permute-start.54) | collective-permute-done | bytes 294944 | tf_op jit(solution)/shard_map/ppermute | solution.py:38
  263.5 11.6 %attend_back.1 = (bf16[1024,256]{1,0:T(8,128)(2,1)}, f32[1024,128]{1,0:T(8,128)}, f32[1024,128]{1,0:T(8,128)}, f32[1,128]{1,0:T(1,128)}) custom-call(bf16[1024,256]{1,0:T(8,128)(2,1)} %get-tuple-element.46.q_ref, bf16[1024,128]{1,0:T(8,128)(2,1)} %get-tuple-element.47.k_ref, bf16[1024,128]{1,0:T(8,128)(2,1)} %get-tuple-element.48.v_ref, ...), custom_call_target="tpu_custom_call" | custom-call | flops 2684354560 | bytes 8388608 | tf_op jit(solution)/shard_map/attend_back/pallas_call | solution.py:564
  275.1 8.1 %project_back.1 = (bf16[1024,512]{1,0:T(8,128)(2,1)}, bf16[512,2048]{1,0:T(8,128)(2,1)}, bf16[512,2048]{1,0:T(8,128)(2,1)}, f32[1,1024]{1,0:T(1,128)}, f32[1,128]{1,0:T(1,128)}) custom-call(bf16[1024,256]{1,0:T(8,128)(2,1)} %get-tuple-element.56.low_ref, f32[1024,128]{1,0:T(8,128)} %get-tuple-element.57.dk_ref, f32[1024,128]{1,0:T(8,128)} %get-tuple-element.58.dv_ref, ...), custom_call_target="tpu_custom_call" | custom-call | flops 1073741824 | bytes 12582912 | tf_op jit(solution)/shard_map/project_back/pallas_call | solution.py:646
  291.7 9.0 %collective-permute-done.42 = bf16[256,768]{1,0:T(8,128)(2,1)S(1)} collective-permute-done((bf16[256,768]{1,0:T(8,128)(2,1)S(1)}, bf16[256,768]{1,0:T(8,128)(2,1)S(1)}, u32[]{:S(2)}, u32[]{:S(2)}) %collective-permute-start.42) | collective-permute-done | bytes 393248 | tf_op jit(solution)/shard_map/ppermute | solution.py:38
  302.2 12.5 %collective-permute-done.41 = bf16[256,768]{1,0:T(8,128)(2,1)S(1)} collective-permute-done((bf16[256,768]{1,0:T(8,128)(2,1)S(1)}, bf16[256,768]{1,0:T(8,128)(2,1)S(1)}, u32[]{:S(2)}, u32[]{:S(2)}) %collective-permute-start.41) | collective-permute-done | bytes 393248 | tf_op jit(solution)/shard_map/ppermute | solution.py:38
  314.7 5.7 %collective-permute-done.43 = bf16[256,768]{1,0:T(8,128)(2,1)S(1)} collective-permute-done((bf16[256,768]{1,0:T(8,128)(2,1)S(1)}, bf16[256,768]{1,0:T(8,128)(2,1)S(1)}, u32[]{:S(2)}, u32[]{:S(2)}) %collective-permute-start.43) | collective-permute-done | bytes 393248 | tf_op jit(solution)/shard_map/ppermute | solution.py:38
  322.0 7.9 %collective-permute-done.45 = bf16[256,768]{1,0:T(8,128)(2,1)S(1)} collective-permute-done((bf16[256,768]{1,0:T(8,128)(2,1)S(1)}, bf16[256,768]{1,0:T(8,128)(2,1)S(1)}, u32[]{:S(2)}, u32[]{:S(2)}) %collective-permute-start.45) | collective-permute-done | bytes 393248 | tf_op jit(solution)/shard_map/ppermute | solution.py:38
  354.1 5.5 %collective-permute-done.37 = f32[2304]{0:T(1024)S(1)} collective-permute-done((f32[2304]{0:T(1024)S(1)}, f32[2304]{0:T(1024)S(1)}, u32[]{:S(2)}, u32[]{:S(2)}) %collective-permute-start.37) | collective-permute-done | bytes 9248 | tf_op jit(solution)/shard_map/ppermute | solution.py:38
  372.7 7.2 %place_columns.3 = (f32[256,3072]{1,0:T(8,128)}, f32[256,3072]{1,0:T(8,128)}, f32[256,3072]{1,0:T(8,128)}) custom-call(s32[5]{0:T(128)} %stack.65.index_ref, bf16[1024,1152]{1,0:T(8,128)(2,1)} %constant_dynamic-update-slice_fusion.21.even_ref, bf16[1024,1152]{1,0:T(8,128)(2,1)} %collective-permute-done.56.odd_ref), custom_call_target="tpu_custom_call" | custom-call | bytes 14155776 | tf_op jit(solution)/shard_map/place_columns/pallas_call | solution.py:235
  379.9 5.9 %place_columns.2 = (f32[256,2048]{1,0:T(8,128)}, f32[256,1024]{1,0:T(8,128)}, f32[256,1024]{1,0:T(8,128)}, f32[256,2048]{1,0:T(8,128)}) custom-call(s32[5]{0:T(128)} %stack.65.index_ref, bf16[1024,768]{1,0:T(8,128)(2,1)} %copy-done.10, bf16[1024,768]{1,0:T(8,128)(2,1)} %collective-permute-done.48.odd_ref), custom_call_target="tpu_custom_call" | custom-call | bytes 9437184 | tf_op jit(solution)/shard_map/place_columns/pallas_call | solution.py:235
  (290 shorter events, 165.3 us)
Async XLA Ops:
  28.4 36.8 %collective-permute-start.4 = (bf16[512,2048]{1,0:T(8,128)(2,1)S(1)}, bf16[512,2048]{1,0:T(8,128)(2,1)}, u32[]{:S(2)}, u32[]{:S(2)}) collective-permute-start(bf16[512,2048]{1,0:T(8,128)(2,1)S(1)} %constant_dynamic-update-slice_fusion.x_even.c_even), channel_id=1, source_target_pairs={{0,1},{1,0},{2,3},{3,2},{4,5},{5,4},{6,7},{7,6},{8,9},{9,8},{10,11... | collective-permute-start | bytes 6291464 | tf_op jit(solution)/shard_map/ppermute | solution.py:38
  31.6 21.1 %collective-permute-start.6 = (bf16[256,768]{1,0:T(8,128)(2,1)}, bf16[256,768]{1,0:T(8,128)(2,1)S(1)}, u32[]{:S(2)}, u32[]{:S(2)}) collective-permute-start(bf16[256,768]{1,0:T(8,128)(2,1)} %pick_columns.2), channel_id=1, source_target_pairs={{0,16},{8,24},{16,0},{24,8},{1,17},{9,25},{17,1},{25,9},{2,18},{10... | collective-permute-start | bytes 1179656 | tf_op jit(solution)/shard_map/ppermute | solution.py:38
  34.2 24.9 %collective-permute-start.5 = (bf16[256,768]{1,0:T(8,128)(2,1)}, bf16[256,768]{1,0:T(8,128)(2,1)S(1)}, u32[]{:S(2)}, u32[]{:S(2)}) collective-permute-start(bf16[256,768]{1,0:T(8,128)(2,1)} %pick_columns.2), channel_id=1, source_target_pairs={{0,8},{8,0},{16,24},{24,16},{1,9},{9,1},{17,25},{25,17},{2,10},{10... | collective-permute-start | bytes 1179656 | tf_op jit(solution)/shard_map/ppermute | solution.py:38
  110.0 26.6 %collective-permute-start.19 = (bf16[256,1152]{1,0:T(8,128)(2,1)}, bf16[256,1152]{1,0:T(8,128)(2,1)S(1)}, u32[]{:S(2)}, u32[]{:S(2)}) collective-permute-start(bf16[256,1152]{1,0:T(8,128)(2,1)} %pick_columns.3), channel_id=1, source_target_pairs={{0,16},{8,24},{16,0},{24,8},{1,17},{9,25},{17,1},{25,9},{2,18},{10... | collective-permute-start | bytes 1769480 | tf_op jit(solution)/shard_map/ppermute | solution.py:38
  120.5 42.9 %collective-permute-start.17 = (bf16[512,1024]{1,0:T(8,128)(2,1)}, bf16[512,1024]{1,0:T(8,128)(2,1)}, u32[]{:S(2)}, u32[]{:S(2)}) collective-permute-start(bf16[512,1024]{1,0:T(8,128)(2,1)} %constant_dynamic-update-slice_fusion.5.x_even), channel_id=1, source_target_pairs={{0,1},{1,0},{2,3},{3,2},{4,5},{5,4},{6,7},{7,6},{8,9},{9,8},{10,11... | collective-permute-start | bytes 3145736 | tf_op jit(solution)/shard_map/ppermute | solution.py:38
  120.5 27.8 %collective-permute-start.18 = (bf16[256,1152]{1,0:T(8,128)(2,1)}, bf16[256,1152]{1,0:T(8,128)(2,1)S(1)}, u32[]{:S(2)}, u32[]{:S(2)}) collective-permute-start(bf16[256,1152]{1,0:T(8,128)(2,1)} %pick_columns.3), channel_id=1, source_target_pairs={{0,8},{8,0},{16,24},{24,16},{1,9},{9,1},{17,25},{25,17},{2,10},{10... | collective-permute-start | bytes 1769480 | tf_op jit(solution)/shard_map/ppermute | solution.py:38
  136.6 23.8 %collective-permute-start.20 = (bf16[256,1152]{1,0:T(8,128)(2,1)S(1)}, bf16[256,1152]{1,0:T(8,128)(2,1)S(1)}, u32[]{:S(2)}, u32[]{:S(2)}) collective-permute-start(bf16[256,1152]{1,0:T(8,128)(2,1)S(1)} %collective-permute-done.19), channel_id=1, source_target_pairs={{0,8},{8,0},{16,24},{24,16},{1,9},{9,1},{17,25},{25,17},{2,10},{10... | collective-permute-start | bytes 1769480 | tf_op jit(solution)/shard_map/ppermute | solution.py:38
  184.1 16.5 %collective-permute-start.50 = (bf16[256,1152]{1,0:T(8,128)(2,1)}, bf16[256,1152]{1,0:T(8,128)(2,1)}, u32[]{:S(2)}, u32[]{:S(2)}) collective-permute-start(bf16[256,1152]{1,0:T(8,128)(2,1)} %get-tuple-element.97), channel_id=1, source_target_pairs={{0,8},{8,0},{16,24},{24,16},{1,9},{9,1},{17,25},{25,17},{2,10},{10... | collective-permute-start | bytes 1769480 | tf_op jit(solution)/shard_map/ppermute | solution.py:38
  185.3 37.4 %collective-permute-start.49 = (bf16[256,1152]{1,0:T(8,128)(2,1)S(1)}, bf16[256,1152]{1,0:T(8,128)(2,1)S(1)}, u32[]{:S(2)}, u32[]{:S(2)}) collective-permute-start(bf16[256,1152]{1,0:T(8,128)(2,1)S(1)} %copy-done.22), channel_id=1, source_target_pairs={{0,8},{8,0},{16,24},{24,16},{1,9},{9,1},{17,25},{25,17},{2,10},{10... | collective-permute-start | bytes 1769480 | tf_op jit(solution)/shard_map/ppermute | solution.py:38
  188.8 16.3 %collective-permute-start.25 = (bf16[128,1024]{1,0:T(8,128)(2,1)S(1)}, bf16[128,1024]{1,0:T(8,128)(2,1)S(1)}, u32[]{:S(2)}, u32[]{:S(2)}) collective-permute-start(bf16[128,1024]{1,0:T(8,128)(2,1)S(1)} %pad_maximum_fusion.12), channel_id=1, source_target_pairs={{0,4},{1,5},{2,6},{3,7},{4,0},{5,1},{6,2},{7,3},{8,12},{9,13},{10,... | collective-permute-start | bytes 786440 | tf_op jit(solution)/shard_map/ppermute | solution.py:38
  201.9 27.9 %collective-permute-start.51 = (bf16[256,1152]{1,0:T(8,128)(2,1)S(1)}, bf16[256,1152]{1,0:T(8,128)(2,1)S(1)}, u32[]{:S(2)}, u32[]{:S(2)}) collective-permute-start(bf16[256,1152]{1,0:T(8,128)(2,1)S(1)} %add_convert_fusion.1), channel_id=1, source_target_pairs={{0,16},{8,24},{16,0},{24,8},{1,17},{9,25},{17,1},{25,9},{2,18},{10... | collective-permute-start | bytes 1769480 | tf_op jit(solution)/shard_map/ppermute | solution.py:38
  206.4 26.4 %collective-permute-start.27 = (bf16[128,1024]{1,0:T(8,128)(2,1)S(1)}, bf16[128,1024]{1,0:T(8,128)(2,1)S(1)}, u32[]{:S(2)}, u32[]{:S(2)}) collective-permute-start(bf16[128,1024]{1,0:T(8,128)(2,1)S(1)} %get-tuple-element.84), channel_id=1, source_target_pairs={{0,4},{1,5},{2,6},{3,7},{4,0},{5,1},{6,2},{7,3},{8,12},{9,13},{10,... | collective-permute-start | bytes 786440 | tf_op jit(solution)/shard_map/ppermute | solution.py:38
  206.7 26.7 %collective-permute-start.26 = (bf16[128,1024]{1,0:T(8,128)(2,1)S(1)}, bf16[128,1024]{1,0:T(8,128)(2,1)S(1)}, u32[]{:S(2)}, u32[]{:S(2)}) collective-permute-start(bf16[128,1024]{1,0:T(8,128)(2,1)S(1)} %get-tuple-element.84), channel_id=1, source_target_pairs={{0,2},{1,3},{2,0},{3,1},{4,6},{5,7},{6,4},{7,5},{8,10},{9,11},{10,... | collective-permute-start | bytes 786440 | tf_op jit(solution)/shard_map/ppermute | solution.py:38
  230.9 20.4 %collective-permute-start.53 = (bf16[256,1152]{1,0:T(8,128)(2,1)S(1)}, bf16[256,1152]{1,0:T(8,128)(2,1)S(1)}, u32[]{:S(2)}, u32[]{:S(2)}) collective-permute-start(bf16[256,1152]{1,0:T(8,128)(2,1)S(1)} %get-tuple-element.80), channel_id=1, source_target_pairs={{0,4},{1,5},{2,6},{3,7},{4,0},{5,1},{6,2},{7,3},{8,12},{9,13},{10,... | collective-permute-start | bytes 1769480 | tf_op jit(solution)/shard_map/ppermute | solution.py:38
  231.3 21.5 %collective-permute-start.52 = (bf16[256,1152]{1,0:T(8,128)(2,1)S(1)}, bf16[256,1152]{1,0:T(8,128)(2,1)S(1)}, u32[]{:S(2)}, u32[]{:S(2)}) collective-permute-start(bf16[256,1152]{1,0:T(8,128)(2,1)S(1)} %get-tuple-element.80), channel_id=1, source_target_pairs={{0,2},{1,3},{2,0},{3,1},{4,6},{5,7},{6,4},{7,5},{8,10},{9,11},{10,... | collective-permute-start | bytes 1769480 | tf_op jit(solution)/shard_map/ppermute | solution.py:38
  247.2 15.4 %collective-permute-start.30 = (bf16[512,1024]{1,0:T(8,128)(2,1)S(1)}, bf16[512,1024]{1,0:T(8,128)(2,1)S(1)}, u32[]{:S(2)}, u32[]{:S(2)}) collective-permute-start(bf16[512,1024]{1,0:T(8,128)(2,1)S(1)} %constant_dynamic-update-slice_fusion.10.g_even), channel_id=1, source_target_pairs={{0,1},{1,0},{2,3},{3,2},{4,5},{5,4},{6,7},{7,6},{8,9},{9,8},{10,11... | collective-permute-start | bytes 3145736 | tf_op jit(solution)/shard_map/ppermute | solution.py:38
  251.3 37.3 %collective-permute-start.55 = (bf16[128,1152]{1,0:T(8,128)(2,1)S(1)}, bf16[128,1152]{1,0:T(8,128)(2,1)S(1)}, u32[]{:S(2)}, u32[]{:S(2)}) collective-permute-start(bf16[128,1152]{1,0:T(8,128)(2,1)S(1)} %slice.380), channel_id=1, source_target_pairs={{0,2},{1,3},{2,0},{3,1},{4,6},{5,7},{6,4},{7,5},{8,10},{9,11},{10,... | collective-permute-start | bytes 884744 | tf_op jit(solution)/shard_map/ppermute | solution.py:38
  283.3 49.1 %collective-permute-start.31 = (bf16[512,2048]{1,0:T(8,128)(2,1)}, bf16[512,2048]{1,0:T(8,128)(2,1)S(1)}, u32[]{:S(2)}, u32[]{:S(2)}) collective-permute-start(bf16[512,2048]{1,0:T(8,128)(2,1)} %get-tuple-element.61), channel_id=1, source_target_pairs={{0,1},{1,0},{2,3},{3,2},{4,5},{5,4},{6,7},{7,6},{8,9},{9,8},{10,11... | collective-permute-start | bytes 6291464 | tf_op jit(solution)/shard_map/ppermute | solution.py:38
  289.4 83.3 %collective-permute-start.56 = (bf16[1024,1152]{1,0:T(8,128)(2,1)}, bf16[1024,1152]{1,0:T(8,128)(2,1)}, u32[]{:S(2)}, u32[]{:S(2)}) collective-permute-start(bf16[1024,1152]{1,0:T(8,128)(2,1)} %constant_dynamic-update-slice_fusion.21.even_ref), channel_id=1, source_target_pairs={{0,1},{1,0},{2,3},{3,2},{4,5},{5,4},{6,7},{7,6},{8,9},{9,8},{10,11... | collective-permute-start | bytes 7077896 | tf_op jit(solution)/shard_map/ppermute | solution.py:38
  289.9 24.8 %collective-permute-start.41 = (bf16[256,768]{1,0:T(8,128)(2,1)S(1)}, bf16[256,768]{1,0:T(8,128)(2,1)S(1)}, u32[]{:S(2)}, u32[]{:S(2)}) collective-permute-start(bf16[256,768]{1,0:T(8,128)(2,1)S(1)} %get-tuple-element.114), channel_id=1, source_target_pairs={{0,8},{8,0},{16,24},{24,16},{1,9},{9,1},{17,25},{25,17},{2,10},{10... | collective-permute-start | bytes 1179656 | tf_op jit(solution)/shard_map/ppermute | solution.py:38
  300.7 19.6 %collective-permute-start.43 = (bf16[256,768]{1,0:T(8,128)(2,1)S(1)}, bf16[256,768]{1,0:T(8,128)(2,1)S(1)}, u32[]{:S(2)}, u32[]{:S(2)}) collective-permute-start(bf16[256,768]{1,0:T(8,128)(2,1)S(1)} %add_convert_fusion.3), channel_id=1, source_target_pairs={{0,16},{8,24},{16,0},{24,8},{1,17},{9,25},{17,1},{25,9},{2,18},{10... | collective-permute-start | bytes 1179656 | tf_op jit(solution)/shard_map/ppermute | solution.py:38
  343.2 36.7 %collective-permute-start.48 = (bf16[1024,768]{1,0:T(8,128)(2,1)S(1)}, bf16[1024,768]{1,0:T(8,128)(2,1)}, u32[]{:S(2)}, u32[]{:S(2)}) collective-permute-start(bf16[1024,768]{1,0:T(8,128)(2,1)S(1)} %constant_dynamic-update-slice_fusion.16.even_ref), channel_id=1, source_target_pairs={{0,1},{1,0},{2,3},{3,2},{4,5},{5,4},{6,7},{7,6},{8,9},{9,8},{10,11... | collective-permute-start | bytes 4718600 | tf_op jit(solution)/shard_map/ppermute | solution.py:38
  344.3 41.5 %collective-permute-start.33 = (bf16[128,2048]{1,0:T(8,128)(2,1)}, bf16[128,2048]{1,0:T(8,128)(2,1)}, u32[]{:S(2)}, u32[]{:S(2)}) collective-permute-start(bf16[128,2048]{1,0:T(8,128)(2,1)} %pad_maximum_fusion.6), channel_id=1, source_target_pairs={{0,2},{1,3},{2,0},{3,1},{4,6},{5,7},{6,4},{7,5},{8,10},{9,11},{10,... | collective-permute-start | bytes 1572872 | tf_op jit(solution)/shard_map/ppermute | solution.py:38
  349.7 36.1 %collective-permute-start.35 = (bf16[128,2048]{1,0:T(8,128)(2,1)}, bf16[128,2048]{1,0:T(8,128)(2,1)}, u32[]{:S(2)}, u32[]{:S(2)}) collective-permute-start(bf16[128,2048]{1,0:T(8,128)(2,1)} %pad_maximum_fusion.7), channel_id=1, source_target_pairs={{0,4},{1,5},{2,6},{3,7},{4,0},{5,1},{6,2},{7,3},{8,12},{9,13},{10,... | collective-permute-start | bytes 1572872 | tf_op jit(solution)/shard_map/ppermute | solution.py:38
  (71 other events, 697.4 us)
where the time goes:
time: 390 us; the launch traced here: 389 us
  waiting for transfers between devices  199 us (51%)
  Pallas kernels  67.8 us (17%)
  starting transfers between devices  60.9 us (16%)
  other arithmetic  28.2 us (7%)
  local copies, waits for them, and re-layouts  20.2 us (5%)
  matrix products  11.3 us (3%)
    ppermute x57, waiting for transfers between devices, exchange(): lax.ppermute(value, axis, [(index, index ^ bit) for index in range(count)])  199 us
    ppermute x57, starting transfers between devices, exchange(): lax.ppermute(value, axis, [(index, index ^ bit) for index in range(count)])  60.9 us
    pallas_call x2, Pallas kernels, place_columns(): pl.pallas_call(kernel, out_shape=[jax.ShapeDtypeStruct((rows, count * wid...  13 us
    pallas_call x1, Pallas kernels, attend_back(): pl.pallas_call(attend_back_kernel, out_shape=[jax.ShapeDtypeStruct((total...  11.6 us
    pallas_call x1, Pallas kernels, attend(): pl.pallas_call(attend_kernel, out_shape=[jax.ShapeDtypeStruct((total, q_w...  11.2 us
    pallas_call x1, Pallas kernels, mlp_both(): pl.pallas_call(mlp_kernel, out_shape=[jax.ShapeDtypeStruct((total, 2 * hi...  10.7 us
    unnamed x101, local copies, waits for them, and re-layouts  9.59 us
    pallas_call x1, Pallas kernels, project_back(): pl.pallas_call(project_back_kernel, out_shape=[jax.ShapeDtypeStruct((tota...  8.15 us
  transfers between devices with their start and end apart: 57, of which 32 were waited for; matrix products, arithmetic and copies ran while one was open for 12% of the time, Pallas kernels for 10%

commit v1 on v0

v1 whole, which is shorter than its diff:
```python
import functools
import math

import jax
import jax.numpy as jnp
from jax import lax
from jax.experimental import pallas as pl
from jax.experimental.pallas import tpu as pltpu
from jax.sharding import PartitionSpec as P


NORM_EPS = 1e-06
ROPE_BASE = 1000000.0
MASKED = -1e30
F32 = jnp.float32
BF16 = jnp.bfloat16


def rms_norm(values, gain_vec):
    return (
        values * lax.rsqrt(jnp.mean(values * values, axis=-1, keepdims=True) + NORM_EPS) * gain_vec
    )


def times_transposed(lhs_mat, rhs_mat):
    return lax.dot_general(
        lhs_mat, rhs_mat, (((1,), (1,)), ((), ())), preferred_element_type=F32
    )


def transposed_times(lhs_mat, rhs_mat):
    return lax.dot_general(
        lhs_mat, rhs_mat, (((0,), (0,)), ((), ())), preferred_element_type=F32
    )


def tie(*values):
    return lax.optimization_barrier(values)


def exchange(value, bit, axis):
    count = lax.axis_size(axis)
    return lax.ppermute(value, axis, [(index, index ^ bit) for index in range(count)])


def low_bit(number):
    return number & -number


def top_bit(number):
    return 1 << (number.bit_length() - 1)


def level_of(number):
    return bin(number).count("1")


def even_numbers(count, level):
    return [number for number in range(0, count, 2) if level_of(number) == level]


def gather_levels(count):
    return (count // 2).bit_length() - 1


def gather_ctx(own):
    count = lax.axis_size("ctx")
    rows = own.shape[0]
    half = rows // 2
    parts = {0: [own]}
    for level in range(1, gather_levels(count) + 1):
        for number in even_numbers(count, level):
            low, top = low_bit(number), top_bit(number)
            if level == 1:
                parts[number] = [exchange(own, low, "ctx")]
            else:
                parts[number] = [
                    exchange(rows_of(parts[number ^ top], 0, half), top, "ctx"),
                    exchange(rows_of(parts[number ^ low], half, rows), low, "ctx"),
                ]
    pieces = []
    for number in range(0, count, 2):
        start = number // 2 * rows
        for part in parts[number]:
            pieces.append((0, start, part))
            other = exchange(part, 1, "ctx")
            pieces.append((1, start, other))
            start += part.shape[0]
    return pieces


def rows_of(parts, start, stop):
    if len(parts) > 1:
        return parts[0 if start == 0 else 1]
    return parts[0][start:stop]


def fetch_pieces(step, refs, plan, buffers, sems, block_rows, columns=None):
    copies = []
    for number, (ref, (odd, start, rows)) in enumerate(zip(refs, plan)):
        source = ref if columns is None else ref.at[:, columns]
        copies.append(
            (
                start // block_rows,
                pltpu.make_async_copy(
                    source, buffers[odd].at[pl.ds(start, rows), :], sems.at[number]
                ),
            )
        )

    @pl.when(step == 0)
    def _():
        for _, copy in copies:
            copy.start()

    for block in range(buffers[0].shape[0] // block_rows):

        @pl.when(step == block)
        def _():
            for owner, copy in copies:
                if owner == block:
                    copy.wait()


def piece_plan(pieces):
    return [(odd, start, array.shape[0]) for odd, start, array in pieces]


def piece_arrays(pieces):
    return [array for _, _, array in pieces]


def piece_scratch(pieces, rows, width):
    return [
        pltpu.VMEM((rows, width), BF16),
        pltpu.VMEM((rows, width), BF16),
        pltpu.SemaphoreType.DMA((len(pieces),)),
    ]


def in_place(pieces):
    return [pl.BlockSpec(memory_space=pl.ANY)] * len(pieces)


def first_sums_kernel(even_ref, odd_ref, first_ref, second_ref):
    half = first_ref.shape[0]
    total = (even_ref[...].astype(F32) + odd_ref[...].astype(F32)).astype(BF16)
    first_ref[...] = total[:half]
    second_ref[...] = total[half:]


def next_sums_kernel(even_two, odd_two, even_four, odd_four, first, second, two_ref, four_ref):
    half = first.shape[0]
    two = even_two[...].astype(F32) + odd_two[...].astype(F32)
    two_ref[:half, :] = (two[:half] + first[...].astype(F32)).astype(BF16)
    two_ref[half:, :] = two[half:].astype(BF16)
    four = even_four[...].astype(F32) + odd_four[...].astype(F32)
    four_ref[:half, :] = four[:half].astype(BF16)
    four_ref[half:, :] = (four[half:] + second[...].astype(F32)).astype(BF16)


def scatter_eight(even, odd):
    moved = exchange(odd, 1, "ctx")
    rows = even.shape[0] // 4
    half = rows // 2
    width = even.shape[1]

    def block(number):
        return pl.BlockSpec((rows, width), lambda step: (number, 0))

    part = pl.BlockSpec((half, width), lambda step: (0, 0))
    cost = pl.CostEstimate(flops=0, bytes_accessed=8 * rows * width, transcendentals=0)
    first, second = pl.pallas_call(
        first_sums_kernel,
        out_shape=[jax.ShapeDtypeStruct((half, width), BF16)] * 2,
        grid=(1,),
        in_specs=[block(3), block(3)],
        out_specs=[part, part],
        cost_estimate=cost,
        name="first_sums",
    )(even, moved)
    first = exchange(first, 4, "ctx")
    second = exchange(second, 2, "ctx")
    two, four = pl.pallas_call(
        next_sums_kernel,
        out_shape=[jax.ShapeDtypeStruct((rows, width), BF16)] * 2,
        grid=(1,),
        in_specs=[block(1), block(1), block(2), block(2), part, part],
        out_specs=[block(0), block(0)],
        cost_estimate=cost,
        name="next_sums",
    )(even, moved, even, moved, first, second)
    two = exchange(two, 2, "ctx")
    four = exchange(four, 4, "ctx")
    return (
        (even[:rows].astype(F32) + moved[:rows].astype(F32))
        + two.astype(F32)
        + four.astype(F32)
    )


def scatter_ctx(even, odd):
    count = lax.axis_size("ctx")
    if count == 8:
        return scatter_eight(even, odd)
    rows = even.shape[0] * 2 // count
    half = rows // 2
    moved = exchange(odd, 1, "ctx")

    def piece(number, start, stop):
        base = number // 2 * rows
        return even[base + start : base + stop].astype(F32) + moved[
            base + start : base + stop
        ].astype(F32)

    halves = {
        number: [piece(number, 0, half), piece(number, half, rows)]
        for number in range(0, count, 2)
    }
    for level in range(gather_levels(count), 1, -1):
        for number in even_numbers(count, level):
            low, top = low_bit(number), top_bit(number)
            first, second = tie(*(part.astype(BF16) for part in halves[number]))
            halves[number ^ top][0] += exchange(first, top, "ctx").astype(F32)
            halves[number ^ low][1] += exchange(second, low, "ctx").astype(F32)
    total = jnp.concatenate(halves[0], axis=0)
    for number in even_numbers(count, 1):
        sent = jnp.concatenate(halves[number], axis=0).astype(BF16)
        total = total + exchange(sent, number, "ctx").astype(F32)
    return total


def gather_fsdp_step(blocks, count, level):
    blocks = dict(blocks)
    for number in range(1, count):
        if level_of(number) == level:
            low = low_bit(number)
            blocks[number] = exchange(blocks[number ^ low], low, "fsdp")
    return blocks


def scatter_fsdp_step(sums, count, level):
    sums = dict(sums)
    for number in range(1, count):
        if level_of(number) == level:
            low = low_bit(number)
            sums[number ^ low] = sums[number ^ low].astype(F32) + exchange(
                sums[number].astype(BF16), low, "fsdp"
            ).astype(F32)
    return sums


def sum_all(value):
    for axis in ("ctx", "fsdp"):
        bit = 1
        while bit < lax.axis_size(axis):
            value = value + exchange(value, bit, axis)
            bit *= 2
    return value


def whole(array):
    return pl.BlockSpec(array.shape, lambda *ids: (0,) * len(array.shape))


def pick_columns(picks):
    rows = picks[0][0].shape[0]
    widths = [width for _, _, width in picks]
    if any(width % 128 for width in widths):
        return jnp.concatenate(
            [
                lax.dynamic_slice_in_dim(array, index * width, width, axis=1)
                for array, index, width in picks
            ],
            axis=1,
        )

    def kernel(index_ref, *refs):
        start = 0
        for ref, width in zip(refs, widths):
            refs[-1][:, start : start + width] = ref[...]
            start += width

    def spec(number, width):
        return pl.BlockSpec((rows, width), lambda step, index_ref: (0, index_ref[number]))

    total = sum(widths)
    return pl.pallas_call(
        kernel,
        out_shape=jax.ShapeDtypeStruct((rows, total), picks[0][0].dtype),
        grid_spec=pltpu.PrefetchScalarGridSpec(
            num_scalar_prefetch=1,
            grid=(1,),
            in_specs=[spec(number, width) for number, width in enumerate(widths)],
            out_specs=pl.BlockSpec((rows, total), lambda step, index_ref: (0, 0)),
        ),
        cost_estimate=pl.CostEstimate(
            flops=0, bytes_accessed=4 * rows * total, transcendentals=0
        ),
        name="pick_columns",
    )(jnp.stack([index for _, index, _ in picks]).astype(jnp.int32), *[p[0] for p in picks])


def place_columns(pieces, widths, ctx_index):
    count = lax.axis_size("ctx")
    rows = pieces[0][2].shape[0]
    starts = [sum(widths[:number]) for number in range(len(widths))]
    if any(width % 128 for width in widths):
        placed = []
        for start, width in zip(starts, widths):
            result = jnp.zeros((rows, count * width), F32)
            for odd, row, array in pieces:
                result = lax.dynamic_update_slice(
                    result,
                    array[:, start : start + width].astype(F32),
                    (row % rows, (ctx_index ^ (row // rows * 2 + odd)) * width),
                )
            placed.append(result)
        return placed
    plan = piece_plan(pieces)

    def kernel(index_ref, *refs):
        step = pl.program_id(0)
        out_refs = refs[len(plan) : len(plan) + len(widths)]
        buffers, sems = refs[-3:-1], refs[-1]
        fetch_pieces(step, refs[: len(plan)], plan, buffers, sems, rows)
        here = pl.ds(pl.multiple_of(step * rows, rows), rows)
        for parity in range(2):

            @pl.when(index_ref[0] == parity)
            def _():
                sides = (buffers[1], buffers[0]) if parity else buffers
                for out_ref, start, width in zip(out_refs, starts, widths):
                    for side, ref in enumerate(sides):
                        out_ref[:, side * width : (side + 1) * width] = ref[
                            here, start : start + width
                        ].astype(F32)

    index = [ctx_index % 2] + [(ctx_index ^ number) // 2 for number in range(0, count, 2)]
    return pl.pallas_call(
        kernel,
        out_shape=[jax.ShapeDtypeStruct((rows, count * width), F32) for width in widths],
        grid_spec=pltpu.PrefetchScalarGridSpec(
            num_scalar_prefetch=1,
            grid=(count // 2,),
            in_specs=in_place(pieces),
            out_specs=[
                pl.BlockSpec((rows, 2 * width), lambda step, index_ref: (0, index_ref[step + 1]))
                for width in widths
            ],
            scratch_shapes=piece_scratch(pieces, rows * count // 2, sum(widths)),
        ),
        cost_estimate=pl.CostEstimate(
            flops=0, bytes_accessed=6 * count * rows * sum(widths), transcendentals=0
        ),
        name="place_columns",
    )(jnp.stack(index).astype(jnp.int32), *piece_arrays(pieces))


def own_kernel(index_ref, hidden_ref, cot_ref, both_ref):
    width = hidden_ref.shape[1]
    count = index_ref.shape[0]
    size = width // count
    for number in range(count):
        source = pl.ds(pl.multiple_of(index_ref[number] * size, size), size)
        target = slice(number * size, (number + 1) * size)
        both_ref[:, target] = hidden_ref[:, source]
        both_ref[:, width + target.start : width + target.stop] = cot_ref[:, source]


def own_blocks(hidden, cot, indices):
    rows, width = hidden.shape
    return pl.pallas_call(
        own_kernel,
        out_shape=jax.ShapeDtypeStruct((rows, 2 * width), BF16),
        in_specs=[pl.BlockSpec(memory_space=pltpu.SMEM)]
        + [pl.BlockSpec(memory_space=pltpu.VMEM)] * 2,
        out_specs=pl.BlockSpec(memory_space=pltpu.VMEM),
        cost_estimate=pl.CostEstimate(
            flops=0, bytes_accessed=8 * rows * width, transcendentals=0
        ),
        name="own_blocks",
    )(indices, hidden, cot)


def here_rows(buffers, step, rows):
    here = pl.ds(pl.multiple_of(step * rows, rows), rows)
    return jnp.concatenate([buffers[0][here, :], buffers[1][here, :]], axis=0)


def mlp_kernel(plan, chunks, *refs):
    pieces, refs = refs[: len(plan)], refs[len(plan) :]
    c_ref, w_refs, refs = refs[0], refs[1 : 1 + chunks], refs[1 + chunks :]
    right_ref, act_ref, even_ref, odd_ref, x_all = refs[:5]
    buffers, sems = refs[5:7], refs[7]
    step = pl.program_id(0)
    hidden = act_ref.shape[1]
    rows = even_ref.shape[0]
    size = even_ref.shape[1] // chunks
    fetch_pieces(step, pieces, plan, buffers, sems, rows)
    x = here_rows(buffers, step, rows)
    x_all[...] = x
    c = c_ref[...]
    both = jnp.zeros((2 * rows, 2 * hidden), F32)
    grad = jnp.zeros((2 * rows, hidden), F32)
    for number, w_ref in enumerate(w_refs):
        side = slice(number * size, (number + 1) * size)
        both += jnp.dot(x[:, side], w_ref[:, : 2 * hidden], preferred_element_type=F32)
        grad += jnp.dot(c[:, side], w_ref[:, 2 * hidden :], preferred_element_type=F32)
    gate = both[:, :hidden]
    upper = both[:, hidden:]
    sigma = jax.nn.sigmoid(gate)
    gate_sigma = gate * sigma
    act_ref[...] = (gate_sigma * upper).astype(BF16)
    right_ref[:, :hidden] = (grad * upper * sigma * (1.0 + gate * (1.0 - sigma))).astype(BF16)
    right_ref[:, hidden:] = (grad * gate_sigma).astype(BF16)
    right = right_ref[...]
    for number, w_ref in enumerate(w_refs):
        part = nt(right, w_ref[:, : 2 * hidden]).astype(BF16)
        even_ref[:, number * size : (number + 1) * size] = part[:rows]
        odd_ref[:, number * size : (number + 1) * size] = part[rows:]


def mlp_both(pieces, both_all, weights, count):
    total, width = both_all.shape
    width //= 2
    rows = total // count
    hidden = weights[0].shape[1] // 3
    block = pl.BlockSpec((rows, width), lambda step: (step, 0))

    def wide(columns):
        return pl.BlockSpec((2 * rows, columns), lambda step: (step, 0))

    return pl.pallas_call(
        functools.partial(mlp_kernel, piece_plan(pieces), len(weights)),
        out_shape=[
            jax.ShapeDtypeStruct((total, 2 * hidden), BF16),
            jax.ShapeDtypeStruct((total, hidden), BF16),
            jax.ShapeDtypeStruct((total // 2, width), BF16),
            jax.ShapeDtypeStruct((total // 2, width), BF16),
            jax.ShapeDtypeStruct((total, width), BF16),
        ],
        grid=(count // 2,),
        in_specs=in_place(pieces)
        + [pl.BlockSpec((2 * rows, width), lambda step: (step, 1))]
        + [whole(part) for part in weights],
        out_specs=[wide(2 * hidden), wide(hidden), block, block, wide(width)],
        scratch_shapes=piece_scratch(pieces, total // 2, width),
        cost_estimate=pl.CostEstimate(
            flops=10 * total * width * hidden,
            bytes_accessed=12 * total * width,
            transcendentals=total * hidden,
        ),
        name="mlp_both",
    )(*piece_arrays(pieces), both_all, *weights)


def grads_kernel(left_one, right_one, left_two, right_two, *out_refs):
    split = right_one.shape[1]
    for number, out_ref in enumerate(out_refs):

        @pl.when(pl.program_id(0) == number)
        def _():
            out_ref[:, :split] = transposed_times(left_one[...], right_one[...]).astype(BF16)
            out_ref[:, split:] = transposed_times(left_two[...], right_two[...]).astype(BF16)


def weight_grads(left_one, right_one, left_two, right_two, skipped=0):
    chunks = lax.axis_size("fsdp")
    total, width = left_one.shape
    size = width // chunks
    columns = right_one.shape[1] + right_two.shape[1]
    block = pl.BlockSpec((total, size), lambda step: (0, step))
    return pl.pallas_call(
        grads_kernel,
        out_shape=[jax.ShapeDtypeStruct((size, columns), BF16)] * chunks,
        grid=(chunks,),
        in_specs=[
            block,
            whole(right_one),
            pl.BlockSpec((total, size), lambda step: (0, skipped + step)),
            whole(right_two),
        ],
        out_specs=[pl.BlockSpec((size, columns), lambda step: (0, 0))] * chunks,
        cost_estimate=pl.CostEstimate(
            flops=2 * total * width * columns,
            bytes_accessed=4 * total * (width + columns),
            transcendentals=0,
        ),
        name="weight_grads",
    )(left_one, right_one, left_two, right_two)


def rotated(values, cosine, sine_part):
    return values * cosine + pltpu.roll(values, values.shape[1] // 2, 1) * sine_part


def head_scale(raw):
    return lax.rsqrt(jnp.mean(raw * raw, axis=-1, keepdims=True) + NORM_EPS)


def head_back(grad, raw, gain_row, cosine, sine_part):
    turned = grad * cosine + pltpu.roll(grad * sine_part, grad.shape[1] // 2, 1)
    scale = head_scale(raw)
    scaled = turned * gain_row
    mean_part = jnp.mean(scaled * raw, axis=-1, keepdims=True)
    return scale * scaled - raw * (scale * scale * scale * mean_part), turned * raw * scale


def project_kernel(plan, chunks, *refs):
    pieces, refs = refs[: len(plan)], refs[len(plan) :]
    w_refs, refs = refs[:chunks], refs[chunks:]
    gain_ref, qgain_ref, kgain_ref, cos_ref, sin_ref = refs[:5]
    in_ref, raw_ref, q_ref, k_ref, v_ref, both_ref = refs[5:11]
    buffers, sems = refs[11:13], refs[13]
    step = pl.program_id(0)
    head = qgain_ref.shape[1]
    q_width = q_ref.shape[1]
    kv_width = k_ref.shape[1]
    width = in_ref.shape[1]
    size = width // chunks
    rows = in_ref.shape[0] // 2
    fetch_pieces(step, pieces, plan, buffers, sems, rows)
    both = here_rows(buffers, step, rows)
    both_ref[...] = both
    normed = rms_norm(both[:, :width].astype(F32), gain_ref[...]).astype(BF16)
    in_ref[...] = normed
    raw = jnp.zeros((2 * rows, q_width + 2 * kv_width), F32)
    for number, w_ref in enumerate(w_refs):
        raw += jnp.dot(
            normed[:, number * size : (number + 1) * size],
            w_ref[...],
            preferred_element_type=F32,
        )
    raw_ref[...] = raw[:, : q_width + kv_width]
    cosine = cos_ref[...]
    sine_part = sin_ref[...]
    for column in range(0, q_width, head):
        part = raw[:, column : column + head]
        q_ref[:, column : column + head] = rotated(
            part * head_scale(part) * qgain_ref[...], cosine, sine_part
        ).astype(BF16)
    for column in range(0, kv_width, head):
        part = raw[:, q_width + column : q_width + column + head]
        k_ref[:, column : column + head] = rotated(
            part * head_scale(part) * kgain_ref[...], cosine, sine_part
        ).astype(BF16)
    v_ref[...] = raw[:, q_width + kv_width :].astype(BF16)


def project(pieces, weights, gain, q_gain, k_gain, cosine, sine_part, q_width, kv_width):
    width = gain.shape[1]
    head = q_gain.shape[1]
    total = cosine.shape[0]
    steps = lax.axis_size("ctx") // 2
    rows = total // (2 * steps)

    def wide(columns):
        return pl.BlockSpec((2 * rows, columns), lambda step: (step, 0))

    first_columns = pl.BlockSpec(
        (weights[0].shape[0], q_width + 2 * kv_width), lambda step: (0, 0)
    )
    return pl.pallas_call(
        functools.partial(project_kernel, piece_plan(pieces), len(weights)),
        out_shape=[
            jax.ShapeDtypeStruct((total, width), BF16),
            jax.ShapeDtypeStruct((total, q_width + kv_width), F32),
            jax.ShapeDtypeStruct((total, q_width), BF16),
            jax.ShapeDtypeStruct((total, kv_width), BF16),
            jax.ShapeDtypeStruct((total, kv_width), BF16),
            jax.ShapeDtypeStruct((total, 2 * width), BF16),
        ],
        grid=(steps,),
        in_specs=in_place(pieces)
        + [first_columns] * len(weights)
        + [whole(gain), whole(q_gain), whole(k_gain), wide(head), wide(head)],
        out_specs=[
            wide(width), wide(q_width + kv_width), wide(q_width), wide(kv_width), wide(kv_width),
            wide(2 * width),
        ],
        scratch_shapes=piece_scratch(pieces, total // 2, 2 * width),
        cost_estimate=pl.CostEstimate(
            flops=2 * total * width * (q_width + 2 * kv_width),
            bytes_accessed=12 * total * width,
            transcendentals=total,
        ),
        name="project",
    )(*piece_arrays(pieces), *weights, gain, q_gain, k_gain, cosine, sine_part)


def nt(lhs, rhs):
    return lax.dot_general(lhs, rhs, (((1,), (1,)), ((), ())), preferred_element_type=F32)


def attend_kernel(chunks, q_ref, k_ref, v_ref, row_ref, col_ref, *refs):
    w_refs, refs = refs[:chunks], refs[chunks:]
    mix_ref, lse_ref, even_ref, odd_ref, vt_ref = refs
    kv_width = k_ref.shape[1]
    q_width = q_ref.shape[1]
    head = q_width // lse_ref.shape[0]
    group = q_width // kv_width
    scale = 1.0 / math.sqrt(head)

    @pl.when(pl.program_id(0) == 0)
    def _():
        vt_ref[...] = v_ref[...].astype(F32).T.astype(BF16)

    allowed = col_ref[...] <= row_ref[...]
    for number in range(q_width // head):
        kv = number // group * head
        column = number * head
        scores = jnp.where(
            allowed, nt(k_ref[:, kv : kv + head], q_ref[:, column : column + head]) * scale, MASKED
        )
        top = jnp.max(scores, axis=0, keepdims=True)
        raised = jnp.exp(scores - top)
        total = jnp.sum(raised, axis=0, keepdims=True)
        lse_ref[number : number + 1, :] = top + jnp.log(total)
        probs = (raised * (1.0 / total)).astype(BF16)
        mixed = jnp.dot(vt_ref[kv : kv + head, :], probs, preferred_element_type=F32)
        mix_ref[:, column : column + head] = mixed.T.astype(BF16)
    rows = even_ref.shape[0]
    size = even_ref.shape[1] // chunks
    mix = mix_ref[...]
    for number, w_ref in enumerate(w_refs):
        out = nt(mix, w_ref[...]).astype(BF16)
        even_ref[:, number * size : (number + 1) * size] = out[:rows]
        odd_ref[:, number * size : (number + 1) * size] = out[rows:]


def attend(q, k, v, pos_row, pos_col, weights, head):
    total, q_width = q.shape
    kv_width = k.shape[1]
    width = weights[0].shape[0] * len(weights)
    steps = lax.axis_size("ctx") // 2
    rows = total // (2 * steps)
    heads = q_width // head
    last_columns = pl.BlockSpec(
        (weights[0].shape[0], q_width), lambda step: (0, weights[0].shape[1] // q_width - 1)
    )

    def wide(columns):
        return pl.BlockSpec((2 * rows, columns), lambda step: (step, 0))

    half = pl.BlockSpec((rows, width), lambda step: (step, 0))
    return pl.pallas_call(
        functools.partial(attend_kernel, len(weights)),
        out_shape=[
            jax.ShapeDtypeStruct((total, q_width), BF16),
            jax.ShapeDtypeStruct((heads, total), F32),
            jax.ShapeDtypeStruct((total // 2, width), BF16),
            jax.ShapeDtypeStruct((total // 2, width), BF16),
        ],
        grid=(steps,),
        in_specs=[
            wide(q_width), whole(k), whole(v),
            pl.BlockSpec((1, 2 * rows), lambda step: (0, step)),
            whole(pos_col),
        ]
        + [last_columns] * len(weights),
        out_specs=[
            wide(q_width), pl.BlockSpec((heads, 2 * rows), lambda step: (0, step)), half, half,
        ],
        scratch_shapes=[pltpu.VMEM((kv_width, total), BF16)],
        cost_estimate=pl.CostEstimate(
            flops=4 * total * total * q_width,
            bytes_accessed=8 * total * width,
            transcendentals=total * total * heads,
        ),
        name="attend",
    )(q, k, v, pos_row, pos_col, *weights)


def attend_back_kernel(plan, chunks, *refs):
    pieces, refs = refs[: len(plan)], refs[len(plan) :]
    w_refs, refs = refs[:chunks], refs[chunks:]
    q_ref, k_ref, v_ref, row_ref, col_ref, mix_ref, lse_ref = refs[:7]
    raw_ref, qgain_ref, cos_ref, sin_ref = refs[7:11]
    low_ref, dk_ref, dv_ref, dgain_ref, all_ref = refs[11:16]
    buffers, sems, kt_ref = refs[16:18], refs[18], refs[19]
    step = pl.program_id(0)
    head = qgain_ref.shape[1]
    kv_width = k_ref.shape[1]
    q_width = q_ref.shape[1]
    group = q_width // kv_width
    scale = 1.0 / math.sqrt(head)
    rows = q_ref.shape[0] // 2
    size = all_ref.shape[1] // chunks

    @pl.when(pl.program_id(0) == 0)
    def _():
        kt_ref[...] = k_ref[...].astype(F32).T.astype(BF16)
        dk_ref[...] = jnp.zeros_like(dk_ref)
        dv_ref[...] = jnp.zeros_like(dv_ref)
        dgain_ref[...] = jnp.zeros_like(dgain_ref)

    fetch_pieces(step, pieces, plan, buffers, sems, rows)
    grad = here_rows(buffers, step, rows)
    all_ref[...] = grad
    dmix_all = jnp.zeros((2 * rows, q_width), F32)
    for number, w_ref in enumerate(w_refs):
        dmix_all += jnp.dot(
            grad[:, number * size : (number + 1) * size],
            w_ref[...],
            preferred_element_type=F32,
        )
    dmix_all = dmix_all.astype(BF16)
    allowed = col_ref[...] <= row_ref[...]
    for number in range(q_width // head):
        kv = number // group * head
        column = number * head
        q = q_ref[:, column : column + head]
        dmix = dmix_all[:, column : column + head]
        mix = mix_ref[:, column : column + head]
        delta = jnp.sum((dmix.astype(F32) * mix.astype(F32)).T, axis=0, keepdims=True)
        scores = nt(k_ref[:, kv : kv + head], q) * scale
        probs = jnp.exp(jnp.where(allowed, scores - lse_ref[number : number + 1, :], MASKED))
        dv_ref[:, kv : kv + head] += jnp.dot(
            probs.astype(BF16), dmix, preferred_element_type=F32
        )
        prob_grad = nt(v_ref[:, kv : kv + head], dmix)
        score_grad = (probs * (prob_grad - delta) * scale).astype(BF16)
        dk_ref[:, kv : kv + head] += jnp.dot(score_grad, q, preferred_element_type=F32)
        dq = jnp.dot(kt_ref[kv : kv + head, :], score_grad, preferred_element_type=F32).T
        raw_grad, gain_part = head_back(
            dq, raw_ref[:, column : column + head], qgain_ref[...], cos_ref[...], sin_ref[...]
        )
        low_ref[:, column : column + head] = raw_grad.astype(BF16)
        dgain_ref[...] += jnp.sum(gain_part, axis=0, keepdims=True)


def attend_back(pieces, weights, q, k, v, pos_row, pos_col, mix, lse, raw, q_gain, cosine, sine_part):
    total, q_width = q.shape
    kv_width = k.shape[1]
    width = weights[0].shape[0] * len(weights)
    steps = lax.axis_size("ctx") // 2
    rows = total // (2 * steps)
    heads = lse.shape[0]
    last_columns = pl.BlockSpec(
        (weights[0].shape[0], q_width), lambda step: (0, weights[0].shape[1] // q_width - 1)
    )
    head = q_gain.shape[1]

    def wide(columns):
        return pl.BlockSpec((2 * rows, columns), lambda step: (step, 0))

    def fixed(shape):
        return pl.BlockSpec(shape, lambda step: (0, 0))

    return pl.pallas_call(
        functools.partial(attend_back_kernel, piece_plan(pieces), len(weights)),
        out_shape=[
            jax.ShapeDtypeStruct((total, q_width), BF16),
            jax.ShapeDtypeStruct((total, kv_width), F32),
            jax.ShapeDtypeStruct((total, kv_width), F32),
            jax.ShapeDtypeStruct((1, head), F32),
            jax.ShapeDtypeStruct((total, width), BF16),
        ],
        grid=(steps,),
        in_specs=in_place(pieces)
        + [last_columns] * len(weights)
        + [
            wide(q_width), whole(k), whole(v),
            pl.BlockSpec((1, 2 * rows), lambda step: (0, step)),
            whole(pos_col), wide(q_width),
            pl.BlockSpec((heads, 2 * rows), lambda step: (0, step)),
            wide(q_width), whole(q_gain), wide(head), wide(head),
        ],
        out_specs=[
            wide(q_width), fixed((total, kv_width)), fixed((total, kv_width)), fixed((1, head)),
            wide(width),
        ],
        scratch_shapes=piece_scratch(pieces, total // 2, width)
        + [pltpu.VMEM((kv_width, total), BF16)],
        cost_estimate=pl.CostEstimate(
            flops=10 * total * total * q_width,
            bytes_accessed=8 * total * width,
            transcendentals=total * total * heads,
        ),
        name="attend_back",
    )(
        *piece_arrays(pieces), *weights,
        q, k, v, pos_row, pos_col, mix, lse, raw, q_gain, cosine, sine_part,
    )


def project_back_kernel(
    chunks, low_ref, dk_ref, dv_ref, raw_ref, kgain_ref, cos_ref, sin_ref, x_ref, blk_ref, *refs
):
    w_refs, refs = refs[:chunks], refs[chunks:]
    right_ref, even_ref, odd_ref, again_ref, dgain_ref = refs
    head = kgain_ref.shape[1]
    kv_width = dk_ref.shape[1]
    q_width = low_ref.shape[1]
    rows = even_ref.shape[0]
    width = x_ref.shape[1]
    size = width // chunks

    @pl.when(pl.program_id(0) == 0)
    def _():
        again_ref[...] = jnp.zeros_like(again_ref)
        dgain_ref[...] = jnp.zeros_like(dgain_ref)

    right_ref[:, :q_width] = low_ref[...]
    for column in range(0, kv_width, head):
        raw_grad, gain_part = head_back(
            dk_ref[:, column : column + head],
            raw_ref[:, q_width + column : q_width + column + head],
            kgain_ref[...],
            cos_ref[...],
            sin_ref[...],
        )
        right_ref[:, q_width + column : q_width + column + head] = raw_grad.astype(BF16)
        dgain_ref[...] += jnp.sum(gain_part, axis=0, keepdims=True)
    right_ref[:, q_width + kv_width :] = dv_ref[...].astype(BF16)
    right = right_ref[...]
    x = x_ref[...].astype(F32)
    normed = x * head_scale(x)
    for number, w_ref in enumerate(w_refs):
        side = slice(number * size, (number + 1) * size)
        part = nt(right, w_ref[...])
        again_ref[:, side] += jnp.sum(part * normed[:, side], axis=0, keepdims=True)
        part = part.astype(BF16)
        even_ref[:, side] = part[:rows]
        odd_ref[:, side] = part[rows:]
    even_ref[:, width:] = blk_ref[:rows, :]
    odd_ref[:, width:] = blk_ref[rows:, :]


def project_back(low, dk, dv, raw, k_gain, cosine, sine_part, both_all, weights, block_part):
    total, q_width = low.shape
    kv_width = dk.shape[1]
    width = both_all.shape[1] // 2
    steps = lax.axis_size("ctx") // 2
    rows = total // (2 * steps)
    head = k_gain.shape[1]

    def wide(columns):
        return pl.BlockSpec((2 * rows, columns), lambda step: (step, 0))

    def fixed(shape):
        return pl.BlockSpec(shape, lambda step: (0, 0))

    first_columns = pl.BlockSpec(
        (weights[0].shape[0], q_width + 2 * kv_width), lambda step: (0, 0)
    )
    both = pl.BlockSpec((rows, 2 * width), lambda step: (step, 0))
    return pl.pallas_call(
        functools.partial(project_back_kernel, len(weights)),
        out_shape=[
            jax.ShapeDtypeStruct((total, q_width + 2 * kv_width), BF16),
            jax.ShapeDtypeStruct((total // 2, 2 * width), BF16),
            jax.ShapeDtypeStruct((total // 2, 2 * width), BF16),
            jax.ShapeDtypeStruct((1, width), F32),
            jax.ShapeDtypeStruct((1, head), F32),
        ],
        grid=(steps,),
        in_specs=[
            wide(q_width), wide(kv_width), wide(kv_width), wide(q_width + kv_width),
            whole(k_gain), wide(head), wide(head), wide(width), wide(width),
        ]
        + [first_columns] * len(weights),
        out_specs=[
            wide(q_width + 2 * kv_width), both, both, fixed((1, width)), fixed((1, head)),
        ],
        cost_estimate=pl.CostEstimate(
            flops=2 * total * width * (q_width + 2 * kv_width),
            bytes_accessed=12 * total * width,
            transcendentals=total,
        ),
        name="project_back",
    )(low, dk, dv, raw, k_gain, cosine, sine_part, both_all, block_part, *weights)


def on_device_all(
    hidden_in,
    pair_table,
    attn_gain,
    query_proj,
    key_proj,
    value_proj,
    query_gain,
    key_gain,
    output_proj,
    mlp_gain,
    gate_proj,
    up_proj,
    down_proj,
    cotangent,
):
    fsdp_count = lax.axis_size("fsdp")
    fsdp_index = lax.axis_index("fsdp")
    ctx_count = lax.axis_size("ctx")
    ctx_index = lax.axis_index("ctx")
    row_count, width = hidden_in.shape[1:]
    block_len = row_count // 2
    total_rows = ctx_count * row_count
    shard_rows = width // fsdp_count
    head_width = query_gain.shape[0]
    half_head = head_width // 2
    kvhead_total = key_proj.shape[1] // head_width
    kv_count = max(1, kvhead_total // ctx_count)
    kv_share = max(1, ctx_count // kvhead_total)
    query_width = query_proj.shape[1] // ctx_count
    kv_width = kv_count * head_width
    kv_own = key_proj.shape[1] // ctx_count
    hidden_width = gate_proj.shape[1] // ctx_count

    fsdp_order = fsdp_index ^ jnp.arange(fsdp_count, dtype=jnp.int32)

    def block_order(values):
        return jnp.concatenate(
            [
                lax.dynamic_slice_in_dim(
                    values, (fsdp_index ^ number) * shard_rows, shard_rows, axis=values.ndim - 1
                )
                for number in range(fsdp_count)
            ],
            axis=-1,
        )

    def columns(weights, start, size):
        return lax.dynamic_slice_in_dim(weights, start, size, axis=1)

    kv_index = ctx_index // kv_share
    both_own = own_blocks(hidden_in[0], cotangent[0], fsdp_order)
    inputs = both_own[:, :width]
    cot_low = both_own[:, width:]
    gains_rel = block_order(jnp.stack([attn_gain, mlp_gain]))
    attn_gain_rel = gains_rel[0]
    mlp_gain_rel = gains_rel[1]
    fsdp_levels = (fsdp_count - 1).bit_length()
    attn_width = query_width + 2 * kv_width

    both_pieces = gather_ctx(both_own)
    first_shard = pick_columns(
        [
            (query_proj, ctx_index, query_width),
            (key_proj, kv_index, kv_width),
            (value_proj, kv_index, kv_width),
            (output_proj, ctx_index, query_width),
        ]
    )
    first_blocks = {0: first_shard}
    for level in range(1, fsdp_levels + 1):
        first_blocks = gather_fsdp_step(first_blocks, fsdp_count, level)
    first_parts = [first_blocks[number] for number in range(fsdp_count)]
    mlp_shard = pick_columns(
        [(weights, ctx_index, hidden_width) for weights in (gate_proj, up_proj, down_proj)]
    )
    mlp_blocks = gather_fsdp_step({0: mlp_shard}, fsdp_count, 1)

    owner_ids = ctx_index ^ jnp.arange(ctx_count, dtype=jnp.int32)
    picked = owner_ids[:, None] == jnp.arange(ctx_count, dtype=jnp.int32)[None, :]
    block_ids = jnp.sum(jnp.where(picked[:, :, None], pair_table[None], 0), axis=1)
    positions = (
        block_ids[:, :, None] * block_len + jnp.arange(block_len, dtype=jnp.int32)
    ).reshape(total_rows)
    pos_row = positions.reshape(1, total_rows)
    pos_col = positions.reshape(total_rows, 1)
    lanes = jnp.arange(head_width, dtype=jnp.int32)
    frequency = ROPE_BASE ** (-((lanes % half_head).astype(F32) * 2.0 / head_width))
    angles = positions.astype(F32)[:, None] * frequency[None, :]
    cosine = jnp.cos(angles)
    sine_part = jnp.sin(angles) * jnp.where(lanes < half_head, -1.0, 1.0)[None, :]

    query_row = query_gain.reshape(1, head_width)
    key_row = key_gain.reshape(1, head_width)
    attn_in, attn_raw, query_heads, key_heads, value_heads, both_all = project(
        both_pieces, first_parts, attn_gain_rel.reshape(1, width), query_row, key_row,
        cosine, sine_part, query_width, kv_width,
    )
    attn_mix, log_total, mix_even, mix_odd = attend(
        query_heads, key_heads, value_heads, pos_row, pos_col, first_parts, head_width
    )

    resid_sum = scatter_ctx(mix_even, mix_odd)
    resid = inputs.astype(F32) + resid_sum
    mlp_in = rms_norm(resid, mlp_gain_rel).astype(BF16)
    for level in range(2, fsdp_levels + 1):
        mlp_blocks = gather_fsdp_step(mlp_blocks, fsdp_count, level)
    mlp_parts = [mlp_blocks[number] for number in range(fsdp_count)]
    mlp_pieces = gather_ctx(mlp_in)
    mlp_right, hidden_act, part_even, part_odd, mlp_all = mlp_both(
        mlp_pieces, both_all, mlp_parts, ctx_count
    )
    mlp_in_grad = scatter_ctx(part_even, part_odd)
    mlp_sums = dict(enumerate(weight_grads(mlp_all, mlp_right, both_all, hidden_act, fsdp_count)))
    down_w = jnp.concatenate([part[:, 2 * hidden_width :] for part in mlp_parts], axis=0)
    block_part = times_transposed(hidden_act, down_w).astype(BF16)
    resid_part, mlp_gain_grad = jax.vjp(rms_norm, resid, mlp_gain_rel)[1](mlp_in_grad)
    resid_grad = cot_low.astype(F32) + resid_part
    resid_low = resid_grad.astype(BF16)
    for level in range(fsdp_levels, 1, -1):
        mlp_sums = scatter_fsdp_step(mlp_sums, fsdp_count, level)
    resid_pieces = gather_ctx(resid_low)
    mlp_moved = {
        number: exchange(mlp_sums[number].astype(BF16), number, "fsdp")
        for number in range(1, fsdp_count)
        if level_of(number) == 1
    }
    query_low, key_grad, value_grad, query_gain_grad, resid_all = attend_back(
        resid_pieces, first_parts, query_heads, key_heads, value_heads, pos_row, pos_col,
        attn_mix, log_total, attn_raw, query_row, cosine, sine_part,
    )
    bit = 1
    while bit < kv_share:
        moved = exchange(jnp.concatenate([key_grad, value_grad], axis=1), bit, "ctx")
        moved = moved.reshape(ctx_count, row_count, 2 * kv_width)
        moved = jnp.concatenate([moved[number ^ bit] for number in range(ctx_count)], axis=0)
        key_grad = key_grad + moved[:, :kv_width]
        value_grad = value_grad + moved[:, kv_width:]
        bit *= 2
    own_parts = first_parts
    own_start = (ctx_index % kv_share) * kv_own
    if kv_share > 1:
        place = jnp.arange(attn_width) - query_width
        owned = (place < 0) | (
            (place % kv_width >= own_start) & (place % kv_width < own_start + kv_own)
        )
        own_parts = [
            jnp.where(owned[None, :], part[:, :attn_width], 0).astype(BF16)
            for part in first_parts
        ]
    attn_right, tail_even, tail_odd, attn_gain_grad, key_gain_grad = project_back(
        query_low, key_grad, value_grad, attn_raw, key_row, cosine, sine_part,
        both_all, own_parts, block_part,
    )
    attn_gain_grad = attn_gain_grad[0]
    query_gain_grad = query_gain_grad[0]
    key_gain_grad = key_gain_grad[0]
    if kv_share > 1:
        attn_right = jnp.concatenate(
            [
                attn_right[:, :query_width],
                columns(attn_right, query_width + own_start, kv_own),
                columns(attn_right, query_width + kv_width + own_start, kv_own),
            ],
            axis=1,
        )
        key_gain_grad = jnp.where(ctx_index % kv_share == 0, key_gain_grad, 0.0)
    attn_sums = dict(enumerate(weight_grads(attn_in, attn_right, resid_all, attn_mix)))
    for level in range(fsdp_levels, 0, -1):
        attn_sums = scatter_fsdp_step(attn_sums, fsdp_count, level)
    attn_grads = attn_sums[0].astype(BF16)
    both_sums = scatter_ctx(tail_even, tail_odd)
    attn_in_grad = both_sums[:, :width]
    block_out = (resid + both_sums[:, width:]).astype(BF16)
    mlp_total = mlp_sums[0].astype(F32)
    for moved in mlp_moved.values():
        mlp_total = mlp_total + moved.astype(F32)
    mlp_grads = mlp_total.astype(BF16)
    own_wide = inputs.astype(F32)
    input_part = jax.vjp(lambda values: rms_norm(values, attn_gain_rel), own_wide)[1](
        attn_in_grad
    )[0]
    input_grad = resid_grad + input_part
    gains = sum_all(
        jnp.concatenate(
            [
                block_order(attn_gain_grad),
                block_order(mlp_gain_grad),
                query_gain_grad,
                key_gain_grad,
            ]
        )
    )

    outs = (
        block_order(block_out)[None],
        block_order(input_grad)[None],
        gains[:width],
        gains[2 * width : 2 * width + head_width],
        gains[2 * width + head_width :],
        gains[width : 2 * width],
    )
    mlp_pieces = gather_ctx(mlp_grads)
    mlp_outs = place_columns(mlp_pieces, (hidden_width,) * 3, ctx_index)
    attn_pieces = gather_ctx(attn_grads)
    last_piece, *outs = tie(attn_pieces[-1][2], *outs)
    attn_pieces[-1] = attn_pieces[-1][:2] + (last_piece,)
    attn_outs = place_columns(attn_pieces, (query_width, kv_own, kv_own, query_width), ctx_index)
    return (
        outs[0],
        outs[1],
        outs[2],
        attn_outs[0],
        attn_outs[1],
        attn_outs[2],
        outs[3],
        outs[4],
        attn_outs[3],
        outs[5],
        mlp_outs[0],
        mlp_outs[1],
        mlp_outs[2],
    )


def solution(mesh):
    in_specs = (
        P("fsdp", "ctx", None),
        P(),
        P(),
        P("fsdp", None),
        P("fsdp", None),
        P("fsdp", None),
        P(),
        P(),
        P("fsdp", None),
        P(),
        P("fsdp", None),
        P("fsdp", None),
        P("fsdp", None),
        P("fsdp", "ctx", None),
    )
    out_specs = (
        P("fsdp", "ctx", None),
        P("fsdp", "ctx", None),
        P(),
        P("fsdp", None),
        P("fsdp", None),
        P("fsdp", None),
        P(),
        P(),
        P("fsdp", None),
        P(),
        P("fsdp", None),
        P("fsdp", None),
        P("fsdp", None),
    )
    return jax.shard_map(
        on_device_all, mesh=mesh, in_specs=in_specs, out_specs=out_specs, check_vma=False
    )
```

time: 390 us -> 314 us (0.81)
  waiting for transfers between devices: 199 us -> 117 us
  Pallas kernels: 67.8 us -> 93.2 us
  other arithmetic: 28.2 us -> 18.8 us
  matrix products: 11.3 us -> 2.61 us
  starting transfers between devices: 60.9 us -> 54.3 us
  local copies, waits for them, and re-layouts: 20.2 us -> 24.8 us
    ppermute x57 -> x77, waiting for transfers between devices: 199 us -> 117 us  [exchange(): lax.ppermute(value, axis, [(index, index ^ bit) for index in range(count)])]
    pallas_call x6 -> x14, Pallas kernels: 49.7 us -> 77.1 us  [the longest x2 13.4 us: weight_grads(): pl.pallas_call(grads_kernel, out_shape=[jax.ShapeDtypeStruct((size, colum...]
    another operation x8 -> x1, other arithmetic: 7.42 us -> 0.09 us  [on_device_all(): gains_rel = block_order(jnp.stack([attn_gain, mlp_gain]))]
    dot_general x4 -> x0, matrix products: 7.23 us -> none  [transposed_times(): lax.dot_general(lhs_mat, rhs_mat, (((0,), (0,)), ((), ())), preferred_ele...]
    ppermute x57 -> x77, starting transfers between devices: 60.9 us -> 54.3 us  [exchange(): lax.ppermute(value, axis, [(index, index ^ bit) for index in range(count)])]
    concatenate x10 -> x1, other arithmetic: 5.77 us -> 0.01 us  [block_order(): jnp.concatenate([lax.dynamic_slice_in_dim(values, (fsdp_index ^ number) *...]
    slice x14 -> x16, local copies, waits for them, and re-layouts: 3.56 us -> 8.62 us  [the longest x10 6.65 us: rows_of(): return parts[0][start:stop]]
    convert_element_type x1 -> x4, other arithmetic: 0.06 us -> 4.54 us  [the longest x1 2.1 us: on_device_all(): mlp_grads = mlp_total.astype(BF16)]
  transfers between devices with their start and end apart: 57 -> 77, of which waited for: 32 -> 25; matrix products, arithmetic and copies ran while one was open for 12% -> 12% of each run, Pallas kernels for 10% -> 18%
where the time goes in v1:
time: 314 us; the launch traced here: 312 us
  waiting for transfers between devices  117 us (37%)
  Pallas kernels  93.2 us (30%)
  starting transfers between devices  54.3 us (17%)
  local copies, waits for them, and re-layouts  24.8 us (8%)
  other arithmetic  18.8 us (6%)
    ppermute x77, waiting for transfers between devices, exchange(): lax.ppermute(value, axis, [(index, index ^ bit) for index in range(count)])  117 us
    ppermute x77, starting transfers between devices, exchange(): lax.ppermute(value, axis, [(index, index ^ bit) for index in range(count)])  54.3 us
    pallas_call x2, Pallas kernels, weight_grads(): pl.pallas_call(grads_kernel, out_shape=[jax.ShapeDtypeStruct((size, colum...  13.4 us
    pallas_call x1, Pallas kernels, attend_back(): pl.pallas_call(functools.partial(attend_back_kernel, piece_plan(pieces),...  12 us
    pallas_call x1, Pallas kernels, attend(): pl.pallas_call(functools.partial(attend_kernel, len(weights)), out_shape=...  11.2 us
    pallas_call x2, Pallas kernels, place_columns(): pl.pallas_call(kernel, out_shape=[jax.ShapeDtypeStruct((rows, count * wid...  10.8 us
    unnamed x137, local copies, waits for them, and re-layouts  9.88 us
    pallas_call x1, Pallas kernels, mlp_both(): pl.pallas_call(functools.partial(mlp_kernel, piece_plan(pieces), len(weig...  9.68 us
  transfers between devices with their start and end apart: 77, of which 25 were waited for; matrix products, arithmetic and copies ran while one was open for 12% of the time, Pallas kernels for 18%

profile of v1, /device:TPU:0, one launch (start us, length us, event | category | flops | bytes accessed | tf_op | source)
XLA Modules:
  0.0 312.4 jit_solution(6672285822431723668)
XLA Ops:
  22.3 10.3 %collective-permute-done.10.refs_12_.refs_2_ = bf16[256,768]{1,0:T(8,128)(2,1)S(1)} collective-permute-done((bf16[256,768]{1,0:T(8,128)(2,1)}, bf16[256,768]{1,0:T(8,128)(2,1)S(1)}, u32[]{:S(2)}, u32[]{:S(2)}) %collective-permute-start.10) | collective-permute-done | bytes 393248 | tf_op jit(solution)/shard_map/ppermute | solution.py:43
  37.9 3.7 %fusion.7 = (f32[1024,128]{1,0:T(8,128)}, f32[1024,128]{1,0:T(8,128)}) fusion(f32[128]{0:T(128)S(1)} %get-tuple-element.169, f32[128]{0:T(128)} %get-tuple-element.170, f32[1024]{0:T(1024)S(1)} %convert_element_type.115), kind=kLoop, calls=%fused_computation.21 | loop fusion | flops 262144 | bytes 1053696 | tf_op jit(solution)/shard_map/mul | solution.py:966
  42.6 8.2 %project.1 = (bf16[1024,1024]{1,0:T(8,128)(2,1)}, f32[1024,384]{1,0:T(8,128)}, bf16[1024,256]{1,0:T(8,128)(2,1)}, bf16[1024,128]{1,0:T(8,128)(2,1)}, bf16[1024,1...) custom-call(bf16[128,2048]{1,0:T(8,128)(2,1)} %own_blocks.1.refs_0_, bf16[128,2048]{1,0:T(8,128)(2,1)} %copy-done.20, ...), custom_call_target="tpu_custom_call" | custom-call | flops 1073741824 | bytes 12582912 | tf_op jit(solution)/shard_map/project/pallas_call | solution.py:564
  50.7 11.2 %attend.1 = (bf16[1024,256]{1,0:T(8,128)(2,1)}, f32[2,1024]{1,0:T(2,128)}, bf16[512,1024]{1,0:T(8,128)(2,1)}, bf16[512,1024]{1,0:T(8,128)(2,1)}) custom-call(bf16[1024,256]{1,0:T(8,128)(2,1)} %get-tuple-element.73.q_ref.refs_14_, bf16[1024,128]{1,0:T(8,128)(2,1)} %get-tuple-element.74.k_ref.refs_15_, bf16[1024,128]{1,0:T(8,128)(2,1)} %get-tuple-element.75.v_ref.refs_16_, ...), custom_call_target="tpu_custom_call" | custom-call | flops 1073741824 | bytes 8388608 | tf_op jit(solution)/shard_map/attend/pallas_call | solution.py:647
  71.8 4.6 %collective-permute-done.13.first = bf16[64,1024]{1,0:T(8,128)(2,1)S(1)} collective-permute-done((bf16[64,1024]{1,0:T(8,128)(2,1)}, bf16[64,1024]{1,0:T(8,128)(2,1)S(1)}, u32[]{:S(2)}, u32[]{:S(2)}) %collective-permute-start.13) | collective-permute-done | bytes 131104 | tf_op jit(solution)/shard_map/ppermute | solution.py:43
  81.6 13.3 %collective-permute-done.27.refs_13_ = bf16[256,1152]{1,0:T(8,128)(2,1)} collective-permute-done((bf16[256,1152]{1,0:T(8,128)(2,1)}, bf16[256,1152]{1,0:T(8,128)(2,1)}, u32[]{:S(2)}, u32[]{:S(2)}) %collective-permute-start.27) | collective-permute-done | bytes 589856 | tf_op jit(solution)/shard_map/ppermute | solution.py:43
  97.5 6.6 %collective-permute-done.18.refs_2_ = bf16[128,1024]{1,0:T(8,128)(2,1)S(1)} collective-permute-done((bf16[128,1024]{1,0:T(8,128)(2,1)S(1)}, bf16[128,1024]{1,0:T(8,128)(2,1)S(1)}, u32[]{:S(2)}, u32[]{:S(2)}) %collective-permute-start.18) | collective-permute-done | bytes 262176 | tf_op jit(solution)/shard_map/ppermute | solution.py:43
  107.4 11.9 %collective-permute-done.28.refs_14_ = bf16[256,1152]{1,0:T(8,128)(2,1)S(1)} collective-permute-done((bf16[256,1152]{1,0:T(8,128)(2,1)}, bf16[256,1152]{1,0:T(8,128)(2,1)S(1)}, u32[]{:S(2)}, u32[]{:S(2)}) %collective-permute-start.28) | collective-permute-done | bytes 589856 | tf_op jit(solution)/shard_map/ppermute | solution.py:43
  120.5 3.8 %collective-permute-done.24.refs_8_ = bf16[64,1024]{1,0:T(8,128)(2,1)S(1)} collective-permute-done((bf16[64,1024]{1,0:T(8,128)(2,1)S(1)}, bf16[64,1024]{1,0:T(8,128)(2,1)S(1)}, u32[]{:S(2)}, u32[]{:S(2)}) %collective-permute-start.24) | collective-permute-done | bytes 131104 | tf_op jit(solution)/shard_map/ppermute | solution.py:43
  126.4 9.7 %mlp_both.1 = (bf16[1024,768]{1,0:T(8,128)(2,1)}, bf16[1024,384]{1,0:T(8,128)(2,1)}, bf16[512,1024]{1,0:T(8,128)(2,1)}, bf16[512,1024]{1,0:T(8,128)(2,1)}, bf16[1024,1024]{1,0:T(8,128)(2,1)}) custom-call(bf16[128,1024]{1,0:T(8,128)(2,1)} %copy-done.30, bf16[128,1024]{1,0:T(8,128)(2,1)} %copy-done.48, bf16[128,1024]{1,0:T(8,128)(2,1)} %copy-done.39, ...), custom_call_target="tpu_custom_call" | custom-call | flops 4026531840 | bytes 12582912 | tf_op jit(solution)/shard_map/mlp_both/pallas_call | solution.py:434
  136.3 7.3 %weight_grads.3 = (bf16[256,1152]{1,0:T(8,128)(2,1)}, bf16[256,1152]{1,0:T(8,128)(2,1)}, bf16[256,1152]{1,0:T(8,128)(2,1)}, bf16[256,1152]{1,0:T(8,128)(2,1)}) custom-call(bf16[1024,1024]{1,0:T(8,128)(2,1)} %get-tuple-element.122.left_one, bf16[1024,768]{1,0:T(8,128)(2,1)} %get-tuple-element.123.right_one, ...), custom_call_target="tpu_custom_call" | custom-call | flops 2415919104 | bytes 8912896 | tf_op jit(solution)/shard_map/weight_grads/pallas_call | solution.py:474
  180.6 8.6 %collective-permute-done.67 = bf16[256,1152]{1,0:T(8,128)(2,1)S(1)} collective-permute-done((bf16[256,1152]{1,0:T(8,128)(2,1)S(1)}, bf16[256,1152]{1,0:T(8,128)(2,1)S(1)}, u32[]{:S(2)}, u32[]{:S(2)}) %collective-permute-start.67) | collective-permute-done | bytes 589856 | tf_op jit(solution)/shard_map/ppermute | solution.py:43
  194.3 12.0 %attend_back.1 = (bf16[1024,256]{1,0:T(8,128)(2,1)}, f32[1024,128]{1,0:T(8,128)}, f32[1024,128]{1,0:T(8,128)}, f32[1,128]{1,0:T(1,128)}, bf16[1024,1024]{1,0:T(8,128)(2,1)}) custom-call(bf16[128,1024]{1,0:T(8,128)(2,1)} %copy-done.26, bf16[128,1024]{1,0:T(8,128)(2,1)} %copy-done.47, bf16[128,1024]{1,0:T(8,128)(2,1)} %collective-permute-done.35.refs_2_, ...), custom_call_target="tpu_custom_call" | custom-call | flops 2684354560 | bytes 8388608 | tf_op jit(solution)/shard_map/attend_back/pallas_call | solution.py:751
  206.3 7.9 %project_back.1 = (bf16[1024,512]{1,0:T(8,128)(2,1)}, bf16[512,2048]{1,0:T(8,128)(2,1)}, bf16[512,2048]{1,0:T(8,128)(2,1)}, f32[1,1024]{1,0:T(1,128)}, f32[1,128]{1,0:T(1,128)}) custom-call(bf16[1024,256]{1,0:T(8,128)(2,1)} %get-tuple-element.92.low_ref, f32[1024,128]{1,0:T(8,128)} %get-tuple-element.93.dk_ref, f32[1024,128]{1,0:T(8,128)} %get-tuple-element.94.dv_ref, ...), custom_call_target="tpu_custom_call" | custom-call | flops 1073741824 | bytes 12582912 | tf_op jit(solution)/shard_map/project_back/pallas_call | solution.py:849
  214.2 6.1 %weight_grads.2 = (bf16[256,768]{1,0:T(8,128)(2,1)}, bf16[256,768]{1,0:T(8,128)(2,1)}, bf16[256,768]{1,0:T(8,128)(2,1)}, bf16[256,768]{1,0:T(8,128)(2,1)}) custom-call(bf16[1024,1024]{1,0:T(8,128)(2,1)} %get-tuple-element.72.left_one, bf16[1024,512]{1,0:T(8,128)(2,1)} %get-tuple-element.96.right_one, bf16[1024,1024]{1,0:T(8,128)(2,1)} %get-tuple-element.97.left_two, ...), custom_call_target="tpu_custom_call" | custom-call | flops 1610612736 | bytes 7340032 | tf_op jit(solution)/shard_map/weight_grads/pallas_call | solution.py:474
  221.3 3.4 %collective-permute-done.54 = f32[2304]{0:T(1024)S(1)} collective-permute-done((f32[2304]{0:T(1024)S(1)}, f32[2304]{0:T(1024)S(1)}, u32[]{:S(2)}, u32[]{:S(2)}) %collective-permute-start.54) | collective-permute-done | bytes 9248 | tf_op jit(solution)/shard_map/ppermute | solution.py:43
  225.2 3.2 %collective-permute-done.55 = f32[2304]{0:T(1024)S(1)} collective-permute-done((f32[2304]{0:T(1024)S(1)}, f32[2304]{0:T(1024)S(1)}, u32[]{:S(2)}, u32[]{:S(2)}) %collective-permute-start.55) | collective-permute-done | bytes 9248 | tf_op jit(solution)/shard_map/ppermute | solution.py:43
  228.9 3.2 %collective-permute-done.56 = f32[2304]{0:T(1024)S(1)} collective-permute-done((f32[2304]{0:T(1024)S(1)}, f32[2304]{0:T(1024)S(1)}, u32[]{:S(2)}, u32[]{:S(2)}) %collective-permute-start.56) | collective-permute-done | bytes 9248 | tf_op jit(solution)/shard_map/ppermute | solution.py:43
  236.6 5.9 %collective-permute-done.57 = f32[2304]{0:T(1024)S(1)} collective-permute-done((f32[2304]{0:T(1024)S(1)}, f32[2304]{0:T(1024)S(1)}, u32[]{:S(2)}, u32[]{:S(2)}) %collective-permute-start.57) | collective-permute-done | bytes 9248 | tf_op jit(solution)/shard_map/ppermute | solution.py:43
  251.9 9.1 %collective-permute-done.45 = bf16[256,768]{1,0:T(8,128)(2,1)} collective-permute-done((bf16[256,768]{1,0:T(8,128)(2,1)}, bf16[256,768]{1,0:T(8,128)(2,1)}, u32[]{:S(2)}, u32[]{:S(2)}) %collective-permute-start.45) | collective-permute-done | bytes 393248 | tf_op jit(solution)/shard_map/ppermute | solution.py:43
  274.0 9.3 %collective-permute-done.75.refs_8_ = bf16[128,1152]{1,0:T(8,128)(2,1)} collective-permute-done((bf16[128,1152]{1,0:T(8,128)(2,1)}, bf16[128,1152]{1,0:T(8,128)(2,1)}, u32[]{:S(2)}, u32[]{:S(2)}) %collective-permute-start.75) | collective-permute-done | bytes 294944 | tf_op jit(solution)/shard_map/ppermute | solution.py:43
  291.1 5.9 %place_columns.3 = (f32[256,3072]{1,0:T(8,128)}, f32[256,3072]{1,0:T(8,128)}, f32[256,3072]{1,0:T(8,128)}) custom-call(s32[5]{0:T(128)} %stack.56.index_ref, bf16[256,1152]{1,0:T(8,128)(2,1)} %add_convert_fusion.refs_0_, bf16[256,1152]{1,0:T(8,128)(2,1)} %collective-permute-done.68.refs_1_, bf16[256,1152]{1,0:T(8,128)(2,1)} %collective-permute-done.69.refs_2_, ...), custom_call_target="tpu_custom_call" | custom-call | bytes 14155776 | tf_op jit(solution)/shard_map/place_columns/pallas_call | solution.py:340
  297.1 3.8 %collective-permute-done.47.refs_8_ = bf16[128,768]{1,0:T(8,128)(2,1)} collective-permute-done((bf16[128,768]{1,0:T(8,128)(2,1)}, bf16[128,768]{1,0:T(8,128)(2,1)}, u32[]{:S(2)}, u32[]{:S(2)}) %collective-permute-start.47) | collective-permute-done | bytes 196640 | tf_op jit(solution)/shard_map/ppermute | solution.py:43
  307.4 4.9 %place_columns.2 = (f32[256,2048]{1,0:T(8,128)}, f32[256,1024]{1,0:T(8,128)}, f32[256,1024]{1,0:T(8,128)}, f32[256,2048]{1,0:T(8,128)}) custom-call(s32[5]{0:T(128)} %stack.56.index_ref, bf16[256,768]{1,0:T(8,128)(2,1)} %copy-done.10, bf16[256,768]{1,0:T(8,128)(2,1)} %copy-done.23, bf16[256,768]{1,0:T(8,128)(2,1)} %copy-done.15, ...), custom_call_target="tpu_custom_call" | custom-call | bytes 9437184 | tf_op jit(solution)/shard_map/place_columns/pallas_call | solution.py:340
  (348 shorter events, 136.7 us)
Async XLA Ops:
  3.1 29.9 %collective-permute-start = (bf16[128,2048]{1,0:T(8,128)(2,1)}, bf16[128,2048]{1,0:T(8,128)(2,1)S(1)}, u32[]{:S(2)}, u32[]{:S(2)}) collective-permute-start(bf16[128,2048]{1,0:T(8,128)(2,1)} %own_blocks.1.refs_0_), channel_id=1, source_target_pairs={{0,1},{1,0},{2,3},{3,2},{4,5},{5,4},{6,7},{7,6},{8,9},{9,8},{10,11... | collective-permute-start | bytes 1572872 | tf_op jit(solution)/shard_map/ppermute | solution.py:43
  10.7 22.3 %collective-permute-start.9 = (bf16[256,768]{1,0:T(8,128)(2,1)}, bf16[256,768]{1,0:T(8,128)(2,1)S(1)}, u32[]{:S(2)}, u32[]{:S(2)}) collective-permute-start(bf16[256,768]{1,0:T(8,128)(2,1)} %pick_columns.2.refs_10_.refs_0_), channel_id=1, source_target_pairs={{0,8},{8,0},{16,24},{24,16},{1,9},{9,1},{17,25},{25,17},{2,10},{10... | collective-permute-start | bytes 1179656 | tf_op jit(solution)/shard_map/ppermute | solution.py:43
  12.3 20.3 %collective-permute-start.10 = (bf16[256,768]{1,0:T(8,128)(2,1)}, bf16[256,768]{1,0:T(8,128)(2,1)S(1)}, u32[]{:S(2)}, u32[]{:S(2)}) collective-permute-start(bf16[256,768]{1,0:T(8,128)(2,1)} %pick_columns.2.refs_10_.refs_0_), channel_id=1, source_target_pairs={{0,16},{8,24},{16,0},{24,8},{1,17},{9,25},{17,1},{25,9},{2,18},{10... | collective-permute-start | bytes 1179656 | tf_op jit(solution)/shard_map/ppermute | solution.py:43
  65.3 29.6 %collective-permute-start.27 = (bf16[256,1152]{1,0:T(8,128)(2,1)}, bf16[256,1152]{1,0:T(8,128)(2,1)}, u32[]{:S(2)}, u32[]{:S(2)}) collective-permute-start(bf16[256,1152]{1,0:T(8,128)(2,1)} %pick_columns.3.refs_11_), channel_id=1, source_target_pairs={{0,16},{8,24},{16,0},{24,8},{1,17},{9,25},{17,1},{25,9},{2,18},{10... | collective-permute-start | bytes 1769480 | tf_op jit(solution)/shard_map/ppermute | solution.py:43
  81.5 25.9 %collective-permute-start.26 = (bf16[256,1152]{1,0:T(8,128)(2,1)S(1)}, bf16[256,1152]{1,0:T(8,128)(2,1)S(1)}, u32[]{:S(2)}, u32[]{:S(2)}) collective-permute-start(bf16[256,1152]{1,0:T(8,128)(2,1)S(1)} %copy-done.13), channel_id=1, source_target_pairs={{0,8},{8,0},{16,24},{24,16},{1,9},{9,1},{17,25},{25,17},{2,10},{10... | collective-permute-start | bytes 1769480 | tf_op jit(solution)/shard_map/ppermute | solution.py:43
  94.9 24.5 %collective-permute-start.28 = (bf16[256,1152]{1,0:T(8,128)(2,1)}, bf16[256,1152]{1,0:T(8,128)(2,1)S(1)}, u32[]{:S(2)}, u32[]{:S(2)}) collective-permute-start(bf16[256,1152]{1,0:T(8,128)(2,1)} %collective-permute-done.27.refs_13_), channel_id=1, source_target_pairs={{0,8},{8,0},{16,24},{24,16},{1,9},{9,1},{17,25},{25,17},{2,10},{10... | collective-permute-start | bytes 1769480 | tf_op jit(solution)/shard_map/ppermute | solution.py:43
  97.5 26.9 %collective-permute-start.17 = (bf16[128,1024]{1,0:T(8,128)(2,1)S(1)}, bf16[128,1024]{1,0:T(8,128)(2,1)S(1)}, u32[]{:S(2)}, u32[]{:S(2)}) collective-permute-start(bf16[128,1024]{1,0:T(8,128)(2,1)S(1)} %multiply_convert_fusion.refs_0_), channel_id=1, source_target_pairs={{0,1},{1,0},{2,3},{3,2},{4,5},{5,4},{6,7},{7,6},{8,9},{9,8},{10,11... | collective-permute-start | bytes 786440 | tf_op jit(solution)/shard_map/ppermute | solution.py:43
  104.7 19.7 %collective-permute-start.19 = (bf16[128,1024]{1,0:T(8,128)(2,1)S(1)}, bf16[128,1024]{1,0:T(8,128)(2,1)S(1)}, u32[]{:S(2)}, u32[]{:S(2)}) collective-permute-start(bf16[128,1024]{1,0:T(8,128)(2,1)S(1)} %collective-permute-done.18.refs_2_), channel_id=1, source_target_pairs={{0,1},{1,0},{2,3},{3,2},{4,5},{5,4},{6,7},{7,6},{8,9},{9,8},{10,11... | collective-permute-start | bytes 786440 | tf_op jit(solution)/shard_map/ppermute | solution.py:43
  107.4 17.0 %collective-permute-start.21 = (bf16[128,1024]{1,0:T(8,128)(2,1)S(1)}, bf16[128,1024]{1,0:T(8,128)(2,1)S(1)}, u32[]{:S(2)}, u32[]{:S(2)}) collective-permute-start(bf16[128,1024]{1,0:T(8,128)(2,1)S(1)} %collective-permute-done.20.refs_4_), channel_id=1, source_target_pairs={{0,1},{1,0},{2,3},{3,2},{4,5},{5,4},{6,7},{7,6},{8,9},{9,8},{10,11... | collective-permute-start | bytes 786440 | tf_op jit(solution)/shard_map/ppermute | solution.py:43
  148.5 31.6 %collective-permute-start.65 = (bf16[256,1152]{1,0:T(8,128)(2,1)}, bf16[256,1152]{1,0:T(8,128)(2,1)}, u32[]{:S(2)}, u32[]{:S(2)}) collective-permute-start(bf16[256,1152]{1,0:T(8,128)(2,1)} %get-tuple-element.125), channel_id=1, source_target_pairs={{0,8},{8,0},{16,24},{24,16},{1,9},{9,1},{17,25},{25,17},{2,10},{10... | collective-permute-start | bytes 1769480 | tf_op jit(solution)/shard_map/ppermute | solution.py:43
  161.4 27.8 %collective-permute-start.67 = (bf16[256,1152]{1,0:T(8,128)(2,1)S(1)}, bf16[256,1152]{1,0:T(8,128)(2,1)S(1)}, u32[]{:S(2)}, u32[]{:S(2)}) collective-permute-start(bf16[256,1152]{1,0:T(8,128)(2,1)S(1)} %add_convert_fusion.1), channel_id=1, source_target_pairs={{0,16},{8,24},{16,0},{24,8},{1,17},{9,25},{17,1},{25,9},{2,18},{10... | collective-permute-start | bytes 1769480 | tf_op jit(solution)/shard_map/ppermute | solution.py:43
  191.9 40.8 %collective-permute-start.69 = (bf16[256,1152]{1,0:T(8,128)(2,1)}, bf16[256,1152]{1,0:T(8,128)(2,1)}, u32[]{:S(2)}, u32[]{:S(2)}) collective-permute-start(bf16[256,1152]{1,0:T(8,128)(2,1)} %add_convert_fusion.refs_0_), channel_id=1, source_target_pairs={{0,2},{1,3},{2,0},{3,1},{4,6},{5,7},{6,4},{7,5},{8,10},{9,11},{10,... | collective-permute-start | bytes 1769480 | tf_op jit(solution)/shard_map/ppermute | solution.py:43
  220.3 25.7 %collective-permute-start.49 = (bf16[512,2048]{1,0:T(8,128)(2,1)}, bf16[512,2048]{1,0:T(8,128)(2,1)S(1)}, u32[]{:S(2)}, u32[]{:S(2)}) collective-permute-start(bf16[512,2048]{1,0:T(8,128)(2,1)} %get-tuple-element.103), channel_id=1, source_target_pairs={{0,1},{1,0},{2,3},{3,2},{4,5},{5,4},{6,7},{7,6},{8,9},{9,8},{10,11... | collective-permute-start | bytes 6291464 | tf_op jit(solution)/shard_map/ppermute | solution.py:43
  228.9 20.5 %collective-permute-start.68 = (bf16[256,1152]{1,0:T(8,128)(2,1)}, bf16[256,1152]{1,0:T(8,128)(2,1)}, u32[]{:S(2)}, u32[]{:S(2)}) collective-permute-start(bf16[256,1152]{1,0:T(8,128)(2,1)} %add_convert_fusion.refs_0_), channel_id=1, source_target_pairs={{0,1},{1,0},{2,3},{3,2},{4,5},{5,4},{6,7},{7,6},{8,9},{9,8},{10,11... | collective-permute-start | bytes 1769480 | tf_op jit(solution)/shard_map/ppermute | solution.py:43
  232.1 17.3 %collective-permute-start.71 = (bf16[256,1152]{1,0:T(8,128)(2,1)}, bf16[256,1152]{1,0:T(8,128)(2,1)}, u32[]{:S(2)}, u32[]{:S(2)}) collective-permute-start(bf16[256,1152]{1,0:T(8,128)(2,1)} %add_convert_fusion.refs_0_), channel_id=1, source_target_pairs={{0,4},{1,5},{2,6},{3,7},{4,0},{5,1},{6,2},{7,3},{8,12},{9,13},{10,... | collective-permute-start | bytes 1769480 | tf_op jit(solution)/shard_map/ppermute | solution.py:43
  232.6 18.1 %collective-permute-start.43 = (bf16[256,768]{1,0:T(8,128)(2,1)}, bf16[256,768]{1,0:T(8,128)(2,1)}, u32[]{:S(2)}, u32[]{:S(2)}) collective-permute-start(bf16[256,768]{1,0:T(8,128)(2,1)} %get-tuple-element.99), channel_id=1, source_target_pairs={{0,8},{8,0},{16,24},{24,16},{1,9},{9,1},{17,25},{25,17},{2,10},{10... | collective-permute-start | bytes 1179656 | tf_op jit(solution)/shard_map/ppermute | solution.py:43
  242.4 18.6 %collective-permute-start.45 = (bf16[256,768]{1,0:T(8,128)(2,1)}, bf16[256,768]{1,0:T(8,128)(2,1)}, u32[]{:S(2)}, u32[]{:S(2)}) collective-permute-start(bf16[256,768]{1,0:T(8,128)(2,1)} %add_convert_fusion.3), channel_id=1, source_target_pairs={{0,16},{8,24},{16,0},{24,8},{1,17},{9,25},{17,1},{25,9},{2,18},{10... | collective-permute-start | bytes 1179656 | tf_op jit(solution)/shard_map/ppermute | solution.py:43
  246.0 18.4 %collective-permute-start.73 = (bf16[128,1152]{1,0:T(8,128)(2,1)}, bf16[128,1152]{1,0:T(8,128)(2,1)}, u32[]{:S(2)}, u32[]{:S(2)}) collective-permute-start(bf16[128,1152]{1,0:T(8,128)(2,1)} %slice.145), channel_id=1, source_target_pairs={{0,4},{1,5},{2,6},{3,7},{4,0},{5,1},{6,2},{7,3},{8,12},{9,13},{10,... | collective-permute-start | bytes 884744 | tf_op jit(solution)/shard_map/ppermute | solution.py:43
  249.5 35.1 %collective-permute-start.70 = (bf16[256,1152]{1,0:T(8,128)(2,1)}, bf16[256,1152]{1,0:T(8,128)(2,1)S(1)}, u32[]{:S(2)}, u32[]{:S(2)}) collective-permute-start(bf16[256,1152]{1,0:T(8,128)(2,1)} %collective-permute-done.69.refs_2_), channel_id=1, source_target_pairs={{0,1},{1,0},{2,3},{3,2},{4,5},{5,4},{6,7},{7,6},{8,9},{9,8},{10,11... | collective-permute-start | bytes 1769480 | tf_op jit(solution)/shard_map/ppermute | solution.py:43
  263.6 21.8 %collective-permute-start.46 = (bf16[256,768]{1,0:T(8,128)(2,1)S(1)}, bf16[256,768]{1,0:T(8,128)(2,1)S(1)}, u32[]{:S(2)}, u32[]{:S(2)}) collective-permute-start(bf16[256,768]{1,0:T(8,128)(2,1)S(1)} %add_convert_fusion.2.refs_0_), channel_id=1, source_target_pairs={{0,4},{1,5},{2,6},{3,7},{4,0},{5,1},{6,2},{7,3},{8,12},{9,13},{10,... | collective-permute-start | bytes 1179656 | tf_op jit(solution)/shard_map/ppermute | solution.py:43
  264.5 21.6 %collective-permute-start.60 = (bf16[256,768]{1,0:T(8,128)(2,1)S(1)}, bf16[256,768]{1,0:T(8,128)(2,1)S(1)}, u32[]{:S(2)}, u32[]{:S(2)}) collective-permute-start(bf16[256,768]{1,0:T(8,128)(2,1)S(1)} %add_convert_fusion.2.refs_0_), channel_id=1, source_target_pairs={{0,2},{1,3},{2,0},{3,1},{4,6},{5,7},{6,4},{7,5},{8,10},{9,11},{10,... | collective-permute-start | bytes 1179656 | tf_op jit(solution)/shard_map/ppermute | solution.py:43
  271.1 17.4 %collective-permute-start.72 = (bf16[256,1152]{1,0:T(8,128)(2,1)}, bf16[256,1152]{1,0:T(8,128)(2,1)S(1)}, u32[]{:S(2)}, u32[]{:S(2)}) collective-permute-start(bf16[256,1152]{1,0:T(8,128)(2,1)} %collective-permute-done.71.refs_4_), channel_id=1, source_target_pairs={{0,1},{1,0},{2,3},{3,2},{4,5},{5,4},{6,7},{7,6},{8,9},{9,8},{10,11... | collective-permute-start | bytes 1769480 | tf_op jit(solution)/shard_map/ppermute | solution.py:43
  283.3 18.1 %collective-permute-start.53 = (bf16[128,2048]{1,0:T(8,128)(2,1)}, bf16[128,2048]{1,0:T(8,128)(2,1)}, u32[]{:S(2)}, u32[]{:S(2)}) collective-permute-start(bf16[128,2048]{1,0:T(8,128)(2,1)} %get-tuple-element.107), channel_id=1, source_target_pairs={{0,4},{1,5},{2,6},{3,7},{4,0},{5,1},{6,2},{7,3},{8,12},{9,13},{10,... | collective-permute-start | bytes 1572872 | tf_op jit(solution)/shard_map/ppermute | solution.py:43
  284.6 16.9 %collective-permute-start.52 = (bf16[128,2048]{1,0:T(8,128)(2,1)}, bf16[128,2048]{1,0:T(8,128)(2,1)}, u32[]{:S(2)}, u32[]{:S(2)}) collective-permute-start(bf16[128,2048]{1,0:T(8,128)(2,1)} %get-tuple-element.106), channel_id=1, source_target_pairs={{0,2},{1,3},{2,0},{3,1},{4,6},{5,7},{6,4},{7,5},{8,10},{9,11},{10,... | collective-permute-start | bytes 1572872 | tf_op jit(solution)/shard_map/ppermute | solution.py:43
  (119 other events, 969.7 us)

commit v2 on v1

--- a/solution.py
+++ b/solution.py
@@ -19,12 +19,6 @@
 def rms_norm(values, gain_vec):
     return (
         values * lax.rsqrt(jnp.mean(values * values, axis=-1, keepdims=True) + NORM_EPS) * gain_vec
-    )
-
-
-def times_transposed(lhs_mat, rhs_mat):
-    return lax.dot_general(
-        lhs_mat, rhs_mat, (((1,), (1,)), ((), ())), preferred_element_type=F32
     )
 
 
@@ -366,6 +360,32 @@
         target = slice(number * size, (number + 1) * size)
         both_ref[:, target] = hidden_ref[:, source]
         both_ref[:, width + target.start : width + target.stop] = cot_ref[:, source]
+
+
+def gains_kernel(index_ref, attn_ref, mlp_ref, query_ref, key_ref, out_ref):
+    width = attn_ref.shape[1]
+    head = query_ref.shape[1]
+    count = index_ref.shape[0]
+    size = width // count
+    for start, ref in ((0, attn_ref), (width, mlp_ref)):
+        for number in range(count):
+            source = pl.ds(pl.multiple_of(index_ref[number] * size, size), size)
+            out_ref[:, start + number * size : start + (number + 1) * size] = ref[:, source]
+    out_ref[:, 2 * width : 2 * width + head] = query_ref[...]
+    out_ref[:, 2 * width + head :] = key_ref[...]
+
+
+def join_gains(attn, mlp, query, key, indices):
+    columns = 2 * attn.shape[1] + 2 * query.shape[1]
+    return pl.pallas_call(
+        gains_kernel,
+        out_shape=jax.ShapeDtypeStruct((1, columns), F32),
+        in_specs=[pl.BlockSpec(memory_space=pltpu.SMEM)]
+        + [pl.BlockSpec(memory_space=pltpu.VMEM)] * 4,
+        out_specs=pl.BlockSpec(memory_space=pltpu.VMEM),
+        cost_estimate=pl.CostEstimate(flops=0, bytes_accessed=8 * columns, transcendentals=0),
+        name="join_gains",
+    )(indices, attn, mlp, query, key)
 
 
 def own_blocks(hidden, cot, indices):
@@ -465,12 +485,12 @@
             out_ref[:, split:] = transposed_times(left_two[...], right_two[...]).astype(BF16)
 
 
-def weight_grads(left_one, right_one, left_two, right_two, skipped=0):
-    chunks = lax.axis_size("fsdp")
+def weight_grads(numbers, left_one, right_one, left_two, right_two, skipped=0):
+    first, chunks = numbers[0], len(numbers)
     total, width = left_one.shape
-    size = width // chunks
+    size = width // lax.axis_size("fsdp")
     columns = right_one.shape[1] + right_two.shape[1]
-    block = pl.BlockSpec((total, size), lambda step: (0, step))
+    block = pl.BlockSpec((total, size), lambda step: (0, first + step))
     return pl.pallas_call(
         grads_kernel,
         out_shape=[jax.ShapeDtypeStruct((size, columns), BF16)] * chunks,
@@ -478,13 +498,13 @@
         in_specs=[
             block,
             whole(right_one),
-            pl.BlockSpec((total, size), lambda step: (0, skipped + step)),
+            pl.BlockSpec((total, size), lambda step: (0, skipped + first + step)),
             whole(right_two),
         ],
         out_specs=[pl.BlockSpec((size, columns), lambda step: (0, 0))] * chunks,
         cost_estimate=pl.CostEstimate(
-            flops=2 * total * width * columns,
-            bytes_accessed=4 * total * (width + columns),
+            flops=2 * total * size * chunks * columns,
+            bytes_accessed=4 * total * (size * chunks + columns),
             transcendentals=0,
         ),
         name="weight_grads",
@@ -786,9 +806,9 @@
 
 
 def project_back_kernel(
-    chunks, low_ref, dk_ref, dv_ref, raw_ref, kgain_ref, cos_ref, sin_ref, x_ref, blk_ref, *refs
+    chunks, low_ref, dk_ref, dv_ref, raw_ref, kgain_ref, cos_ref, sin_ref, x_ref, act_ref, *refs
 ):
-    w_refs, refs = refs[:chunks], refs[chunks:]
+    w_refs, d_refs, refs = refs[:chunks], refs[chunks : 2 * chunks], refs[2 * chunks :]
     right_ref, even_ref, odd_ref, again_ref, dgain_ref = refs
     head = kgain_ref.shape[1]
     kv_width = dk_ref.shape[1]
@@ -824,11 +844,15 @@
         part = part.astype(BF16)
         even_ref[:, side] = part[:rows]
         odd_ref[:, side] = part[rows:]
-    even_ref[:, width:] = blk_ref[:rows, :]
-    odd_ref[:, width:] = blk_ref[rows:, :]
-
-
-def project_back(low, dk, dv, raw, k_gain, cosine, sine_part, both_all, weights, block_part):
+    act = act_ref[...]
+    for number, d_ref in enumerate(d_refs):
+        side = slice(width + number * size, width + (number + 1) * size)
+        part = nt(act, d_ref[:, d_ref.shape[1] - act.shape[1] :]).astype(BF16)
+        even_ref[:, side] = part[:rows]
+        odd_ref[:, side] = part[rows:]
+
+
+def project_back(low, dk, dv, raw, k_gain, cosine, sine_part, both_all, weights, act, mlp_parts):
     total, q_width = low.shape
     kv_width = dk.shape[1]
     width = both_all.shape[1] // 2
@@ -845,6 +869,11 @@
     first_columns = pl.BlockSpec(
         (weights[0].shape[0], q_width + 2 * kv_width), lambda step: (0, 0)
     )
+    hidden = act.shape[1]
+    if hidden % 128:
+        down_columns = whole(mlp_parts[0])
+    else:
+        down_columns = pl.BlockSpec((mlp_parts[0].shape[0], hidden), lambda step: (0, 2))
     both = pl.BlockSpec((rows, 2 * width), lambda step: (step, 0))
     return pl.pallas_call(
         functools.partial(project_back_kernel, len(weights)),
@@ -858,9 +887,10 @@
         grid=(steps,),
         in_specs=[
             wide(q_width), wide(kv_width), wide(kv_width), wide(q_width + kv_width),
-            whole(k_gain), wide(head), wide(head), wide(width), wide(width),
+            whole(k_gain), wide(head), wide(head), wide(width), wide(hidden),
         ]
-        + [first_columns] * len(weights),
+        + [first_columns] * len(weights)
+        + [down_columns] * len(weights),
         out_specs=[
             wide(q_width + 2 * kv_width), both, both, fixed((1, width)), fixed((1, head)),
         ],
@@ -870,7 +900,7 @@
             transcendentals=total,
         ),
         name="project_back",
-    )(low, dk, dv, raw, k_gain, cosine, sine_part, both_all, block_part, *weights)
+    )(low, dk, dv, raw, k_gain, cosine, sine_part, both_all, act, *weights, *mlp_parts)
 
 
 def on_device_all(
@@ -986,9 +1016,16 @@
         mlp_pieces, both_all, mlp_parts, ctx_count
     )
     mlp_in_grad = scatter_ctx(part_even, part_odd)
-    mlp_sums = dict(enumerate(weight_grads(mlp_all, mlp_right, both_all, hidden_act, fsdp_count)))
-    down_w = jnp.concatenate([part[:, 2 * hidden_width :] for part in mlp_parts], axis=0)
-    block_part = times_transposed(hidden_act, down_w).astype(BF16)
+    last = fsdp_count - 1
+
+    def all_grads(*operands):
+        sums = {last: weight_grads([last], *operands)[0]}
+        if last:
+            numbers = list(range(last))
+            sums.update(zip(numbers, weight_grads(numbers, *operands)))
+        return sums
+
+    mlp_sums = all_grads(mlp_all, mlp_right, both_all, hidden_act, fsdp_count)
     resid_part, mlp_gain_grad = jax.vjp(rms_norm, resid, mlp_gain_rel)[1](mlp_in_grad)
     resid_grad = cot_low.astype(F32) + resid_part
     resid_low = resid_grad.astype(BF16)
@@ -1025,11 +1062,8 @@
         ]
     attn_right, tail_even, tail_odd, attn_gain_grad, key_gain_grad = project_back(
         query_low, key_grad, value_grad, attn_raw, key_row, cosine, sine_part,
-        both_all, own_parts, block_part,
-    )
-    attn_gain_grad = attn_gain_grad[0]
-    query_gain_grad = query_gain_grad[0]
-    key_gain_grad = key_gain_grad[0]
+        both_all, own_parts, hidden_act, mlp_parts,
+    )
     if kv_share > 1:
         attn_right = jnp.concatenate(
             [
@@ -1040,7 +1074,7 @@
             axis=1,
         )
         key_gain_grad = jnp.where(ctx_index % kv_share == 0, key_gain_grad, 0.0)
-    attn_sums = dict(enumerate(weight_grads(attn_in, attn_right, resid_all, attn_mix)))
+    attn_sums = all_grads(attn_in, attn_right, resid_all, attn_mix)
     for level in range(fsdp_levels, 0, -1):
         attn_sums = scatter_fsdp_step(attn_sums, fsdp_count, level)
     attn_grads = attn_sums[0].astype(BF16)
@@ -1056,17 +1090,11 @@
         attn_in_grad
     )[0]
     input_grad = resid_grad + input_part
-    gains = sum_all(
-        jnp.concatenate(
-            [
-                block_order(attn_gain_grad),
-                block_order(mlp_gain_grad),
-                query_gain_grad,
-                key_gain_grad,
-            ]
-        )
-    )
-
+    gains = join_gains(
+        attn_gain_grad, mlp_gain_grad.reshape(1, width), query_gain_grad, key_gain_grad,
+        fsdp_order,
+    )
+    gains = sum_all(gains)[0]
     outs = (
         block_order(block_out)[None],
         block_order(input_grad)[None],

time: 314 us -> 321 us (1.022)
  Pallas kernels: 93.2 us -> 99.6 us
  other arithmetic: 18.8 us -> 24.3 us
  local copies, waits for them, and re-layouts: 24.8 us -> 20.4 us
    pallas_call x2 -> x4, Pallas kernels: 13.4 us -> 18.2 us  [weight_grads(): pl.pallas_call(grads_kernel, out_shape=[jax.ShapeDtypeStruct((size, colum...]
    unnamed x137 -> x124, local copies, waits for them, and re-layouts: 9.88 us -> 9.3 us
  transfers between devices with their start and end apart: 77 -> 77, of which waited for: 25 -> 26; matrix products, arithmetic and copies ran while one was open for 12% -> 11% of each run, Pallas kernels for 18% -> 19%
where the time goes in v2:
time: 321 us; the launch traced here: 319 us
  waiting for transfers between devices  119 us (37%)
  Pallas kernels  99.6 us (31%)
  starting transfers between devices  54.4 us (17%)
  other arithmetic  24.3 us (8%)
  local copies, waits for them, and re-layouts  20.4 us (6%)
    ppermute x77, waiting for transfers between devices, exchange(): lax.ppermute(value, axis, [(index, index ^ bit) for index in range(count)])  119 us
    ppermute x77, starting transfers between devices, exchange(): lax.ppermute(value, axis, [(index, index ^ bit) for index in range(count)])  54.4 us
    pallas_call x4, Pallas kernels, weight_grads(): pl.pallas_call(grads_kernel, out_shape=[jax.ShapeDtypeStruct((size, colum...  18.2 us
    pallas_call x1, Pallas kernels, attend_back(): pl.pallas_call(functools.partial(attend_back_kernel, piece_plan(pieces),...  12 us
    pallas_call x1, Pallas kernels, attend(): pl.pallas_call(functools.partial(attend_kernel, len(weights)), out_shape=...  11.3 us
    pallas_call x2, Pallas kernels, place_columns(): pl.pallas_call(kernel, out_shape=[jax.ShapeDtypeStruct((rows, count * wid...  10.8 us
    pallas_call x1, Pallas kernels, mlp_both(): pl.pallas_call(functools.partial(mlp_kernel, piece_plan(pieces), len(weig...  9.69 us
    unnamed x124, local copies, waits for them, and re-layouts  9.3 us
  transfers between devices with their start and end apart: 77, of which 26 were waited for; matrix products, arithmetic and copies ran while one was open for 11% of the time, Pallas kernels for 19%

profile of v2, /device:TPU:0, one launch (start us, length us, event | category | flops | bytes accessed | tf_op | source)
XLA Modules:
  0.0 319.3 jit_solution(12312189283960578097)
XLA Ops:
  22.4 10.1 %collective-permute-done.10.refs_12_.refs_2_ = bf16[256,768]{1,0:T(8,128)(2,1)S(1)} collective-permute-done((bf16[256,768]{1,0:T(8,128)(2,1)}, bf16[256,768]{1,0:T(8,128)(2,1)S(1)}, u32[]{:S(2)}, u32[]{:S(2)}) %collective-permute-start.10) | collective-permute-done | bytes 393248 | tf_op jit(solution)/shard_map/ppermute | solution.py:37
  37.8 3.7 %fusion = (f32[1024,128]{1,0:T(8,128)}, f32[1024,128]{1,0:T(8,128)}) fusion(f32[128]{0:T(128)S(1)} %get-tuple-element.161, f32[128]{0:T(128)} %get-tuple-element.162, f32[1024]{0:T(1024)S(1)} %convert_element_type.112), kind=kLoop, calls=%fused_computation.13 | loop fusion | flops 262144 | bytes 1053696 | tf_op jit(solution)/shard_map/mul | solution.py:996
  42.5 8.2 %project.1 = (bf16[1024,1024]{1,0:T(8,128)(2,1)}, f32[1024,384]{1,0:T(8,128)}, bf16[1024,256]{1,0:T(8,128)(2,1)}, bf16[1024,128]{1,0:T(8,128)(2,1)}, bf16[1024,1...) custom-call(bf16[128,2048]{1,0:T(8,128)(2,1)} %own_blocks.1.refs_0_, bf16[128,2048]{1,0:T(8,128)(2,1)} %copy-done.21, ...), custom_call_target="tpu_custom_call" | custom-call | flops 1073741824 | bytes 12582912 | tf_op jit(solution)/shard_map/project/pallas_call | solution.py:584
  50.7 11.3 %attend.1 = (bf16[1024,256]{1,0:T(8,128)(2,1)}, f32[2,1024]{1,0:T(2,128)}, bf16[512,1024]{1,0:T(8,128)(2,1)}, bf16[512,1024]{1,0:T(8,128)(2,1)}) custom-call(bf16[1024,256]{1,0:T(8,128)(2,1)} %get-tuple-element.71.q_ref.refs_14_, bf16[1024,128]{1,0:T(8,128)(2,1)} %get-tuple-element.72.k_ref.refs_15_, bf16[1024,128]{1,0:T(8,128)(2,1)} %get-tuple-element.73.v_ref.refs_16_, ...), custom_call_target="tpu_custom_call" | custom-call | flops 1073741824 | bytes 8388608 | tf_op jit(solution)/shard_map/attend/pallas_call | solution.py:667
  71.7 4.6 %collective-permute-done.13.first = bf16[64,1024]{1,0:T(8,128)(2,1)S(1)} collective-permute-done((bf16[64,1024]{1,0:T(8,128)(2,1)}, bf16[64,1024]{1,0:T(8,128)(2,1)S(1)}, u32[]{:S(2)}, u32[]{:S(2)}) %collective-permute-start.13) | collective-permute-done | bytes 131104 | tf_op jit(solution)/shard_map/ppermute | solution.py:37
  81.5 13.2 %collective-permute-done.27.refs_13_.refs_6_ = bf16[256,1152]{1,0:T(8,128)(2,1)S(1)} collective-permute-done((bf16[256,1152]{1,0:T(8,128)(2,1)}, bf16[256,1152]{1,0:T(8,128)(2,1)S(1)}, u32[]{:S(2)}, u32[]{:S(2)}) %collective-permute-start.27) | collective-permute-done | bytes 589856 | tf_op jit(solution)/shard_map/ppermute | solution.py:37
  97.6 6.6 %collective-permute-done.18.refs_2_ = bf16[128,1024]{1,0:T(8,128)(2,1)S(1)} collective-permute-done((bf16[128,1024]{1,0:T(8,128)(2,1)S(1)}, bf16[128,1024]{1,0:T(8,128)(2,1)S(1)}, u32[]{:S(2)}, u32[]{:S(2)}) %collective-permute-start.18) | collective-permute-done | bytes 262176 | tf_op jit(solution)/shard_map/ppermute | solution.py:37
  107.4 11.8 %collective-permute-done.28.refs_14_.refs_7_ = bf16[256,1152]{1,0:T(8,128)(2,1)S(1)} collective-permute-done((bf16[256,1152]{1,0:T(8,128)(2,1)S(1)}, bf16[256,1152]{1,0:T(8,128)(2,1)S(1)}, u32[]{:S(2)}, u32[]{:S(2)}) %collective-permute-start.28) | collective-permute-done | bytes 589856 | tf_op jit(solution)/shard_map/ppermute | solution.py:37
  120.5 3.7 %collective-permute-done.24.refs_8_ = bf16[64,1024]{1,0:T(8,128)(2,1)S(1)} collective-permute-done((bf16[64,1024]{1,0:T(8,128)(2,1)S(1)}, bf16[64,1024]{1,0:T(8,128)(2,1)S(1)}, u32[]{:S(2)}, u32[]{:S(2)}) %collective-permute-start.24) | collective-permute-done | bytes 131104 | tf_op jit(solution)/shard_map/ppermute | solution.py:37
  126.3 9.7 %mlp_both.1 = (bf16[1024,768]{1,0:T(8,128)(2,1)}, bf16[1024,384]{1,0:T(8,128)(2,1)}, bf16[512,1024]{1,0:T(8,128)(2,1)}, bf16[512,1024]{1,0:T(8,128)(2,1)}, bf16[1024,1024]{1,0:T(8,128)(2,1)}) custom-call(bf16[128,1024]{1,0:T(8,128)(2,1)} %copy-done.32, bf16[128,1024]{1,0:T(8,128)(2,1)} %copy-done.49, bf16[128,1024]{1,0:T(8,128)(2,1)} %copy-done.41, ...), custom_call_target="tpu_custom_call" | custom-call | flops 4026531840 | bytes 12582912 | tf_op jit(solution)/shard_map/mlp_both/pallas_call | solution.py:454
  153.6 3.8 %weight_grads.7 = bf16[256,1152]{1,0:T(8,128)(2,1)} custom-call(bf16[1024,1024]{1,0:T(8,128)(2,1)} %get-tuple-element.119.left_one, bf16[1024,768]{1,0:T(8,128)(2,1)} %get-tuple-element.120.right_one, bf16[1024,2048]{1,0:T(8,128)(2,1)} %get-tuple-element.80.refs_10_.x_ref.left_two, bf16[1024,384]{1,0:T(8,128)(2,1)} %get-tuple-element.93.act_ref.right_two), custom_call_target="tpu_custom_call" | custom-call | flops 603979776 | bytes 5767168 | tf_op jit(solution)/shard_map/weight_grads/pallas_call | solution.py:494
  165.9 4.2 %collective-permute-done.35.refs_2_ = bf16[128,1024]{1,0:T(8,128)(2,1)S(1)} collective-permute-done((bf16[128,1024]{1,0:T(8,128)(2,1)S(1)}, bf16[128,1024]{1,0:T(8,128)(2,1)S(1)}, u32[]{:S(2)}, u32[]{:S(2)}) %collective-permute-start.35) | collective-permute-done | bytes 262176 | tf_op jit(solution)/shard_map/ppermute | solution.py:37
  173.4 6.1 %weight_grads.6 = (bf16[256,1152]{1,0:T(8,128)(2,1)}, bf16[256,1152]{1,0:T(8,128)(2,1)}, bf16[256,1152]{1,0:T(8,128)(2,1)}) custom-call(bf16[1024,1024]{1,0:T(8,128)(2,1)} %get-tuple-element.119.left_one, bf16[1024,768]{1,0:T(8,128)(2,1)} %get-tuple-element.120.right_one, bf16[1024,2048]{1,0:T(8,128)(2,1)} %get-tuple-element.80.refs_10_.x_ref.left_two, ...), custom_call_target="tpu_custom_call" | custom-call | flops 1811939328 | bytes 7864320 | tf_op jit(solution)/shard_map/weight_grads/pallas_call | solution.py:494
  184.7 12.0 %attend_back.1 = (bf16[1024,256]{1,0:T(8,128)(2,1)}, f32[1024,128]{1,0:T(8,128)}, f32[1024,128]{1,0:T(8,128)}, f32[1,128]{1,0:T(1,128)}, bf16[1024,1024]{1,0:T(8,128)(2,1)}) custom-call(bf16[128,1024]{1,0:T(8,128)(2,1)} %copy-done.27, bf16[128,1024]{1,0:T(8,128)(2,1)} %copy-done.48, bf16[128,1024]{1,0:T(8,128)(2,1)} %copy-done.39, ...), custom_call_target="tpu_custom_call" | custom-call | flops 2684354560 | bytes 8388608 | tf_op jit(solution)/shard_map/attend_back/pallas_call | solution.py:771
  196.7 8.3 %project_back.1 = (bf16[1024,512]{1,0:T(8,128)(2,1)}, bf16[512,2048]{1,0:T(8,128)(2,1)}, bf16[512,2048]{1,0:T(8,128)(2,1)}, f32[1,1024]{1,0:T(1,128)}, f32[1,128]{1,0:T(1,128)}) custom-call(bf16[1024,256]{1,0:T(8,128)(2,1)} %get-tuple-element.90.low_ref, f32[1024,128]{1,0:T(8,128)} %get-tuple-element.91.dk_ref, f32[1024,128]{1,0:T(8,128)} %get-tuple-element.92.dv_ref, ...), custom_call_target="tpu_custom_call" | custom-call | flops 1073741824 | bytes 12582912 | tf_op jit(solution)/shard_map/project_back/pallas_call | solution.py:878
  205.1 4.1 %collective-permute-done.65 = bf16[256,1152]{1,0:T(8,128)(2,1)} collective-permute-done((bf16[256,1152]{1,0:T(8,128)(2,1)}, bf16[256,1152]{1,0:T(8,128)(2,1)}, u32[]{:S(2)}, u32[]{:S(2)}) %collective-permute-start.65) | collective-permute-done | bytes 589856 | tf_op jit(solution)/shard_map/ppermute | solution.py:37
  223.6 6.6 %collective-permute-done.55 = f32[1,2304]{1,0:T(1,128)S(1)} collective-permute-done((f32[1,2304]{1,0:T(1,128)S(1)}, f32[1,2304]{1,0:T(1,128)S(1)}, u32[]{:S(2)}, u32[]{:S(2)}) %collective-permute-start.55) | collective-permute-done | bytes 9248 | tf_op jit(solution)/shard_map/ppermute | solution.py:37
  230.9 5.2 %weight_grads.4 = (bf16[256,768]{1,0:T(8,128)(2,1)}, bf16[256,768]{1,0:T(8,128)(2,1)}, bf16[256,768]{1,0:T(8,128)(2,1)}) custom-call(bf16[1024,1024]{1,0:T(8,128)(2,1)} %get-tuple-element.70.left_one, bf16[1024,512]{1,0:T(8,128)(2,1)} %get-tuple-element.94.right_one, bf16[1024,1024]{1,0:T(8,128)(2,1)} %get-tuple-element.95.left_two, ...), custom_call_target="tpu_custom_call" | custom-call | flops 1207959552 | bytes 6291456 | tf_op jit(solution)/shard_map/weight_grads/pallas_call | solution.py:494
  242.1 5.8 %collective-permute-done.57 = f32[1,2304]{1,0:T(1,128)S(1)} collective-permute-done((f32[1,2304]{1,0:T(1,128)S(1)}, f32[1,2304]{1,0:T(1,128)S(1)}, u32[]{:S(2)}, u32[]{:S(2)}) %collective-permute-start.57) | collective-permute-done | bytes 9248 | tf_op jit(solution)/shard_map/ppermute | solution.py:37
  256.9 9.4 %collective-permute-done.45 = bf16[256,768]{1,0:T(8,128)(2,1)} collective-permute-done((bf16[256,768]{1,0:T(8,128)(2,1)}, bf16[256,768]{1,0:T(8,128)(2,1)}, u32[]{:S(2)}, u32[]{:S(2)}) %collective-permute-start.45) | collective-permute-done | bytes 393248 | tf_op jit(solution)/shard_map/ppermute | solution.py:37
  279.3 10.3 %collective-permute-done.75.refs_8_ = bf16[128,1152]{1,0:T(8,128)(2,1)} collective-permute-done((bf16[128,1152]{1,0:T(8,128)(2,1)}, bf16[128,1152]{1,0:T(8,128)(2,1)}, u32[]{:S(2)}, u32[]{:S(2)}) %collective-permute-start.75) | collective-permute-done | bytes 294944 | tf_op jit(solution)/shard_map/ppermute | solution.py:37
  297.4 5.9 %place_columns.3 = (f32[256,3072]{1,0:T(8,128)}, f32[256,3072]{1,0:T(8,128)}, f32[256,3072]{1,0:T(8,128)}) custom-call(s32[5]{0:T(128)} %stack.56.index_ref, bf16[256,1152]{1,0:T(8,128)(2,1)} %add_convert_fusion.refs_0_, bf16[256,1152]{1,0:T(8,128)(2,1)} %collective-permute-done.68.refs_1_, bf16[256,1152]{1,0:T(8,128)(2,1)} %collective-permute-done.69.refs_2_, ...), custom_call_target="tpu_custom_call" | custom-call | bytes 14155776 | tf_op jit(solution)/shard_map/place_columns/pallas_call | solution.py:334
  303.4 4.4 %collective-permute-done.47.refs_8_ = bf16[128,768]{1,0:T(8,128)(2,1)} collective-permute-done((bf16[128,768]{1,0:T(8,128)(2,1)}, bf16[128,768]{1,0:T(8,128)(2,1)}, u32[]{:S(2)}, u32[]{:S(2)}) %collective-permute-start.47) | collective-permute-done | bytes 196640 | tf_op jit(solution)/shard_map/ppermute | solution.py:37
  314.3 4.9 %place_columns.2 = (f32[256,2048]{1,0:T(8,128)}, f32[256,1024]{1,0:T(8,128)}, f32[256,1024]{1,0:T(8,128)}, f32[256,2048]{1,0:T(8,128)}) custom-call(s32[5]{0:T(128)} %stack.56.index_ref, bf16[256,768]{1,0:T(8,128)(2,1)} %copy-done.11, bf16[256,768]{1,0:T(8,128)(2,1)} %copy-done.24, bf16[256,768]{1,0:T(8,128)(2,1)} %copy-done.15, ...), custom_call_target="tpu_custom_call" | custom-call | bytes 9437184 | tf_op jit(solution)/shard_map/place_columns/pallas_call | solution.py:334
  (328 shorter events, 143.5 us)
Async XLA Ops:
  3.1 29.8 %collective-permute-start = (bf16[128,2048]{1,0:T(8,128)(2,1)}, bf16[128,2048]{1,0:T(8,128)(2,1)S(1)}, u32[]{:S(2)}, u32[]{:S(2)}) collective-permute-start(bf16[128,2048]{1,0:T(8,128)(2,1)} %own_blocks.1.refs_0_), channel_id=1, source_target_pairs={{0,1},{1,0},{2,3},{3,2},{4,5},{5,4},{6,7},{7,6},{8,9},{9,8},{10,11... | collective-permute-start | bytes 1572872 | tf_op jit(solution)/shard_map/ppermute | solution.py:37
  10.6 22.3 %collective-permute-start.9 = (bf16[256,768]{1,0:T(8,128)(2,1)}, bf16[256,768]{1,0:T(8,128)(2,1)S(1)}, u32[]{:S(2)}, u32[]{:S(2)}) collective-permute-start(bf16[256,768]{1,0:T(8,128)(2,1)} %pick_columns.2.refs_10_.refs_0_), channel_id=1, source_target_pairs={{0,8},{8,0},{16,24},{24,16},{1,9},{9,1},{17,25},{25,17},{2,10},{10... | collective-permute-start | bytes 1179656 | tf_op jit(solution)/shard_map/ppermute | solution.py:37
  12.2 20.3 %collective-permute-start.10 = (bf16[256,768]{1,0:T(8,128)(2,1)}, bf16[256,768]{1,0:T(8,128)(2,1)S(1)}, u32[]{:S(2)}, u32[]{:S(2)}) collective-permute-start(bf16[256,768]{1,0:T(8,128)(2,1)} %pick_columns.2.refs_10_.refs_0_), channel_id=1, source_target_pairs={{0,16},{8,24},{16,0},{24,8},{1,17},{9,25},{17,1},{25,9},{2,18},{10... | collective-permute-start | bytes 1179656 | tf_op jit(solution)/shard_map/ppermute | solution.py:37
  65.3 29.5 %collective-permute-start.27 = (bf16[256,1152]{1,0:T(8,128)(2,1)}, bf16[256,1152]{1,0:T(8,128)(2,1)S(1)}, u32[]{:S(2)}, u32[]{:S(2)}) collective-permute-start(bf16[256,1152]{1,0:T(8,128)(2,1)} %pick_columns.3.refs_11_.refs_4_), channel_id=1, source_target_pairs={{0,16},{8,24},{16,0},{24,8},{1,17},{9,25},{17,1},{25,9},{2,18},{10... | collective-permute-start | bytes 1769480 | tf_op jit(solution)/shard_map/ppermute | solution.py:37
  81.5 25.9 %collective-permute-start.26 = (bf16[256,1152]{1,0:T(8,128)(2,1)S(1)}, bf16[256,1152]{1,0:T(8,128)(2,1)S(1)}, u32[]{:S(2)}, u32[]{:S(2)}) collective-permute-start(bf16[256,1152]{1,0:T(8,128)(2,1)S(1)} %copy-done.6), channel_id=1, source_target_pairs={{0,8},{8,0},{16,24},{24,16},{1,9},{9,1},{17,25},{25,17},{2,10},{10... | collective-permute-start | bytes 1769480 | tf_op jit(solution)/shard_map/ppermute | solution.py:37
  94.8 24.5 %collective-permute-start.28 = (bf16[256,1152]{1,0:T(8,128)(2,1)S(1)}, bf16[256,1152]{1,0:T(8,128)(2,1)S(1)}, u32[]{:S(2)}, u32[]{:S(2)}) collective-permute-start(bf16[256,1152]{1,0:T(8,128)(2,1)S(1)} %collective-permute-done.27.refs_13_.refs_6_), channel_id=1, source_target_pairs={{0,8},{8,0},{16,24},{24,16},{1,9},{9,1},{17,25},{25,17},{2,10},{10... | collective-permute-start | bytes 1769480 | tf_op jit(solution)/shard_map/ppermute | solution.py:37
  97.5 26.7 %collective-permute-start.17 = (bf16[128,1024]{1,0:T(8,128)(2,1)S(1)}, bf16[128,1024]{1,0:T(8,128)(2,1)S(1)}, u32[]{:S(2)}, u32[]{:S(2)}) collective-permute-start(bf16[128,1024]{1,0:T(8,128)(2,1)S(1)} %multiply_convert_fusion.refs_0_), channel_id=1, source_target_pairs={{0,1},{1,0},{2,3},{3,2},{4,5},{5,4},{6,7},{7,6},{8,9},{9,8},{10,11... | collective-permute-start | bytes 786440 | tf_op jit(solution)/shard_map/ppermute | solution.py:37
  104.8 19.5 %collective-permute-start.19 = (bf16[128,1024]{1,0:T(8,128)(2,1)S(1)}, bf16[128,1024]{1,0:T(8,128)(2,1)S(1)}, u32[]{:S(2)}, u32[]{:S(2)}) collective-permute-start(bf16[128,1024]{1,0:T(8,128)(2,1)S(1)} %collective-permute-done.18.refs_2_), channel_id=1, source_target_pairs={{0,1},{1,0},{2,3},{3,2},{4,5},{5,4},{6,7},{7,6},{8,9},{9,8},{10,11... | collective-permute-start | bytes 786440 | tf_op jit(solution)/shard_map/ppermute | solution.py:37
  157.4 22.7 %collective-permute-start.66 = (bf16[256,1152]{1,0:T(8,128)(2,1)}, bf16[256,1152]{1,0:T(8,128)(2,1)}, u32[]{:S(2)}, u32[]{:S(2)}) collective-permute-start(bf16[256,1152]{1,0:T(8,128)(2,1)} %weight_grads.7), channel_id=1, source_target_pairs={{0,8},{8,0},{16,24},{24,16},{1,9},{9,1},{17,25},{25,17},{2,10},{10... | collective-permute-start | bytes 1769480 | tf_op jit(solution)/shard_map/ppermute | solution.py:37
  182.9 26.4 %collective-permute-start.65 = (bf16[256,1152]{1,0:T(8,128)(2,1)}, bf16[256,1152]{1,0:T(8,128)(2,1)}, u32[]{:S(2)}, u32[]{:S(2)}) collective-permute-start(bf16[256,1152]{1,0:T(8,128)(2,1)} %get-tuple-element.122), channel_id=1, source_target_pairs={{0,8},{8,0},{16,24},{24,16},{1,9},{9,1},{17,25},{25,17},{2,10},{10... | collective-permute-start | bytes 1769480 | tf_op jit(solution)/shard_map/ppermute | solution.py:37
  182.9 29.6 %collective-permute-start.67 = (bf16[256,1152]{1,0:T(8,128)(2,1)}, bf16[256,1152]{1,0:T(8,128)(2,1)}, u32[]{:S(2)}, u32[]{:S(2)}) collective-permute-start(bf16[256,1152]{1,0:T(8,128)(2,1)} %add_convert_fusion.1), channel_id=1, source_target_pairs={{0,16},{8,24},{16,0},{24,8},{1,17},{9,25},{17,1},{25,9},{2,18},{10... | collective-permute-start | bytes 1769480 | tf_op jit(solution)/shard_map/ppermute | solution.py:37
  205.0 45.3 %collective-permute-start.49 = (bf16[512,2048]{1,0:T(8,128)(2,1)}, bf16[512,2048]{1,0:T(8,128)(2,1)S(1)}, u32[]{:S(2)}, u32[]{:S(2)}) collective-permute-start(bf16[512,2048]{1,0:T(8,128)(2,1)} %get-tuple-element.100), channel_id=1, source_target_pairs={{0,1},{1,0},{2,3},{3,2},{4,5},{5,4},{6,7},{7,6},{8,9},{9,8},{10,11... | collective-permute-start | bytes 6291464 | tf_op jit(solution)/shard_map/ppermute | solution.py:37
  215.0 23.2 %collective-permute-start.69 = (bf16[256,1152]{1,0:T(8,128)(2,1)}, bf16[256,1152]{1,0:T(8,128)(2,1)}, u32[]{:S(2)}, u32[]{:S(2)}) collective-permute-start(bf16[256,1152]{1,0:T(8,128)(2,1)} %add_convert_fusion.refs_0_), channel_id=1, source_target_pairs={{0,2},{1,3},{2,0},{3,1},{4,6},{5,7},{6,4},{7,5},{8,10},{9,11},{10,... | collective-permute-start | bytes 1769480 | tf_op jit(solution)/shard_map/ppermute | solution.py:37
  218.7 19.6 %collective-permute-start.44 = (bf16[256,768]{1,0:T(8,128)(2,1)}, bf16[256,768]{1,0:T(8,128)(2,1)S(1)}, u32[]{:S(2)}, u32[]{:S(2)}) collective-permute-start(bf16[256,768]{1,0:T(8,128)(2,1)} %weight_grads.5), channel_id=1, source_target_pairs={{0,8},{8,0},{16,24},{24,16},{1,9},{9,1},{17,25},{25,17},{2,10},{10... | collective-permute-start | bytes 1179656 | tf_op jit(solution)/shard_map/ppermute | solution.py:37
  223.6 30.2 %collective-permute-start.68 = (bf16[256,1152]{1,0:T(8,128)(2,1)}, bf16[256,1152]{1,0:T(8,128)(2,1)}, u32[]{:S(2)}, u32[]{:S(2)}) collective-permute-start(bf16[256,1152]{1,0:T(8,128)(2,1)} %add_convert_fusion.refs_0_), channel_id=1, source_target_pairs={{0,1},{1,0},{2,3},{3,2},{4,5},{5,4},{6,7},{7,6},{8,9},{9,8},{10,11... | collective-permute-start | bytes 1769480 | tf_op jit(solution)/shard_map/ppermute | solution.py:37
  238.2 17.9 %collective-permute-start.43 = (bf16[256,768]{1,0:T(8,128)(2,1)}, bf16[256,768]{1,0:T(8,128)(2,1)}, u32[]{:S(2)}, u32[]{:S(2)}) collective-permute-start(bf16[256,768]{1,0:T(8,128)(2,1)} %get-tuple-element.97), channel_id=1, source_target_pairs={{0,8},{8,0},{16,24},{24,16},{1,9},{9,1},{17,25},{25,17},{2,10},{10... | collective-permute-start | bytes 1179656 | tf_op jit(solution)/shard_map/ppermute | solution.py:37
  247.9 18.4 %collective-permute-start.45 = (bf16[256,768]{1,0:T(8,128)(2,1)}, bf16[256,768]{1,0:T(8,128)(2,1)}, u32[]{:S(2)}, u32[]{:S(2)}) collective-permute-start(bf16[256,768]{1,0:T(8,128)(2,1)} %add_convert_fusion.3), channel_id=1, source_target_pairs={{0,16},{8,24},{16,0},{24,8},{1,17},{9,25},{17,1},{25,9},{2,18},{10... | collective-permute-start | bytes 1179656 | tf_op jit(solution)/shard_map/ppermute | solution.py:37
  250.4 19.8 %collective-permute-start.73 = (bf16[128,1152]{1,0:T(8,128)(2,1)}, bf16[128,1152]{1,0:T(8,128)(2,1)}, u32[]{:S(2)}, u32[]{:S(2)}) collective-permute-start(bf16[128,1152]{1,0:T(8,128)(2,1)} %slice.141), channel_id=1, source_target_pairs={{0,4},{1,5},{2,6},{3,7},{4,0},{5,1},{6,2},{7,3},{8,12},{9,13},{10,... | collective-permute-start | bytes 884744 | tf_op jit(solution)/shard_map/ppermute | solution.py:37
  253.8 36.9 %collective-permute-start.70 = (bf16[256,1152]{1,0:T(8,128)(2,1)}, bf16[256,1152]{1,0:T(8,128)(2,1)S(1)}, u32[]{:S(2)}, u32[]{:S(2)}) collective-permute-start(bf16[256,1152]{1,0:T(8,128)(2,1)} %collective-permute-done.69.refs_2_), channel_id=1, source_target_pairs={{0,1},{1,0},{2,3},{3,2},{4,5},{5,4},{6,7},{7,6},{8,9},{9,8},{10,11... | collective-permute-start | bytes 1769480 | tf_op jit(solution)/shard_map/ppermute | solution.py:37
  268.4 23.6 %collective-permute-start.46 = (bf16[256,768]{1,0:T(8,128)(2,1)S(1)}, bf16[256,768]{1,0:T(8,128)(2,1)S(1)}, u32[]{:S(2)}, u32[]{:S(2)}) collective-permute-start(bf16[256,768]{1,0:T(8,128)(2,1)S(1)} %add_convert_fusion.2.refs_0_), channel_id=1, source_target_pairs={{0,4},{1,5},{2,6},{3,7},{4,0},{5,1},{6,2},{7,3},{8,12},{9,13},{10,... | collective-permute-start | bytes 1179656 | tf_op jit(solution)/shard_map/ppermute | solution.py:37
  270.1 22.5 %collective-permute-start.60 = (bf16[256,768]{1,0:T(8,128)(2,1)S(1)}, bf16[256,768]{1,0:T(8,128)(2,1)S(1)}, u32[]{:S(2)}, u32[]{:S(2)}) collective-permute-start(bf16[256,768]{1,0:T(8,128)(2,1)S(1)} %add_convert_fusion.2.refs_0_), channel_id=1, source_target_pairs={{0,2},{1,3},{2,0},{3,1},{4,6},{5,7},{6,4},{7,5},{8,10},{9,11},{10,... | collective-permute-start | bytes 1179656 | tf_op jit(solution)/shard_map/ppermute | solution.py:37
  276.5 18.7 %collective-permute-start.72 = (bf16[256,1152]{1,0:T(8,128)(2,1)}, bf16[256,1152]{1,0:T(8,128)(2,1)S(1)}, u32[]{:S(2)}, u32[]{:S(2)}) collective-permute-start(bf16[256,1152]{1,0:T(8,128)(2,1)} %collective-permute-done.71.refs_4_), channel_id=1, source_target_pairs={{0,1},{1,0},{2,3},{3,2},{4,5},{5,4},{6,7},{7,6},{8,9},{9,8},{10,11... | collective-permute-start | bytes 1769480 | tf_op jit(solution)/shard_map/ppermute | solution.py:37
  289.6 18.7 %collective-permute-start.53 = (bf16[128,2048]{1,0:T(8,128)(2,1)}, bf16[128,2048]{1,0:T(8,128)(2,1)}, u32[]{:S(2)}, u32[]{:S(2)}) collective-permute-start(bf16[128,2048]{1,0:T(8,128)(2,1)} %get-tuple-element.104), channel_id=1, source_target_pairs={{0,4},{1,5},{2,6},{3,7},{4,0},{5,1},{6,2},{7,3},{8,12},{9,13},{10,... | collective-permute-start | bytes 1572872 | tf_op jit(solution)/shard_map/ppermute | solution.py:37
  290.6 17.7 %collective-permute-start.52 = (bf16[128,2048]{1,0:T(8,128)(2,1)}, bf16[128,2048]{1,0:T(8,128)(2,1)}, u32[]{:S(2)}, u32[]{:S(2)}) collective-permute-start(bf16[128,2048]{1,0:T(8,128)(2,1)} %get-tuple-element.103), channel_id=1, source_target_pairs={{0,2},{1,3},{2,0},{3,1},{4,6},{5,7},{6,4},{7,5},{8,10},{9,11},{10,... | collective-permute-start | bytes 1572872 | tf_op jit(solution)/shard_map/ppermute | solution.py:37
  (115 other events, 921.9 us)

commit v3 on v2

--- a/solution.py
+++ b/solution.py
@@ -14,6 +14,8 @@
 MASKED = -1e30
 F32 = jnp.float32
 BF16 = jnp.bfloat16
+CTX = "ctx"
+FSDP = "fsdp"
 
 
 def rms_norm(values, gain_vec):
@@ -58,7 +60,7 @@
 
 
 def gather_ctx(own):
-    count = lax.axis_size("ctx")
+    count = lax.axis_size(CTX)
     rows = own.shape[0]
     half = rows // 2
     parts = {0: [own]}
@@ -66,18 +68,18 @@
         for number in even_numbers(count, level):
             low, top = low_bit(number), top_bit(number)
             if level == 1:
-                parts[number] = [exchange(own, low, "ctx")]
+                parts[number] = [exchange(own, low, CTX)]
             else:
                 parts[number] = [
-                    exchange(rows_of(parts[number ^ top], 0, half), top, "ctx"),
-                    exchange(rows_of(parts[number ^ low], half, rows), low, "ctx"),
+                    exchange(rows_of(parts[number ^ top], 0, half), top, CTX),
+                    exchange(rows_of(parts[number ^ low], half, rows), low, CTX),
                 ]
     pieces = []
     for number in range(0, count, 2):
         start = number // 2 * rows
         for part in parts[number]:
             pieces.append((0, start, part))
-            other = exchange(part, 1, "ctx")
+            other = exchange(part, 1, CTX)
             pieces.append((1, start, other))
             start += part.shape[0]
     return pieces
@@ -154,7 +156,7 @@
 
 
 def scatter_eight(even, odd):
-    moved = exchange(odd, 1, "ctx")
+    moved = exchange(odd, 1, CTX)
     rows = even.shape[0] // 4
     half = rows // 2
     width = even.shape[1]
@@ -171,10 +173,9 @@
         in_specs=[block(3), block(3)],
         out_specs=[part, part],
         cost_estimate=cost,
-        name="first_sums",
     )(even, moved)
-    first = exchange(first, 4, "ctx")
-    second = exchange(second, 2, "ctx")
+    first = exchange(first, 4, CTX)
+    second = exchange(second, 2, CTX)
     two, four = pl.pallas_call(
         next_sums_kernel,
         out_shape=[jax.ShapeDtypeStruct((rows, width), BF16)] * 2,
@@ -182,10 +183,9 @@
         in_specs=[block(1), block(1), block(2), block(2), part, part],
         out_specs=[block(0), block(0)],
         cost_estimate=cost,
-        name="next_sums",
     )(even, moved, even, moved, first, second)
-    two = exchange(two, 2, "ctx")
-    four = exchange(four, 4, "ctx")
+    two = exchange(two, 2, CTX)
+    four = exchange(four, 4, CTX)
     return (
         (even[:rows].astype(F32) + moved[:rows].astype(F32))
         + two.astype(F32)
@@ -193,13 +193,13 @@
     )
 
 
-def scatter_ctx(even, odd):
-    count = lax.axis_size("ctx")
-    if count == 8:
+def scatter_ctx(even, odd, local_kernels=False):
+    count = lax.axis_size(CTX)
+    if local_kernels and count == 8:
         return scatter_eight(even, odd)
     rows = even.shape[0] * 2 // count
     half = rows // 2
-    moved = exchange(odd, 1, "ctx")
+    moved = exchange(odd, 1, CTX)
 
     def piece(number, start, stop):
         base = number // 2 * rows
@@ -215,12 +215,12 @@
         for number in even_numbers(count, level):
             low, top = low_bit(number), top_bit(number)
             first, second = tie(*(part.astype(BF16) for part in halves[number]))
-            halves[number ^ top][0] += exchange(first, top, "ctx").astype(F32)
-            halves[number ^ low][1] += exchange(second, low, "ctx").astype(F32)
+            halves[number ^ top][0] += exchange(first, top, CTX).astype(F32)
+            halves[number ^ low][1] += exchange(second, low, CTX).astype(F32)
     total = jnp.concatenate(halves[0], axis=0)
     for number in even_numbers(count, 1):
         sent = jnp.concatenate(halves[number], axis=0).astype(BF16)
-        total = total + exchange(sent, number, "ctx").astype(F32)
+        total = total + exchange(sent, number, CTX).astype(F32)
     return total
 
 
@@ -229,7 +229,7 @@
     for number in range(1, count):
         if level_of(number) == level:
             low = low_bit(number)
-            blocks[number] = exchange(blocks[number ^ low], low, "fsdp")
+            blocks[number] = exchange(blocks[number ^ low], low, FSDP)
     return blocks
 
 
@@ -239,13 +239,13 @@
         if level_of(number) == level:
             low = low_bit(number)
             sums[number ^ low] = sums[number ^ low].astype(F32) + exchange(
-                sums[number].astype(BF16), low, "fsdp"
+                sums[number].astype(BF16), low, FSDP
             ).astype(F32)
     return sums
 
 
 def sum_all(value):
-    for axis in ("ctx", "fsdp"):
+    for axis in (CTX, FSDP):
         bit = 1
         while bit < lax.axis_size(axis):
             value = value + exchange(value, bit, axis)
@@ -291,12 +291,11 @@
         cost_estimate=pl.CostEstimate(
             flops=0, bytes_accessed=4 * rows * total, transcendentals=0
         ),
-        name="pick_columns",
     )(jnp.stack([index for _, index, _ in picks]).astype(jnp.int32), *[p[0] for p in picks])
 
 
 def place_columns(pieces, widths, ctx_index):
-    count = lax.axis_size("ctx")
+    count = lax.axis_size(CTX)
     rows = pieces[0][2].shape[0]
     starts = [sum(widths[:number]) for number in range(len(widths))]
     if any(width % 128 for width in widths):
@@ -347,7 +346,6 @@
         cost_estimate=pl.CostEstimate(
             flops=0, bytes_accessed=6 * count * rows * sum(widths), transcendentals=0
         ),
-        name="place_columns",
     )(jnp.stack(index).astype(jnp.int32), *piece_arrays(pieces))
 
 
@@ -384,7 +382,6 @@
         + [pl.BlockSpec(memory_space=pltpu.VMEM)] * 4,
         out_specs=pl.BlockSpec(memory_space=pltpu.VMEM),
         cost_estimate=pl.CostEstimate(flops=0, bytes_accessed=8 * columns, transcendentals=0),
-        name="join_gains",
     )(indices, attn, mlp, query, key)
 
 
@@ -399,7 +396,6 @@
         cost_estimate=pl.CostEstimate(
             flops=0, bytes_accessed=8 * rows * width, transcendentals=0
         ),
-        name="own_blocks",
     )(indices, hidden, cot)
 
 
@@ -471,7 +467,6 @@
             bytes_accessed=12 * total * width,
             transcendentals=total * hidden,
         ),
-        name="mlp_both",
     )(*piece_arrays(pieces), both_all, *weights)
 
 
@@ -488,7 +483,7 @@
 def weight_grads(numbers, left_one, right_one, left_two, right_two, skipped=0):
     first, chunks = numbers[0], len(numbers)
     total, width = left_one.shape
-    size = width // lax.axis_size("fsdp")
+    size = width // lax.axis_size(FSDP)
     columns = right_one.shape[1] + right_two.shape[1]
     block = pl.BlockSpec((total, size), lambda step: (0, first + step))
     return pl.pallas_call(
@@ -507,7 +502,6 @@
             bytes_accessed=4 * total * (size * chunks + columns),
             transcendentals=0,
         ),
-        name="weight_grads",
     )(left_one, right_one, left_two, right_two)
 
 
@@ -572,7 +566,7 @@
     width = gain.shape[1]
     head = q_gain.shape[1]
     total = cosine.shape[0]
-    steps = lax.axis_size("ctx") // 2
+    steps = lax.axis_size(CTX) // 2
     rows = total // (2 * steps)
 
     def wide(columns):
@@ -605,7 +599,6 @@
             bytes_accessed=12 * total * width,
             transcendentals=total,
         ),
-        name="project",
     )(*piece_arrays(pieces), *weights, gain, q_gain, k_gain, cosine, sine_part)
 
 
@@ -653,12 +646,9 @@
     total, q_width = q.shape
     kv_width = k.shape[1]
     width = weights[0].shape[0] * len(weights)
-    steps = lax.axis_size("ctx") // 2
+    steps = lax.axis_size(CTX) // 2
     rows = total // (2 * steps)
     heads = q_width // head
-    last_columns = pl.BlockSpec(
-        (weights[0].shape[0], q_width), lambda step: (0, weights[0].shape[1] // q_width - 1)
-    )
 
     def wide(columns):
         return pl.BlockSpec((2 * rows, columns), lambda step: (step, 0))
@@ -678,7 +668,7 @@
             pl.BlockSpec((1, 2 * rows), lambda step: (0, step)),
             whole(pos_col),
         ]
-        + [last_columns] * len(weights),
+        + [whole(part) for part in weights],
         out_specs=[
             wide(q_width), pl.BlockSpec((heads, 2 * rows), lambda step: (0, step)), half, half,
         ],
@@ -688,7 +678,6 @@
             bytes_accessed=8 * total * width,
             transcendentals=total * total * heads,
         ),
-        name="attend",
     )(q, k, v, pos_row, pos_col, *weights)
 
 
@@ -754,12 +743,9 @@
     total, q_width = q.shape
     kv_width = k.shape[1]
     width = weights[0].shape[0] * len(weights)
-    steps = lax.axis_size("ctx") // 2
+    steps = lax.axis_size(CTX) // 2
     rows = total // (2 * steps)
     heads = lse.shape[0]
-    last_columns = pl.BlockSpec(
-        (weights[0].shape[0], q_width), lambda step: (0, weights[0].shape[1] // q_width - 1)
-    )
     head = q_gain.shape[1]
 
     def wide(columns):
@@ -779,7 +765,7 @@
         ],
         grid=(steps,),
         in_specs=in_place(pieces)
-        + [last_columns] * len(weights)
+        + [whole(part) for part in weights]
         + [
             wide(q_width), whole(k), whole(v),
             pl.BlockSpec((1, 2 * rows), lambda step: (0, step)),
@@ -798,7 +784,6 @@
             bytes_accessed=8 * total * width,
             transcendentals=total * total * heads,
         ),
-        name="attend_back",
     )(
         *piece_arrays(pieces), *weights,
         q, k, v, pos_row, pos_col, mix, lse, raw, q_gain, cosine, sine_part,
@@ -856,7 +841,7 @@
     total, q_width = low.shape
     kv_width = dk.shape[1]
     width = both_all.shape[1] // 2
-    steps = lax.axis_size("ctx") // 2
+    steps = lax.axis_size(CTX) // 2
     rows = total // (2 * steps)
     head = k_gain.shape[1]
 
@@ -899,7 +884,6 @@
             bytes_accessed=12 * total * width,
             transcendentals=total,
         ),
-        name="project_back",
     )(low, dk, dv, raw, k_gain, cosine, sine_part, both_all, act, *weights, *mlp_parts)
 
 
@@ -919,10 +903,10 @@
     down_proj,
     cotangent,
 ):
-    fsdp_count = lax.axis_size("fsdp")
-    fsdp_index = lax.axis_index("fsdp")
-    ctx_count = lax.axis_size("ctx")
-    ctx_index = lax.axis_index("ctx")
+    fsdp_count = lax.axis_size(FSDP)
+    fsdp_index = lax.axis_index(FSDP)
+    ctx_count = lax.axis_size(CTX)
+    ctx_index = lax.axis_index(CTX)
     row_count, width = hidden_in.shape[1:]
     block_len = row_count // 2
     total_rows = ctx_count * row_count
@@ -969,13 +953,16 @@
             (query_proj, ctx_index, query_width),
             (key_proj, kv_index, kv_width),
             (value_proj, kv_index, kv_width),
-            (output_proj, ctx_index, query_width),
         ]
     )
     first_blocks = {0: first_shard}
     for level in range(1, fsdp_levels + 1):
         first_blocks = gather_fsdp_step(first_blocks, fsdp_count, level)
     first_parts = [first_blocks[number] for number in range(fsdp_count)]
+    output_shard = pick_columns([(output_proj, ctx_index, query_width)])
+    output_parts = [output_shard] + [
+        exchange(output_shard, number, FSDP) for number in range(1, fsdp_count)
+    ]
     mlp_shard = pick_columns(
         [(weights, ctx_index, hidden_width) for weights in (gate_proj, up_proj, down_proj)]
     )
@@ -1002,7 +989,7 @@
         cosine, sine_part, query_width, kv_width,
     )
     attn_mix, log_total, mix_even, mix_odd = attend(
-        query_heads, key_heads, value_heads, pos_row, pos_col, first_parts, head_width
+        query_heads, key_heads, value_heads, pos_row, pos_col, output_parts, head_width
     )
 
     resid_sum = scatter_ctx(mix_even, mix_odd)
@@ -1033,17 +1020,17 @@
         mlp_sums = scatter_fsdp_step(mlp_sums, fsdp_count, level)
     resid_pieces = gather_ctx(resid_low)
     mlp_moved = {
-        number: exchange(mlp_sums[number].astype(BF16), number, "fsdp")
+        number: exchange(mlp_sums[number].astype(BF16), number, FSDP)
         for number in range(1, fsdp_count)
         if level_of(number) == 1
     }
     query_low, key_grad, value_grad, query_gain_grad, resid_all = attend_back(
-        resid_pieces, first_parts, query_heads, key_heads, value_heads, pos_row, pos_col,
+        resid_pieces, output_parts, query_heads, key_heads, value_heads, pos_row, pos_col,
         attn_mix, log_total, attn_raw, query_row, cosine, sine_part,
     )
     bit = 1
     while bit < kv_share:
-        moved = exchange(jnp.concatenate([key_grad, value_grad], axis=1), bit, "ctx")
+        moved = exchange(jnp.concatenate([key_grad, value_grad], axis=1), bit, CTX)
         moved = moved.reshape(ctx_count, row_count, 2 * kv_width)
         moved = jnp.concatenate([moved[number ^ bit] for number in range(ctx_count)], axis=0)
         key_grad = key_grad + moved[:, :kv_width]
@@ -1078,7 +1065,7 @@
     for level in range(fsdp_levels, 0, -1):
         attn_sums = scatter_fsdp_step(attn_sums, fsdp_count, level)
     attn_grads = attn_sums[0].astype(BF16)
-    both_sums = scatter_ctx(tail_even, tail_odd)
+    both_sums = scatter_ctx(tail_even, tail_odd, True)
     attn_in_grad = both_sums[:, :width]
     block_out = (resid + both_sums[:, width:]).astype(BF16)
     mlp_total = mlp_sums[0].astype(F32)
@@ -1128,35 +1115,35 @@
 
 def solution(mesh):
     in_specs = (
-        P("fsdp", "ctx", None),
+        P(FSDP, CTX, None),
         P(),
         P(),
-        P("fsdp", None),
-        P("fsdp", None),
-        P("fsdp", None),
+        P(FSDP, None),
+        P(FSDP, None),
+        P(FSDP, None),
         P(),
         P(),
-        P("fsdp", None),
+        P(FSDP, None),
         P(),
-        P("fsdp", None),
-        P("fsdp", None),
-        P("fsdp", None),
-        P("fsdp", "ctx", None),
+        P(FSDP, None),
+        P(FSDP, None),
+        P(FSDP, None),
+        P(FSDP, CTX, None),
     )
     out_specs = (
-        P("fsdp", "ctx", None),
-        P("fsdp", "ctx", None),
+        P(FSDP, CTX, None),
+        P(FSDP, CTX, None),
         P(),
-        P("fsdp", None),
-        P("fsdp", None),
-        P("fsdp", None),
+        P(FSDP, None),
+        P(FSDP, None),
+        P(FSDP, None),
         P(),
         P(),
-        P("fsdp", None),
+        P(FSDP, None),
         P(),
-        P("fsdp", None),
-        P("fsdp", None),
-        P("fsdp", None),
+        P(FSDP, None),
+        P(FSDP, None),
+        P(FSDP, None),
     )
     return jax.shard_map(
         on_device_all, mesh=mesh, in_specs=in_specs, out_specs=out_specs, check_vma=False

time: 321 us -> 312 us (0.972)
  Pallas kernels: 99.6 us -> 93.5 us
  starting transfers between devices: 54.4 us -> 58.5 us
  local copies, waits for them, and re-layouts: 20.4 us -> 16.5 us
    pallas_call x3 -> x1, Pallas kernels: 7.05 us -> 2.81 us  [scatter_eight(): pl.pallas_call(next_sums_kernel, out_shape=[jax.ShapeDtypeStruct((rows, w...]
    unnamed x124 -> x104, local copies, waits for them, and re-layouts: 9.3 us -> 5.08 us
    ppermute x77 -> x80, starting transfers between devices: 54.4 us -> 58.5 us  [exchange(): lax.ppermute(value, axis, [(index, index ^ bit) for index in range(count)])]
    pallas_call x3 -> x1, Pallas kernels: 5.62 us -> 2.1 us  [scatter_eight(): pl.pallas_call(first_sums_kernel, out_shape=[jax.ShapeDtypeStruct((half,...]
    pallas_call x2 -> x3, Pallas kernels: 5.17 us -> 6.75 us  [pick_columns(): pl.pallas_call(kernel, out_shape=jax.ShapeDtypeStruct((rows, total), pick...]
    ppermute x77 -> x80, waiting for transfers between devices: 119 us -> 118 us  [exchange(): lax.ppermute(value, axis, [(index, index ^ bit) for index in range(count)])]
  transfers between devices with their start and end apart: 77 -> 80, of which waited for: 26 -> 28; matrix products, arithmetic and copies ran while one was open for 11% -> 10% of each run, Pallas kernels for 19% -> 21%
where the time goes in v3:
time: 312 us; the launch traced here: 311 us
  waiting for transfers between devices  118 us (38%)
  Pallas kernels  93.5 us (30%)
  starting transfers between devices  58.5 us (19%)
  other arithmetic  23 us (7%)
  local copies, waits for them, and re-layouts  16.5 us (5%)
    ppermute x80, waiting for transfers between devices, exchange(): lax.ppermute(value, axis, [(index, index ^ bit) for index in range(count)])  118 us
    ppermute x80, starting transfers between devices, exchange(): lax.ppermute(value, axis, [(index, index ^ bit) for index in range(count)])  58.5 us
    pallas_call x4, Pallas kernels, weight_grads(): pl.pallas_call(grads_kernel, out_shape=[jax.ShapeDtypeStruct((size, colum...  18.2 us
    pallas_call x1, Pallas kernels, attend_back(): pl.pallas_call(functools.partial(attend_back_kernel, piece_plan(pieces),...  12 us
    pallas_call x1, Pallas kernels, attend(): pl.pallas_call(functools.partial(attend_kernel, len(weights)), out_shape=...  11.2 us
    pallas_call x2, Pallas kernels, place_columns(): pl.pallas_call(kernel, out_shape=[jax.ShapeDtypeStruct((rows, count * wid...  10.8 us
    pallas_call x1, Pallas kernels, mlp_both(): pl.pallas_call(functools.partial(mlp_kernel, piece_plan(pieces), len(weig...  9.69 us
    pallas_call x1, Pallas kernels, project_back(): pl.pallas_call(functools.partial(project_back_kernel, len(weights)), out_...  8.3 us
  transfers between devices with their start and end apart: 80, of which 28 were waited for; matrix products, arithmetic and copies ran while one was open for 10% of the time, Pallas kernels for 21%

profile of v3, /device:TPU:0, one launch (start us, length us, event | category | flops | bytes accessed | tf_op | source)
XLA Modules:
  0.0 310.9 jit_solution(17784174102977122253)
XLA Ops:
  15.1 3.7 %collective-permute-done.1.refs_2_ = bf16[128,2048]{1,0:T(8,128)(2,1)S(1)} collective-permute-done((bf16[128,2048]{1,0:T(8,128)(2,1)}, bf16[128,2048]{1,0:T(8,128)(2,1)S(1)}, u32[]{:S(2)}, u32[]{:S(2)}) %collective-permute-start.1) | collective-permute-done | bytes 524320 | tf_op jit(solution)/shard_map/ppermute | solution.py:39
  20.4 6.4 %collective-permute-done.10.refs_12_.refs_2_ = bf16[256,512]{1,0:T(8,128)(2,1)S(1)} collective-permute-done((bf16[256,512]{1,0:T(8,128)(2,1)}, bf16[256,512]{1,0:T(8,128)(2,1)S(1)}, u32[]{:S(2)}, u32[]{:S(2)}) %collective-permute-start.10) | collective-permute-done | bytes 262176 | tf_op jit(solution)/shard_map/ppermute | solution.py:39
  45.1 8.3 %shard_map.239 = (bf16[1024,1024]{1,0:T(8,128)(2,1)}, f32[1024,384]{1,0:T(8,128)}, bf16[1024,256]{1,0:T(8,128)(2,1)}, bf16[1024,128]{1,0:T(8,128)(2,1)}, bf16[10...) custom-call(bf16[128,2048]{1,0:T(8,128)(2,1)} %shard_map.237.refs_0_, bf16[128,2048]{1,0:T(8,128)(2,1)} %copy-done.18, ...), custom_call_target="tpu_custom_call" | custom-call | flops 1073741824 | bytes 12582912 | tf_op jit(solution)/shard_map/pallas_call | solution.py:578
  53.4 11.2 %shard_map.241 = (bf16[1024,256]{1,0:T(8,128)(2,1)}, f32[2,1024]{1,0:T(2,128)}, bf16[512,1024]{1,0:T(8,128)(2,1)}, bf16[512,1024]{1,0:T(8,128)(2,1)}) custom-call(bf16[1024,256]{1,0:T(8,128)(2,1)} %get-tuple-element.67.q_ref.refs_14_, bf16[1024,128]{1,0:T(8,128)(2,1)} %get-tuple-element.68.k_ref.refs_15_, ...), custom_call_target="tpu_custom_call" | custom-call | flops 1073741824 | bytes 8388608 | tf_op jit(solution)/shard_map/pallas_call | solution.py:657
  79.5 22.6 %collective-permute-done.30.refs_13_.refs_6_ = bf16[256,1152]{1,0:T(8,128)(2,1)S(1)} collective-permute-done((bf16[256,1152]{1,0:T(8,128)(2,1)}, bf16[256,1152]{1,0:T(8,128)(2,1)S(1)}, u32[]{:S(2)}, u32[]{:S(2)}) %collective-permute-start.30) | collective-permute-done | bytes 589856 | tf_op jit(solution)/shard_map/ppermute | solution.py:39
  104.6 5.2 %collective-permute-done.21.refs_2_ = bf16[128,1024]{1,0:T(8,128)(2,1)S(1)} collective-permute-done((bf16[128,1024]{1,0:T(8,128)(2,1)S(1)}, bf16[128,1024]{1,0:T(8,128)(2,1)S(1)}, u32[]{:S(2)}, u32[]{:S(2)}) %collective-permute-start.21) | collective-permute-done | bytes 262176 | tf_op jit(solution)/shard_map/ppermute | solution.py:39
  112.0 4.7 %collective-permute-done.31.refs_14_.refs_7_ = bf16[256,1152]{1,0:T(8,128)(2,1)S(1)} collective-permute-done((bf16[256,1152]{1,0:T(8,128)(2,1)S(1)}, bf16[256,1152]{1,0:T(8,128)(2,1)S(1)}, u32[]{:S(2)}, u32[]{:S(2)}) %collective-permute-start.31) | collective-permute-done | bytes 589856 | tf_op jit(solution)/shard_map/ppermute | solution.py:39
  117.8 3.9 %collective-permute-done.27.refs_8_ = bf16[64,1024]{1,0:T(8,128)(2,1)S(1)} collective-permute-done((bf16[64,1024]{1,0:T(8,128)(2,1)S(1)}, bf16[64,1024]{1,0:T(8,128)(2,1)S(1)}, u32[]{:S(2)}, u32[]{:S(2)}) %collective-permute-start.27) | collective-permute-done | bytes 131104 | tf_op jit(solution)/shard_map/ppermute | solution.py:39
  123.9 9.7 %shard_map.243 = (bf16[1024,768]{1,0:T(8,128)(2,1)}, bf16[1024,384]{1,0:T(8,128)(2,1)}, bf16[512,1024]{1,0:T(8,128)(2,1)}, bf16[512,1024]{1,0:T(8,128)(2,1)}, bf16[1024,1024]{1,0:T(8,128)(2,1)}) custom-call(bf16[128,1024]{1,0:T(8,128)(2,1)} %copy-done.28, bf16[128,1024]{1,0:T(8,128)(2,1)} %copy-done.42, bf16[128,1024]{1,0:T(8,128)(2,1)} %copy-done.33, ...), custom_call_target="tpu_custom_call" | custom-call | flops 4026531840 | bytes 12582912 | tf_op jit(solution)/shard_map/pallas_call | solution.py:450
  139.7 3.7 %collective-permute-done.35 = bf16[64,1024]{1,0:T(8,128)(2,1)S(1)} collective-permute-done((bf16[64,1024]{1,0:T(8,128)(2,1)S(1)}, bf16[64,1024]{1,0:T(8,128)(2,1)S(1)}, u32[]{:S(2)}, u32[]{:S(2)}) %collective-permute-start.35) | collective-permute-done | bytes 131104 | tf_op jit(solution)/shard_map/ppermute | solution.py:39
  148.4 3.6 %shard_map.253 = bf16[256,1152]{1,0:T(8,128)(2,1)} custom-call(bf16[1024,1024]{1,0:T(8,128)(2,1)} %get-tuple-element.111.left_one, bf16[1024,768]{1,0:T(8,128)(2,1)} %get-tuple-element.112.right_one, bf16[1024,2048]{1,0:T(8,128)(2,1)} %get-tuple-element.74.refs_10_.x_ref.left_two, bf16[1024,384]{1,0:T(8,128)(2,1)} %get-tuple-element.85.act_ref.right_two), custom_call_target="tpu_custom_call" | custom-call | flops 603979776 | bytes 5767168 | tf_op jit(solution)/shard_map/pallas_call | solution.py:489
  157.9 4.4 %collective-permute-done.38.refs_2_ = bf16[128,1024]{1,0:T(8,128)(2,1)S(1)} collective-permute-done((bf16[128,1024]{1,0:T(8,128)(2,1)S(1)}, bf16[128,1024]{1,0:T(8,128)(2,1)S(1)}, u32[]{:S(2)}, u32[]{:S(2)}) %collective-permute-start.38) | collective-permute-done | bytes 262176 | tf_op jit(solution)/shard_map/ppermute | solution.py:39
  165.3 6.4 %shard_map.252 = (bf16[256,1152]{1,0:T(8,128)(2,1)}, bf16[256,1152]{1,0:T(8,128)(2,1)}, bf16[256,1152]{1,0:T(8,128)(2,1)}) custom-call(bf16[1024,1024]{1,0:T(8,128)(2,1)} %get-tuple-element.111.left_one, bf16[1024,768]{1,0:T(8,128)(2,1)} %get-tuple-element.112.right_one, bf16[1024,2048]{1,0:T(8,128)(2,1)} %get-tuple-element.74.refs_10_.x_ref.left_two, ...), custom_call_target="tpu_custom_call" | custom-call | flops 1811939328 | bytes 7864320 | tf_op jit(solution)/shard_map/pallas_call | solution.py:489
  176.9 12.0 %shard_map.244 = (bf16[1024,256]{1,0:T(8,128)(2,1)}, f32[1024,128]{1,0:T(8,128)}, f32[1024,128]{1,0:T(8,128)}, f32[1,128]{1,0:T(1,128)}, bf16[1024,1024]{1,0:T(8,128)(2,1)}) custom-call(bf16[128,1024]{1,0:T(8,128)(2,1)} %copy-done.25, bf16[128,1024]{1,0:T(8,128)(2,1)} %copy-done.40, bf16[128,1024]{1,0:T(8,128)(2,1)} %copy-done.31, ...), custom_call_target="tpu_custom_call" | custom-call | flops 2684354560 | bytes 8388608 | tf_op jit(solution)/shard_map/pallas_call | solution.py:757
  188.8 8.3 %shard_map.245 = (bf16[1024,512]{1,0:T(8,128)(2,1)}, bf16[512,2048]{1,0:T(8,128)(2,1)}, bf16[512,2048]{1,0:T(8,128)(2,1)}, f32[1,1024]{1,0:T(1,128)}, f32[1,128]{1,0:T(1,128)}) custom-call(bf16[1024,256]{1,0:T(8,128)(2,1)} %get-tuple-element.82.low_ref, f32[1024,128]{1,0:T(8,128)} %get-tuple-element.83.dk_ref, f32[1024,128]{1,0:T(8,128)} %get-tuple-element.84.dv_ref, ...), custom_call_target="tpu_custom_call" | custom-call | flops 1073741824 | bytes 12582912 | tf_op jit(solution)/shard_map/pallas_call | solution.py:863
  197.2 4.6 %collective-permute-done.68 = bf16[256,1152]{1,0:T(8,128)(2,1)} collective-permute-done((bf16[256,1152]{1,0:T(8,128)(2,1)}, bf16[256,1152]{1,0:T(8,128)(2,1)}, u32[]{:S(2)}, u32[]{:S(2)}) %collective-permute-start.68) | collective-permute-done | bytes 589856 | tf_op jit(solution)/shard_map/ppermute | solution.py:39
  215.6 6.6 %collective-permute-done.58 = f32[1,2304]{1,0:T(1,128)S(1)} collective-permute-done((f32[1,2304]{1,0:T(1,128)S(1)}, f32[1,2304]{1,0:T(1,128)S(1)}, u32[]{:S(2)}, u32[]{:S(2)}) %collective-permute-start.58) | collective-permute-done | bytes 9248 | tf_op jit(solution)/shard_map/ppermute | solution.py:39
  223.2 5.2 %shard_map.246 = (bf16[256,768]{1,0:T(8,128)(2,1)}, bf16[256,768]{1,0:T(8,128)(2,1)}, bf16[256,768]{1,0:T(8,128)(2,1)}) custom-call(bf16[1024,1024]{1,0:T(8,128)(2,1)} %get-tuple-element.66.left_one, bf16[1024,512]{1,0:T(8,128)(2,1)} %get-tuple-element.86.right_one, bf16[1024,1024]{1,0:T(8,128)(2,1)} %get-tuple-element.87.left_two, ...), custom_call_target="tpu_custom_call" | custom-call | flops 1207959552 | bytes 6291456 | tf_op jit(solution)/shard_map/pallas_call | solution.py:489
  234.1 5.9 %collective-permute-done.60 = f32[1,2304]{1,0:T(1,128)S(1)} collective-permute-done((f32[1,2304]{1,0:T(1,128)S(1)}, f32[1,2304]{1,0:T(1,128)S(1)}, u32[]{:S(2)}, u32[]{:S(2)}) %collective-permute-start.60) | collective-permute-done | bytes 9248 | tf_op jit(solution)/shard_map/ppermute | solution.py:39
  248.9 9.6 %collective-permute-done.48 = bf16[256,768]{1,0:T(8,128)(2,1)} collective-permute-done((bf16[256,768]{1,0:T(8,128)(2,1)}, bf16[256,768]{1,0:T(8,128)(2,1)}, u32[]{:S(2)}, u32[]{:S(2)}) %collective-permute-start.48) | collective-permute-done | bytes 393248 | tf_op jit(solution)/shard_map/ppermute | solution.py:39
  271.4 10.3 %collective-permute-done.78.refs_8_ = bf16[128,1152]{1,0:T(8,128)(2,1)} collective-permute-done((bf16[128,1152]{1,0:T(8,128)(2,1)}, bf16[128,1152]{1,0:T(8,128)(2,1)}, u32[]{:S(2)}, u32[]{:S(2)}) %collective-permute-start.78) | collective-permute-done | bytes 294944 | tf_op jit(solution)/shard_map/ppermute | solution.py:39
  289.6 5.9 %shard_map.254 = (f32[256,3072]{1,0:T(8,128)}, f32[256,3072]{1,0:T(8,128)}, f32[256,3072]{1,0:T(8,128)}) custom-call(s32[5]{0:T(128)} %stack.56.index_ref, bf16[256,1152]{1,0:T(8,128)(2,1)} %add_convert_fusion.refs_0_, bf16[256,1152]{1,0:T(8,128)(2,1)} %collective-permute-done.71.refs_1_, bf16[256,1152]{1,0:T(8,128)(2,1)} %collective-permute-done.72.refs_2_, ...), custom_call_target="tpu_custom_call" | custom-call | bytes 14155776 | tf_op jit(solution)/shard_map/pallas_call | solution.py:333
  295.6 3.8 %collective-permute-done.50.refs_8_ = bf16[128,768]{1,0:T(8,128)(2,1)} collective-permute-done((bf16[128,768]{1,0:T(8,128)(2,1)}, bf16[128,768]{1,0:T(8,128)(2,1)}, u32[]{:S(2)}, u32[]{:S(2)}) %collective-permute-start.50) | collective-permute-done | bytes 196640 | tf_op jit(solution)/shard_map/ppermute | solution.py:39
  305.9 4.9 %shard_map.251 = (f32[256,2048]{1,0:T(8,128)}, f32[256,1024]{1,0:T(8,128)}, f32[256,1024]{1,0:T(8,128)}, f32[256,2048]{1,0:T(8,128)}) custom-call(s32[5]{0:T(128)} %stack.56.index_ref, bf16[256,768]{1,0:T(8,128)(2,1)} %copy-done.4, bf16[256,768]{1,0:T(8,128)(2,1)} %copy-done.22, bf16[256,768]{1,0:T(8,128)(2,1)} %copy-done.12, bf16[256,768]{1,0:T(8,128)(2,1)} %copy-done.23, ...), custom_call_target="tpu_custom_call" | custom-call | bytes 9437184 | tf_op jit(solution)/shard_map/pallas_call | solution.py:333
  (318 shorter events, 138.5 us)
Async XLA Ops:
  3.1 26.1 %collective-permute-start = (bf16[128,2048]{1,0:T(8,128)(2,1)}, bf16[128,2048]{1,0:T(8,128)(2,1)S(1)}, u32[]{:S(2)}, u32[]{:S(2)}) collective-permute-start(bf16[128,2048]{1,0:T(8,128)(2,1)} %shard_map.237.refs_0_), channel_id=1, source_target_pairs={{0,1},{1,0},{2,3},{3,2},{4,5},{5,4},{6,7},{7,6},{8,9},{9,8},{10,11... | collective-permute-start | bytes 1572872 | tf_op jit(solution)/shard_map/ppermute | solution.py:39
  10.6 18.1 %collective-permute-start.9 = (bf16[256,512]{1,0:T(8,128)(2,1)}, bf16[256,512]{1,0:T(8,128)(2,1)S(1)}, u32[]{:S(2)}, u32[]{:S(2)}) collective-permute-start(bf16[256,512]{1,0:T(8,128)(2,1)} %shard_map.238.refs_10_.refs_0_), channel_id=1, source_target_pairs={{0,8},{8,0},{16,24},{24,16},{1,9},{9,1},{17,25},{25,17},{2,10},{10... | collective-permute-start | bytes 786440 | tf_op jit(solution)/shard_map/ppermute | solution.py:39
  18.9 20.2 %collective-permute-start.2 = (bf16[128,2048]{1,0:T(8,128)(2,1)S(1)}, bf16[128,2048]{1,0:T(8,128)(2,1)S(1)}, u32[]{:S(2)}, u32[]{:S(2)}) collective-permute-start(bf16[128,2048]{1,0:T(8,128)(2,1)S(1)} %collective-permute-done.1.refs_2_), channel_id=1, source_target_pairs={{0,1},{1,0},{2,3},{3,2},{4,5},{5,4},{6,7},{7,6},{8,9},{9,8},{10,11... | collective-permute-start | bytes 1572872 | tf_op jit(solution)/shard_map/ppermute | solution.py:39
  20.3 19.9 %collective-permute-start.4 = (bf16[128,2048]{1,0:T(8,128)(2,1)S(1)}, bf16[128,2048]{1,0:T(8,128)(2,1)S(1)}, u32[]{:S(2)}, u32[]{:S(2)}) collective-permute-start(bf16[128,2048]{1,0:T(8,128)(2,1)S(1)} %collective-permute-done.3.refs_4_), channel_id=1, source_target_pairs={{0,1},{1,0},{2,3},{3,2},{4,5},{5,4},{6,7},{7,6},{8,9},{9,8},{10,11... | collective-permute-start | bytes 1572872 | tf_op jit(solution)/shard_map/ppermute | solution.py:39
  73.2 28.9 %collective-permute-start.30 = (bf16[256,1152]{1,0:T(8,128)(2,1)}, bf16[256,1152]{1,0:T(8,128)(2,1)S(1)}, u32[]{:S(2)}, u32[]{:S(2)}) collective-permute-start(bf16[256,1152]{1,0:T(8,128)(2,1)} %shard_map.242.refs_11_.refs_4_), channel_id=1, source_target_pairs={{0,16},{8,24},{16,0},{24,8},{1,17},{9,25},{17,1},{25,9},{2,18},{10... | collective-permute-start | bytes 1769480 | tf_op jit(solution)/shard_map/ppermute | solution.py:39
  76.4 25.7 %collective-permute-start.19 = (bf16[128,1024]{1,0:T(8,128)(2,1)S(1)}, bf16[128,1024]{1,0:T(8,128)(2,1)S(1)}, u32[]{:S(2)}, u32[]{:S(2)}) collective-permute-start(bf16[128,1024]{1,0:T(8,128)(2,1)S(1)} %pad_maximum_fusion.1), channel_id=1, source_target_pairs={{0,4},{1,5},{2,6},{3,7},{4,0},{5,1},{6,2},{7,3},{8,12},{9,13},{10,... | collective-permute-start | bytes 786440 | tf_op jit(solution)/shard_map/ppermute | solution.py:39
  77.0 25.1 %collective-permute-start.17 = (bf16[128,1024]{1,0:T(8,128)(2,1)S(1)}, bf16[128,1024]{1,0:T(8,128)(2,1)S(1)}, u32[]{:S(2)}, u32[]{:S(2)}) collective-permute-start(bf16[128,1024]{1,0:T(8,128)(2,1)S(1)} %pad_maximum_fusion), channel_id=1, source_target_pairs={{0,2},{1,3},{2,0},{3,1},{4,6},{5,7},{6,4},{7,5},{8,10},{9,11},{10,... | collective-permute-start | bytes 786440 | tf_op jit(solution)/shard_map/ppermute | solution.py:39
  78.5 32.9 %collective-permute-start.29 = (bf16[256,1152]{1,0:T(8,128)(2,1)S(1)}, bf16[256,1152]{1,0:T(8,128)(2,1)S(1)}, u32[]{:S(2)}, u32[]{:S(2)}) collective-permute-start(bf16[256,1152]{1,0:T(8,128)(2,1)S(1)} %copy-done.2), channel_id=1, source_target_pairs={{0,8},{8,0},{16,24},{24,16},{1,9},{9,1},{17,25},{25,17},{2,10},{10... | collective-permute-start | bytes 1769480 | tf_op jit(solution)/shard_map/ppermute | solution.py:39
  152.0 20.1 %collective-permute-start.69 = (bf16[256,1152]{1,0:T(8,128)(2,1)}, bf16[256,1152]{1,0:T(8,128)(2,1)S(1)}, u32[]{:S(2)}, u32[]{:S(2)}) collective-permute-start(bf16[256,1152]{1,0:T(8,128)(2,1)} %shard_map.253), channel_id=1, source_target_pairs={{0,8},{8,0},{16,24},{24,16},{1,9},{9,1},{17,25},{25,17},{2,10},{10... | collective-permute-start | bytes 1769480 | tf_op jit(solution)/shard_map/ppermute | solution.py:39
  174.8 27.1 %collective-permute-start.68 = (bf16[256,1152]{1,0:T(8,128)(2,1)}, bf16[256,1152]{1,0:T(8,128)(2,1)}, u32[]{:S(2)}, u32[]{:S(2)}) collective-permute-start(bf16[256,1152]{1,0:T(8,128)(2,1)} %get-tuple-element.114), channel_id=1, source_target_pairs={{0,8},{8,0},{16,24},{24,16},{1,9},{9,1},{17,25},{25,17},{2,10},{10... | collective-permute-start | bytes 1769480 | tf_op jit(solution)/shard_map/ppermute | solution.py:39
  174.8 29.6 %collective-permute-start.70 = (bf16[256,1152]{1,0:T(8,128)(2,1)}, bf16[256,1152]{1,0:T(8,128)(2,1)}, u32[]{:S(2)}, u32[]{:S(2)}) collective-permute-start(bf16[256,1152]{1,0:T(8,128)(2,1)} %add_convert_fusion.1), channel_id=1, source_target_pairs={{0,16},{8,24},{16,0},{24,8},{1,17},{9,25},{17,1},{25,9},{2,18},{10... | collective-permute-start | bytes 1769480 | tf_op jit(solution)/shard_map/ppermute | solution.py:39
  197.1 45.3 %collective-permute-start.52 = (bf16[512,2048]{1,0:T(8,128)(2,1)}, bf16[512,2048]{1,0:T(8,128)(2,1)S(1)}, u32[]{:S(2)}, u32[]{:S(2)}) collective-permute-start(bf16[512,2048]{1,0:T(8,128)(2,1)} %get-tuple-element.92), channel_id=1, source_target_pairs={{0,1},{1,0},{2,3},{3,2},{4,5},{5,4},{6,7},{7,6},{8,9},{9,8},{10,11... | collective-permute-start | bytes 6291464 | tf_op jit(solution)/shard_map/ppermute | solution.py:39
  206.9 23.3 %collective-permute-start.72 = (bf16[256,1152]{1,0:T(8,128)(2,1)}, bf16[256,1152]{1,0:T(8,128)(2,1)}, u32[]{:S(2)}, u32[]{:S(2)}) collective-permute-start(bf16[256,1152]{1,0:T(8,128)(2,1)} %add_convert_fusion.refs_0_), channel_id=1, source_target_pairs={{0,2},{1,3},{2,0},{3,1},{4,6},{5,7},{6,4},{7,5},{8,10},{9,11},{10,... | collective-permute-start | bytes 1769480 | tf_op jit(solution)/shard_map/ppermute | solution.py:39
  211.7 18.5 %collective-permute-start.47 = (bf16[256,768]{1,0:T(8,128)(2,1)}, bf16[256,768]{1,0:T(8,128)(2,1)S(1)}, u32[]{:S(2)}, u32[]{:S(2)}) collective-permute-start(bf16[256,768]{1,0:T(8,128)(2,1)} %shard_map.247), channel_id=1, source_target_pairs={{0,8},{8,0},{16,24},{24,16},{1,9},{9,1},{17,25},{25,17},{2,10},{10... | collective-permute-start | bytes 1179656 | tf_op jit(solution)/shard_map/ppermute | solution.py:39
  215.5 30.3 %collective-permute-start.71 = (bf16[256,1152]{1,0:T(8,128)(2,1)}, bf16[256,1152]{1,0:T(8,128)(2,1)}, u32[]{:S(2)}, u32[]{:S(2)}) collective-permute-start(bf16[256,1152]{1,0:T(8,128)(2,1)} %add_convert_fusion.refs_0_), channel_id=1, source_target_pairs={{0,1},{1,0},{2,3},{3,2},{4,5},{5,4},{6,7},{7,6},{8,9},{9,8},{10,11... | collective-permute-start | bytes 1769480 | tf_op jit(solution)/shard_map/ppermute | solution.py:39
  230.2 18.0 %collective-permute-start.46 = (bf16[256,768]{1,0:T(8,128)(2,1)}, bf16[256,768]{1,0:T(8,128)(2,1)}, u32[]{:S(2)}, u32[]{:S(2)}) collective-permute-start(bf16[256,768]{1,0:T(8,128)(2,1)} %get-tuple-element.89), channel_id=1, source_target_pairs={{0,8},{8,0},{16,24},{24,16},{1,9},{9,1},{17,25},{25,17},{2,10},{10... | collective-permute-start | bytes 1179656 | tf_op jit(solution)/shard_map/ppermute | solution.py:39
  240.0 18.5 %collective-permute-start.48 = (bf16[256,768]{1,0:T(8,128)(2,1)}, bf16[256,768]{1,0:T(8,128)(2,1)}, u32[]{:S(2)}, u32[]{:S(2)}) collective-permute-start(bf16[256,768]{1,0:T(8,128)(2,1)} %add_convert_fusion.3), channel_id=1, source_target_pairs={{0,16},{8,24},{16,0},{24,8},{1,17},{9,25},{17,1},{25,9},{2,18},{10... | collective-permute-start | bytes 1179656 | tf_op jit(solution)/shard_map/ppermute | solution.py:39
  242.4 19.6 %collective-permute-start.76 = (bf16[128,1152]{1,0:T(8,128)(2,1)}, bf16[128,1152]{1,0:T(8,128)(2,1)}, u32[]{:S(2)}, u32[]{:S(2)}) collective-permute-start(bf16[128,1152]{1,0:T(8,128)(2,1)} %slice.267), channel_id=1, source_target_pairs={{0,4},{1,5},{2,6},{3,7},{4,0},{5,1},{6,2},{7,3},{8,12},{9,13},{10,... | collective-permute-start | bytes 884744 | tf_op jit(solution)/shard_map/ppermute | solution.py:39
  245.8 36.3 %collective-permute-start.73 = (bf16[256,1152]{1,0:T(8,128)(2,1)}, bf16[256,1152]{1,0:T(8,128)(2,1)S(1)}, u32[]{:S(2)}, u32[]{:S(2)}) collective-permute-start(bf16[256,1152]{1,0:T(8,128)(2,1)} %collective-permute-done.72.refs_2_), channel_id=1, source_target_pairs={{0,1},{1,0},{2,3},{3,2},{4,5},{5,4},{6,7},{7,6},{8,9},{9,8},{10,11... | collective-permute-start | bytes 1769480 | tf_op jit(solution)/shard_map/ppermute | solution.py:39
  261.4 22.4 %collective-permute-start.49 = (bf16[256,768]{1,0:T(8,128)(2,1)S(1)}, bf16[256,768]{1,0:T(8,128)(2,1)S(1)}, u32[]{:S(2)}, u32[]{:S(2)}) collective-permute-start(bf16[256,768]{1,0:T(8,128)(2,1)S(1)} %add_convert_fusion.2.refs_0_), channel_id=1, source_target_pairs={{0,4},{1,5},{2,6},{3,7},{4,0},{5,1},{6,2},{7,3},{8,12},{9,13},{10,... | collective-permute-start | bytes 1179656 | tf_op jit(solution)/shard_map/ppermute | solution.py:39
  262.0 22.6 %collective-permute-start.63 = (bf16[256,768]{1,0:T(8,128)(2,1)S(1)}, bf16[256,768]{1,0:T(8,128)(2,1)S(1)}, u32[]{:S(2)}, u32[]{:S(2)}) collective-permute-start(bf16[256,768]{1,0:T(8,128)(2,1)S(1)} %add_convert_fusion.2.refs_0_), channel_id=1, source_target_pairs={{0,2},{1,3},{2,0},{3,1},{4,6},{5,7},{6,4},{7,5},{8,10},{9,11},{10,... | collective-permute-start | bytes 1179656 | tf_op jit(solution)/shard_map/ppermute | solution.py:39
  268.6 18.6 %collective-permute-start.75 = (bf16[256,1152]{1,0:T(8,128)(2,1)}, bf16[256,1152]{1,0:T(8,128)(2,1)S(1)}, u32[]{:S(2)}, u32[]{:S(2)}) collective-permute-start(bf16[256,1152]{1,0:T(8,128)(2,1)} %collective-permute-done.74.refs_4_), channel_id=1, source_target_pairs={{0,1},{1,0},{2,3},{3,2},{4,5},{5,4},{6,7},{7,6},{8,9},{9,8},{10,11... | collective-permute-start | bytes 1769480 | tf_op jit(solution)/shard_map/ppermute | solution.py:39
  281.7 18.2 %collective-permute-start.56 = (bf16[128,2048]{1,0:T(8,128)(2,1)}, bf16[128,2048]{1,0:T(8,128)(2,1)}, u32[]{:S(2)}, u32[]{:S(2)}) collective-permute-start(bf16[128,2048]{1,0:T(8,128)(2,1)} %get-tuple-element.96), channel_id=1, source_target_pairs={{0,4},{1,5},{2,6},{3,7},{4,0},{5,1},{6,2},{7,3},{8,12},{9,13},{10,... | collective-permute-start | bytes 1572872 | tf_op jit(solution)/shard_map/ppermute | solution.py:39
  282.1 17.9 %collective-permute-start.55 = (bf16[128,2048]{1,0:T(8,128)(2,1)}, bf16[128,2048]{1,0:T(8,128)(2,1)}, u32[]{:S(2)}, u32[]{:S(2)}) collective-permute-start(bf16[128,2048]{1,0:T(8,128)(2,1)} %get-tuple-element.95), channel_id=1, source_target_pairs={{0,2},{1,3},{2,0},{3,1},{4,6},{5,7},{6,4},{7,5},{8,10},{9,11},{10,... | collective-permute-start | bytes 1572872 | tf_op jit(solution)/shard_map/ppermute | solution.py:39
  (108 other events, 955.4 us)
